TPU v7x, 32 devices: a whole 2x2x4 slice. The times are simulated.
32 devices in a mesh: group: 2 (over x), seq: 16 (over z, y, core).
Axes of the slice: x: 2, y: 2, z: 4, core: 2. Of those that a mesh axis runs over, the one named last changes fastest.
Arguments:
- inputs: float32 [16384, 2560], P(('group', 'seq')), parts along dimension 0, may hold values from -6 to 6
- log_decay: float32 [40, 16384], P(None, ('group', 'seq')), parts along dimension 1, may hold values from -0.8 to 0, as said below
- state_write: float32 [16384, 128], P(('group', 'seq')), parts along dimension 0, may hold values from -0.5 to 0.5
- state_read: float32 [16384, 128], P(('group', 'seq')), parts along dimension 0, may hold values from -0.5 to 0.5
- skip_gain: float32 [40], replicated, may hold values from 0.5 to 1.5
- grad_output: float32 [16384, 2560], P(('group', 'seq')), parts along dimension 0, may hold values from -6 to 6
Outputs:
- outputs: float32 [16384, 2560], P(('group', 'seq')), parts along dimension 0
- grad_inputs: float32 [16384, 2560], P(('group', 'seq')), parts along dimension 0
- grad_decay: float32 [40, 16384], P(None, ('group', 'seq')), parts along dimension 1
- grad_write: float32 [16384, 128], P(('group', 'seq')), parts along dimension 0
- grad_read: float32 [16384, 128], P(('group', 'seq')), parts along dimension 0
There are 2 independent parts, one for each index of `group`. A program takes and returns all parts, laid end to end along the dimension named above; an argument that names none is the same for every part. Nothing has to cross between parts.
Inputs may be any that keep to these rules, and one draw needn't show every extreme that they name: `log_decay`: log retention of each head at each position; never positive.
All inputs are finite; a program needn't handle non-finite values.
Results may differ from a plain program's by a relative error of at most 0.00021.
Values sent between devices are 32-bit elements; how exact they have to be, the bound alone decides.
No kernel may reach another device: no remote copies, remote signals or barrier semaphores. Data moves between devices by JAX's collectives and lax.ppermute only.
A program may use at most 256 MiB of HBM per device.

v0:
```python
import math

import jax
import jax.numpy as jnp
from jax import lax
from jax.sharding import PartitionSpec as P

BLOCK = 256


def from_behind(value, axis, steps):
    count = lax.axis_size(axis)
    first, last = (max(0, -steps), min(count, count - steps))
    return lax.ppermute(value, axis, [(source, source + steps) for source in range(first, last)])


def block_pass(inputs, log_decay, state_write, state_read, skip_gain, start_state):
    tok_rows = inputs.shape[0]
    head_count = log_decay.shape[0]
    head_width = inputs.shape[1] // head_count
    block_count = tok_rows // BLOCK
    shaped = inputs.reshape(block_count, BLOCK, head_count, head_width)
    decays = log_decay.reshape(head_count, block_count, BLOCK).transpose(1, 0, 2)
    writes = state_write.reshape(block_count, BLOCK, -1)
    reads = state_read.reshape(block_count, BLOCK, -1)
    lower_mask = jnp.arange(BLOCK)[:, None] >= jnp.arange(BLOCK)[None, :]

    def advance(carried_state, pieces):
        values, decay_block, write_block, read_block = pieces
        cum_decay = jnp.cumsum(decay_block, axis=1)
        intersection = jnp.dot(read_block, write_block.T, precision=lax.Precision.HIGHEST)
        gap_decay = jnp.where(lower_mask[None], cum_decay[:, :, None] - cum_decay[:, None, :], 0.0)
        mixing = jnp.where(lower_mask[None], jnp.exp(gap_decay), 0.0) * intersection[None]
        inner_part = jnp.einsum("hts,shp->thp", mixing, values, precision=lax.Precision.HIGHEST)
        carried_portion = jnp.einsum(
            "tn,hpn->thp", read_block, carried_state, precision=lax.Precision.HIGHEST
        )
        carried_portion = carried_portion * jnp.exp(cum_decay).T[:, :, None]
        tail_weight = jnp.exp(cum_decay[:, -1:] - cum_decay).T
        update = jnp.einsum(
            "shp,sn->hpn",
            values * tail_weight[:, :, None],
            write_block,
            precision=lax.Precision.HIGHEST,
        )
        next_state = jnp.exp(cum_decay[:, -1])[:, None, None] * carried_state + update
        emitted = inner_part + carried_portion + skip_gain[None, :, None] * values
        return (next_state, emitted.reshape(BLOCK, head_count * head_width))

    final_state, emitted = lax.scan(advance, start_state, (shaped, decays, writes, reads))
    return (emitted.reshape(tok_rows, head_count * head_width), final_state)


def local(inputs, log_decay, state_write, state_read, skip_gain, grad_output):
    head_count = log_decay.shape[0]
    tok_rows = inputs.shape[0]
    head_width = inputs.shape[1] // head_count
    state_size = state_write.shape[1]
    cum_decay = jnp.cumsum(log_decay, axis=1)
    total_decay = cum_decay[:, -1]
    retain = jnp.exp(total_decay)
    tail_weight = jnp.exp(total_decay[:, None] - cum_decay).T
    lead_weight = jnp.exp(cum_decay).T
    shaped = inputs.reshape(tok_rows, head_count, head_width)
    grad_shaped = grad_output.reshape(tok_rows, head_count, head_width)
    local_state = jnp.einsum(
        "thp,tn->hpn",
        shaped * tail_weight[:, :, None],
        state_write,
        precision=lax.Precision.HIGHEST,
    )
    local_grad = jnp.einsum(
        "thp,tn->hpn",
        grad_shaped * lead_weight[:, :, None],
        state_read,
        precision=lax.Precision.HIGHEST,
    )
    blocks = math.gcd(head_count, 8)
    per_block = head_count // blocks
    devices = lax.axis_size("seq")
    position = lax.axis_index("seq")
    block_retain = retain.reshape(blocks, per_block)
    state_blocks = local_state.reshape(blocks, per_block, head_width, state_size)
    grad_blocks = local_grad.reshape(blocks, per_block, head_width, state_size)
    empty = jnp.zeros((blocks, per_block, head_width, state_size), jnp.float32)
    first = jnp.zeros((per_block, head_width, state_size), jnp.float32)

    def forward_turn(turn_index, carried):
        incoming, stored = carried
        block_slot = turn_index - position
        active = jnp.logical_and(block_slot >= 0, block_slot < blocks)
        chosen = jnp.clip(block_slot, 0, blocks - 1)
        own_retain = lax.dynamic_index_in_dim(block_retain, chosen, 0, False)
        own_state = lax.dynamic_index_in_dim(state_blocks, chosen, 0, False)
        outgoing = own_retain[:, None, None] * incoming + own_state
        previous = lax.dynamic_index_in_dim(stored, chosen, 0, False)
        stored = lax.dynamic_update_index_in_dim(
            stored, jnp.where(active, incoming, previous), chosen, 0
        )
        incoming = from_behind(outgoing, "seq", 1)
        return (incoming, stored)

    def backward_turn(turn_index, carried):
        incoming, stored = carried
        block_slot = turn_index - (devices - 1 - position)
        active = jnp.logical_and(block_slot >= 0, block_slot < blocks)
        chosen = jnp.clip(block_slot, 0, blocks - 1)
        own_retain = lax.dynamic_index_in_dim(block_retain, chosen, 0, False)
        own_grad = lax.dynamic_index_in_dim(grad_blocks, chosen, 0, False)
        outgoing = own_retain[:, None, None] * incoming + own_grad
        previous = lax.dynamic_index_in_dim(stored, chosen, 0, False)
        stored = lax.dynamic_update_index_in_dim(
            stored, jnp.where(active, incoming, previous), chosen, 0
        )
        incoming = from_behind(outgoing, "seq", -1)
        return (incoming, stored)

    turns = devices + blocks - 1
    _, stored_state = lax.fori_loop(0, turns, forward_turn, (first, empty))
    _, stored_grad = lax.fori_loop(0, turns, backward_turn, (first, empty))
    state_in = stored_state.reshape(head_count, head_width, state_size)
    state_grad = stored_grad.reshape(head_count, head_width, state_size)

    def local_fn(values, decay_rows, write_rows, read_rows):
        return block_pass(values, decay_rows, write_rows, read_rows, skip_gain, state_in)

    (outputs, final_state), pullback = jax.vjp(local_fn, inputs, log_decay, state_write, state_read)
    grad_inputs, grad_decay, grad_write, grad_read = pullback((grad_output, state_grad))
    return (outputs, grad_inputs, grad_decay, grad_write, grad_read)


def solution(mesh):
    in_specs = (
        P(("group", "seq"), None),
        P(None, ("group", "seq")),
        P(("group", "seq"), None),
        P(("group", "seq"), None),
        P(),
        P(("group", "seq"), None),
    )
    out_specs = (
        P(("group", "seq"), None),
        P(("group", "seq"), None),
        P(None, ("group", "seq")),
        P(("group", "seq"), None),
        P(("group", "seq"), None),
    )
    return jax.shard_map(local, mesh=mesh, in_specs=in_specs, out_specs=out_specs, check_vma=False)
```

profile of v0, /device:TPU:13, one launch (start us, length us, event | category | flops | bytes accessed | tf_op | source)
XLA Modules:
  0.0 745.7 jit_solution(8137901058787150733)
XLA Ops:
  3.3 5.9 copy.104
  9.2 5.9 copy.109
  15.1 9.0 %broadcast_multiply_fusion = (f32[512,40,64]{0,2,1:T(8,128)}, f32[512,40,64]{0,2,1:T(8,128)S(1)}) fusion(f32[512,40,64]{0,2,1:T(8,128)} %bitcast.459, f32[512,40]{0,1:T(8,128)S(1)} %get-tuple-element.1725, f32[512,40,64]{0,2,1:T(8,128)} %bitcast.455, f32[512,40]{0,1:T(8,128)S(1)} %get-tuple-element.1726), kind=kLoop, calls=%fused_computation.149 | loop fusion | flops 2621440 | bytes 21135360 | tf_op jit(solution)/shard_map/mul | solution.py:74
  24.1 5.4 fusion.108
  29.7 196.2 %while.101 = (s32[]{:T(128)}, f32[5,64,128]{2,1,0:T(8,128)S(1)}, f32[8,5,64,128]{3,2,1,0:T(8,128)S(1)}, s32[]{:T(128)}, f32[8,5]{1,0:T(8,128)S(1)}, /*index=5*/f...) while((s32[]{:T(128)}, f32[5,64,128]{2,1,0:T(8,128)S(1)}, ...), condition=%wide.region_3.4_spmd, body=%wide.region_2.3_spmd.sunk | while | flops 122888 | bytes 2294035 | solution.py:119
  225.9 7.4 reshape.457
  233.4 5.6 copy.107
  245.2 89.7 %while.103 = (s32[]{:T(128)}, f32[40,64,128]{2,1,0:T(8,128)S(1)}, f32[2,256,2560]{2,1,0:T(8,128)}, f32[2,128,256]{1,2,0:T(8,128)S(1)}, f32[2,40,256,256]{3,2,1,0...) while((s32[]{:T(128)}, f32[40,64,128]{2,1,0:T(8,128)S(1)}, ...), condition=%wide.region_7.8_spmd.clone.clone, body=%wide.region_4.7_spmd.clone.clone.sunk | while | flops 4154126336 | bytes 164427936 | solution.py:50
  246.8 12.7 %multiply_dynamic-update-slice_fusion.4 = (f32[2,40,256,256]{3,2,1,0:T(8,128)}, f32[2,40,256,256]{3,2,1,0:T(8,128)}, f32[2,40,256,256]{3,2,1,0:T(8,128)}) fusion(f32[2,40,256,256]{3,2,1,0:T(8,128)} %get-tuple-element.2210, s32[]{:T(128)} %get-tuple-element.2203, f32[256,256]{1,0:T(8,128)S(1)} %get-tuple-element.2100, ...), kind=kLoop, calls=%fused_computation.14.clone.1 | loop fusion | flops 10485760 | bytes 31867392 | tf_op jit(solution)/shard_map/jvp()/while/body/jit(dynamic_update_index_in_dim)/dynamic_update_slice | solution.py:50
  262.1 13.3 %fusion.175 = f32[256,40,64]{0,2,1:T(8,128)} fusion(f32[256,40,64]{0,2,1:T(8,128)S(1)} %get-tuple-element.2099, f32[2,256,40,64]{1,3,2,0:T(8,128)S(1)} %bitcast.447, s32[]{:T(128)} %get-tuple-element.2203, f32[256,256]{1,0:T(8,128)S(1)} %get-tuple-element.2100, f32[40,256]{1,0:T(8,128)S(1)} %copy_bitcast_fusion.4, ...), kind=kOutput, calls=%fused_computation.32.clone.1 | convolution fusion | flops 2026373120 | bytes 10937856 | tf_op jit(solution)/shard_map/jvp()/while/body/eval_jaxpr/hts,shp->thp/dot_general | solution.py:34
  291.4 12.7 %multiply_dynamic-update-slice_fusion.4 = (f32[2,40,256,256]{3,2,1,0:T(8,128)}, f32[2,40,256,256]{3,2,1,0:T(8,128)}, f32[2,40,256,256]{3,2,1,0:T(8,128)}) fusion(f32[2,40,256,256]{3,2,1,0:T(8,128)} %get-tuple-element.2210, s32[]{:T(128)} %get-tuple-element.2203, f32[256,256]{1,0:T(8,128)S(1)} %get-tuple-element.2100, ...), kind=kLoop, calls=%fused_computation.14.clone.1 | loop fusion | flops 10485760 | bytes 31867392 | tf_op jit(solution)/shard_map/jvp()/while/body/jit(dynamic_update_index_in_dim)/dynamic_update_slice | solution.py:50
  306.6 13.3 %fusion.175 = f32[256,40,64]{0,2,1:T(8,128)} fusion(f32[256,40,64]{0,2,1:T(8,128)S(1)} %get-tuple-element.2099, f32[2,256,40,64]{1,3,2,0:T(8,128)S(1)} %bitcast.447, s32[]{:T(128)} %get-tuple-element.2203, f32[256,256]{1,0:T(8,128)S(1)} %get-tuple-element.2100, f32[40,256]{1,0:T(8,128)S(1)} %copy_bitcast_fusion.4, ...), kind=kOutput, calls=%fused_computation.32.clone.1 | convolution fusion | flops 2026373120 | bytes 10937856 | tf_op jit(solution)/shard_map/jvp()/while/body/eval_jaxpr/hts,shp->thp/dot_general | solution.py:34
  334.9 8.1 %fusion.106 = f32[8,5,64,128]{3,2,1,0:T(8,128)} fusion(f32[8,5,64,512]{3,2,1,0:T(8,128)} %bitcast.460, f32[512,128]{1,0:T(8,128)S(1)} %bitcast.457), kind=kOutput, calls=%fused_computation.151 | convolution fusion | flops 2013265920 | bytes 6815744 | tf_op jit(solution)/shard_map/thp,tn->hpn/dot_general | solution.py:72
  343.2 198.6 %while.102 = (s32[]{:T(128)}, f32[5,64,128]{2,1,0:T(8,128)S(1)}, f32[8,5,64,128]{3,2,1,0:T(8,128)S(1)}, s32[]{:T(128)}, f32[8,5]{1,0:T(8,128)S(1)}, /*index=5*/f...) while((s32[]{:T(128)}, f32[5,64,128]{2,1,0:T(8,128)S(1)}, ...), condition=%wide.region_9.10_spmd, body=%wide.region_8.9_spmd.sunk | while | flops 122888 | bytes 2294035 | solution.py:120
  346.2 6.3 collective-permute-done.1
  355.6 5.5 collective-permute-done.1
  364.2 5.5 collective-permute-done.1
  372.8 5.5 collective-permute-done.1
  381.4 5.5 collective-permute-done.1
  390.0 5.5 collective-permute-done.1
  398.6 5.5 collective-permute-done.1
  407.2 5.5 collective-permute-done.1
  415.8 5.5 collective-permute-done.1
  424.4 5.5 collective-permute-done.1
  433.0 5.5 collective-permute-done.1
  441.6 5.5 collective-permute-done.1
  450.2 5.5 collective-permute-done.1
  458.8 5.5 collective-permute-done.1
  467.4 5.5 collective-permute-done.1
  476.0 5.5 collective-permute-done.1
  484.6 5.5 collective-permute-done.1
  493.2 5.5 collective-permute-done.1
  501.8 5.5 collective-permute-done.1
  510.4 5.5 collective-permute-done.1
  519.0 5.5 collective-permute-done.1
  527.6 5.5 collective-permute-done.1
  536.2 5.5 collective-permute-done.1
  546.8 179.6 %while.104 = (s32[]{:T(128)}, f32[40,64,128]{2,1,0:T(8,128)S(1)}, f32[2,256,40,64]{1,3,2,0:T(8,128)}, f32[2,40,256]{2,1,0:T(8,128)}, f32[2,256,128]{2,1,0:T(8,12...) while((s32[]{:T(128)}, f32[40,64,128]{2,1,0:T(8,128)S(1)}, ...), condition=%wide.region_20.21_spmd.clone.clone, body=%wide.region_10.20_spmd.clone.clone.sunk | while | flops 8283953152 | bytes 125473504 | solution.py:50
  575.2 18.6 %fusion.192 = (f32[40,256]{1,0:T(8,128)S(1)}, f32[40,256]{1,0:T(8,128)S(1)}, f32[256,256]{1,0:T(8,128)}) fusion(f32[2,40,256,256]{3,2,1,0:T(8,128)} %get-tuple-element.2362, s32[]{:T(128)S(6)} %sub.227, f32[256,256]{1,0:T(8,128)S(1)} %dynamic-slice_bitcast_fusion.6, pred[256,256]{1,0:T(8,128)(4,1)S(1)} %get-tuple-element.2366, ...), kind=kOutput, calls=%fused_computation.97.clone.1 | convolution fusion | flops 2034151424 | bytes 26887168 | tf_op jit(solution)/shard_map/transpose(jvp())/while/body/eval_jaxpr/hts,shp->thp/dot_general | solution.py:34
  594.6 6.0 fusion.191
  617.9 12.8 %bitcast_dynamic-update-slice_fusion.24 = f32[2,256,40,64]{1,3,2,0:T(8,128)} fusion(f32[2,256,40,64]{1,3,2,0:T(8,128)} %get-tuple-element.2315, s32[]{:T(128)S(6)} %sub.227, f32[256,40,64]{0,2,1:T(8,128)} %get-tuple-element.2139, f32[256,40,64]{0,2,1:T(8,128)S(1)} %bitcast.441, f32[40,64,256]{2,1,0:T(8,128)S(1)} %bitcast.442, ...), kind=kOutput, calls=%fused_computation.91.clone.1 | convolution fusion | flops 2015887360 | bytes 21013664 | tf_op jit(solution)/shard_map/transpose(jvp())/while/body/eval_jaxpr/hts,shp->thp/dot_general | solution.py:34
  637.2 6.1 fusion.198
  654.7 18.6 %fusion.192 = (f32[40,256]{1,0:T(8,128)S(1)}, f32[40,256]{1,0:T(8,128)S(1)}, f32[256,256]{1,0:T(8,128)}) fusion(f32[2,40,256,256]{3,2,1,0:T(8,128)} %get-tuple-element.2362, s32[]{:T(128)S(6)} %sub.227, f32[256,256]{1,0:T(8,128)S(1)} %dynamic-slice_bitcast_fusion.6, pred[256,256]{1,0:T(8,128)(4,1)S(1)} %get-tuple-element.2366, ...), kind=kOutput, calls=%fused_computation.97.clone.1 | convolution fusion | flops 2034151424 | bytes 26887168 | tf_op jit(solution)/shard_map/transpose(jvp())/while/body/eval_jaxpr/hts,shp->thp/dot_general | solution.py:34
  674.1 6.0 fusion.191
  697.5 12.9 %bitcast_dynamic-update-slice_fusion.24 = f32[2,256,40,64]{1,3,2,0:T(8,128)} fusion(f32[2,256,40,64]{1,3,2,0:T(8,128)} %get-tuple-element.2315, s32[]{:T(128)S(6)} %sub.227, f32[256,40,64]{0,2,1:T(8,128)} %get-tuple-element.2139, f32[256,40,64]{0,2,1:T(8,128)S(1)} %bitcast.441, f32[40,64,256]{2,1,0:T(8,128)S(1)} %bitcast.442, ...), kind=kOutput, calls=%fused_computation.91.clone.1 | convolution fusion | flops 2015887360 | bytes 21013664 | tf_op jit(solution)/shard_map/transpose(jvp())/while/body/eval_jaxpr/hts,shp->thp/dot_general | solution.py:34
  716.8 6.1 fusion.198
  726.4 8.6 %copy.120 = f32[2,256,40,64]{3,2,1,0:T(8,128)} copy(f32[2,256,40,64]{1,3,2,0:T(8,128)} %get-tuple-element.1119) | data formatting | bytes 10485760
  735.1 9.6 %reshape.491 = f32[512,2560]{1,0:T(8,128)} reshape(f32[2,256,40,64]{3,2,1,0:T(8,128)} %copy.120) | data formatting | bytes 10485760
  (572 shorter events, 386.5 us)
Async XLA Ops:
  30.8 6.0 collective-permute-start
  37.8 7.5 %collective-permute-start = (f32[5,64,128]{2,1,0:T(8,128)S(1)}, f32[5,64,128]{2,1,0:T(8,128)S(1)}, u32[]{:S(2)}, u32[]{:S(2)}) collective-permute-start(f32[5,64,128]{2,1,0:T(8,128)S(1)} %bitcast_add_fusion.6), channel_id=1, source_target_pairs={{0,1},{1,2},{2,3},{3,4},{4,5},{5,6},{6,7},{7,8},{8,9},{9,10},{10,1... | collective-permute-start | bytes 491528 | tf_op jit(solution)/shard_map/while/body/eval_jaxpr/ppermute | solution.py:14
  46.4 7.5 %collective-permute-start = (f32[5,64,128]{2,1,0:T(8,128)S(1)}, f32[5,64,128]{2,1,0:T(8,128)S(1)}, u32[]{:S(2)}, u32[]{:S(2)}) collective-permute-start(f32[5,64,128]{2,1,0:T(8,128)S(1)} %bitcast_add_fusion.6), channel_id=1, source_target_pairs={{0,1},{1,2},{2,3},{3,4},{4,5},{5,6},{6,7},{7,8},{8,9},{9,10},{10,1... | collective-permute-start | bytes 491528 | tf_op jit(solution)/shard_map/while/body/eval_jaxpr/ppermute | solution.py:14
  55.0 7.5 %collective-permute-start = (f32[5,64,128]{2,1,0:T(8,128)S(1)}, f32[5,64,128]{2,1,0:T(8,128)S(1)}, u32[]{:S(2)}, u32[]{:S(2)}) collective-permute-start(f32[5,64,128]{2,1,0:T(8,128)S(1)} %bitcast_add_fusion.6), channel_id=1, source_target_pairs={{0,1},{1,2},{2,3},{3,4},{4,5},{5,6},{6,7},{7,8},{8,9},{9,10},{10,1... | collective-permute-start | bytes 491528 | tf_op jit(solution)/shard_map/while/body/eval_jaxpr/ppermute | solution.py:14
  63.6 7.5 %collective-permute-start = (f32[5,64,128]{2,1,0:T(8,128)S(1)}, f32[5,64,128]{2,1,0:T(8,128)S(1)}, u32[]{:S(2)}, u32[]{:S(2)}) collective-permute-start(f32[5,64,128]{2,1,0:T(8,128)S(1)} %bitcast_add_fusion.6), channel_id=1, source_target_pairs={{0,1},{1,2},{2,3},{3,4},{4,5},{5,6},{6,7},{7,8},{8,9},{9,10},{10,1... | collective-permute-start | bytes 491528 | tf_op jit(solution)/shard_map/while/body/eval_jaxpr/ppermute | solution.py:14
  72.2 7.5 %collective-permute-start = (f32[5,64,128]{2,1,0:T(8,128)S(1)}, f32[5,64,128]{2,1,0:T(8,128)S(1)}, u32[]{:S(2)}, u32[]{:S(2)}) collective-permute-start(f32[5,64,128]{2,1,0:T(8,128)S(1)} %bitcast_add_fusion.6), channel_id=1, source_target_pairs={{0,1},{1,2},{2,3},{3,4},{4,5},{5,6},{6,7},{7,8},{8,9},{9,10},{10,1... | collective-permute-start | bytes 491528 | tf_op jit(solution)/shard_map/while/body/eval_jaxpr/ppermute | solution.py:14
  80.8 7.5 %collective-permute-start = (f32[5,64,128]{2,1,0:T(8,128)S(1)}, f32[5,64,128]{2,1,0:T(8,128)S(1)}, u32[]{:S(2)}, u32[]{:S(2)}) collective-permute-start(f32[5,64,128]{2,1,0:T(8,128)S(1)} %bitcast_add_fusion.6), channel_id=1, source_target_pairs={{0,1},{1,2},{2,3},{3,4},{4,5},{5,6},{6,7},{7,8},{8,9},{9,10},{10,1... | collective-permute-start | bytes 491528 | tf_op jit(solution)/shard_map/while/body/eval_jaxpr/ppermute | solution.py:14
  89.4 7.5 %collective-permute-start = (f32[5,64,128]{2,1,0:T(8,128)S(1)}, f32[5,64,128]{2,1,0:T(8,128)S(1)}, u32[]{:S(2)}, u32[]{:S(2)}) collective-permute-start(f32[5,64,128]{2,1,0:T(8,128)S(1)} %bitcast_add_fusion.6), channel_id=1, source_target_pairs={{0,1},{1,2},{2,3},{3,4},{4,5},{5,6},{6,7},{7,8},{8,9},{9,10},{10,1... | collective-permute-start | bytes 491528 | tf_op jit(solution)/shard_map/while/body/eval_jaxpr/ppermute | solution.py:14
  98.0 7.5 %collective-permute-start = (f32[5,64,128]{2,1,0:T(8,128)S(1)}, f32[5,64,128]{2,1,0:T(8,128)S(1)}, u32[]{:S(2)}, u32[]{:S(2)}) collective-permute-start(f32[5,64,128]{2,1,0:T(8,128)S(1)} %bitcast_add_fusion.6), channel_id=1, source_target_pairs={{0,1},{1,2},{2,3},{3,4},{4,5},{5,6},{6,7},{7,8},{8,9},{9,10},{10,1... | collective-permute-start | bytes 491528 | tf_op jit(solution)/shard_map/while/body/eval_jaxpr/ppermute | solution.py:14
  106.6 7.5 %collective-permute-start = (f32[5,64,128]{2,1,0:T(8,128)S(1)}, f32[5,64,128]{2,1,0:T(8,128)S(1)}, u32[]{:S(2)}, u32[]{:S(2)}) collective-permute-start(f32[5,64,128]{2,1,0:T(8,128)S(1)} %bitcast_add_fusion.6), channel_id=1, source_target_pairs={{0,1},{1,2},{2,3},{3,4},{4,5},{5,6},{6,7},{7,8},{8,9},{9,10},{10,1... | collective-permute-start | bytes 491528 | tf_op jit(solution)/shard_map/while/body/eval_jaxpr/ppermute | solution.py:14
  115.2 7.5 %collective-permute-start = (f32[5,64,128]{2,1,0:T(8,128)S(1)}, f32[5,64,128]{2,1,0:T(8,128)S(1)}, u32[]{:S(2)}, u32[]{:S(2)}) collective-permute-start(f32[5,64,128]{2,1,0:T(8,128)S(1)} %bitcast_add_fusion.6), channel_id=1, source_target_pairs={{0,1},{1,2},{2,3},{3,4},{4,5},{5,6},{6,7},{7,8},{8,9},{9,10},{10,1... | collective-permute-start | bytes 491528 | tf_op jit(solution)/shard_map/while/body/eval_jaxpr/ppermute | solution.py:14
  123.8 7.5 %collective-permute-start = (f32[5,64,128]{2,1,0:T(8,128)S(1)}, f32[5,64,128]{2,1,0:T(8,128)S(1)}, u32[]{:S(2)}, u32[]{:S(2)}) collective-permute-start(f32[5,64,128]{2,1,0:T(8,128)S(1)} %bitcast_add_fusion.6), channel_id=1, source_target_pairs={{0,1},{1,2},{2,3},{3,4},{4,5},{5,6},{6,7},{7,8},{8,9},{9,10},{10,1... | collective-permute-start | bytes 491528 | tf_op jit(solution)/shard_map/while/body/eval_jaxpr/ppermute | solution.py:14
  132.4 7.5 %collective-permute-start = (f32[5,64,128]{2,1,0:T(8,128)S(1)}, f32[5,64,128]{2,1,0:T(8,128)S(1)}, u32[]{:S(2)}, u32[]{:S(2)}) collective-permute-start(f32[5,64,128]{2,1,0:T(8,128)S(1)} %bitcast_add_fusion.6), channel_id=1, source_target_pairs={{0,1},{1,2},{2,3},{3,4},{4,5},{5,6},{6,7},{7,8},{8,9},{9,10},{10,1... | collective-permute-start | bytes 491528 | tf_op jit(solution)/shard_map/while/body/eval_jaxpr/ppermute | solution.py:14
  141.0 7.5 %collective-permute-start = (f32[5,64,128]{2,1,0:T(8,128)S(1)}, f32[5,64,128]{2,1,0:T(8,128)S(1)}, u32[]{:S(2)}, u32[]{:S(2)}) collective-permute-start(f32[5,64,128]{2,1,0:T(8,128)S(1)} %bitcast_add_fusion.6), channel_id=1, source_target_pairs={{0,1},{1,2},{2,3},{3,4},{4,5},{5,6},{6,7},{7,8},{8,9},{9,10},{10,1... | collective-permute-start | bytes 491528 | tf_op jit(solution)/shard_map/while/body/eval_jaxpr/ppermute | solution.py:14
  149.6 7.5 %collective-permute-start = (f32[5,64,128]{2,1,0:T(8,128)S(1)}, f32[5,64,128]{2,1,0:T(8,128)S(1)}, u32[]{:S(2)}, u32[]{:S(2)}) collective-permute-start(f32[5,64,128]{2,1,0:T(8,128)S(1)} %bitcast_add_fusion.6), channel_id=1, source_target_pairs={{0,1},{1,2},{2,3},{3,4},{4,5},{5,6},{6,7},{7,8},{8,9},{9,10},{10,1... | collective-permute-start | bytes 491528 | tf_op jit(solution)/shard_map/while/body/eval_jaxpr/ppermute | solution.py:14
  158.2 7.5 %collective-permute-start = (f32[5,64,128]{2,1,0:T(8,128)S(1)}, f32[5,64,128]{2,1,0:T(8,128)S(1)}, u32[]{:S(2)}, u32[]{:S(2)}) collective-permute-start(f32[5,64,128]{2,1,0:T(8,128)S(1)} %bitcast_add_fusion.6), channel_id=1, source_target_pairs={{0,1},{1,2},{2,3},{3,4},{4,5},{5,6},{6,7},{7,8},{8,9},{9,10},{10,1... | collective-permute-start | bytes 491528 | tf_op jit(solution)/shard_map/while/body/eval_jaxpr/ppermute | solution.py:14
  166.8 7.5 %collective-permute-start = (f32[5,64,128]{2,1,0:T(8,128)S(1)}, f32[5,64,128]{2,1,0:T(8,128)S(1)}, u32[]{:S(2)}, u32[]{:S(2)}) collective-permute-start(f32[5,64,128]{2,1,0:T(8,128)S(1)} %bitcast_add_fusion.6), channel_id=1, source_target_pairs={{0,1},{1,2},{2,3},{3,4},{4,5},{5,6},{6,7},{7,8},{8,9},{9,10},{10,1... | collective-permute-start | bytes 491528 | tf_op jit(solution)/shard_map/while/body/eval_jaxpr/ppermute | solution.py:14
  175.4 7.5 %collective-permute-start = (f32[5,64,128]{2,1,0:T(8,128)S(1)}, f32[5,64,128]{2,1,0:T(8,128)S(1)}, u32[]{:S(2)}, u32[]{:S(2)}) collective-permute-start(f32[5,64,128]{2,1,0:T(8,128)S(1)} %bitcast_add_fusion.6), channel_id=1, source_target_pairs={{0,1},{1,2},{2,3},{3,4},{4,5},{5,6},{6,7},{7,8},{8,9},{9,10},{10,1... | collective-permute-start | bytes 491528 | tf_op jit(solution)/shard_map/while/body/eval_jaxpr/ppermute | solution.py:14
  184.0 7.5 %collective-permute-start = (f32[5,64,128]{2,1,0:T(8,128)S(1)}, f32[5,64,128]{2,1,0:T(8,128)S(1)}, u32[]{:S(2)}, u32[]{:S(2)}) collective-permute-start(f32[5,64,128]{2,1,0:T(8,128)S(1)} %bitcast_add_fusion.6), channel_id=1, source_target_pairs={{0,1},{1,2},{2,3},{3,4},{4,5},{5,6},{6,7},{7,8},{8,9},{9,10},{10,1... | collective-permute-start | bytes 491528 | tf_op jit(solution)/shard_map/while/body/eval_jaxpr/ppermute | solution.py:14
  192.6 7.5 %collective-permute-start = (f32[5,64,128]{2,1,0:T(8,128)S(1)}, f32[5,64,128]{2,1,0:T(8,128)S(1)}, u32[]{:S(2)}, u32[]{:S(2)}) collective-permute-start(f32[5,64,128]{2,1,0:T(8,128)S(1)} %bitcast_add_fusion.6), channel_id=1, source_target_pairs={{0,1},{1,2},{2,3},{3,4},{4,5},{5,6},{6,7},{7,8},{8,9},{9,10},{10,1... | collective-permute-start | bytes 491528 | tf_op jit(solution)/shard_map/while/body/eval_jaxpr/ppermute | solution.py:14
  201.2 7.5 %collective-permute-start = (f32[5,64,128]{2,1,0:T(8,128)S(1)}, f32[5,64,128]{2,1,0:T(8,128)S(1)}, u32[]{:S(2)}, u32[]{:S(2)}) collective-permute-start(f32[5,64,128]{2,1,0:T(8,128)S(1)} %bitcast_add_fusion.6), channel_id=1, source_target_pairs={{0,1},{1,2},{2,3},{3,4},{4,5},{5,6},{6,7},{7,8},{8,9},{9,10},{10,1... | collective-permute-start | bytes 491528 | tf_op jit(solution)/shard_map/while/body/eval_jaxpr/ppermute | solution.py:14
  209.8 7.5 %collective-permute-start = (f32[5,64,128]{2,1,0:T(8,128)S(1)}, f32[5,64,128]{2,1,0:T(8,128)S(1)}, u32[]{:S(2)}, u32[]{:S(2)}) collective-permute-start(f32[5,64,128]{2,1,0:T(8,128)S(1)} %bitcast_add_fusion.6), channel_id=1, source_target_pairs={{0,1},{1,2},{2,3},{3,4},{4,5},{5,6},{6,7},{7,8},{8,9},{9,10},{10,1... | collective-permute-start | bytes 491528 | tf_op jit(solution)/shard_map/while/body/eval_jaxpr/ppermute | solution.py:14
  218.4 7.5 %collective-permute-start = (f32[5,64,128]{2,1,0:T(8,128)S(1)}, f32[5,64,128]{2,1,0:T(8,128)S(1)}, u32[]{:S(2)}, u32[]{:S(2)}) collective-permute-start(f32[5,64,128]{2,1,0:T(8,128)S(1)} %bitcast_add_fusion.6), channel_id=1, source_target_pairs={{0,1},{1,2},{2,3},{3,4},{4,5},{5,6},{6,7},{7,8},{8,9},{9,10},{10,1... | collective-permute-start | bytes 491528 | tf_op jit(solution)/shard_map/while/body/eval_jaxpr/ppermute | solution.py:14
  344.2 8.3 %collective-permute-start.1 = (f32[5,64,128]{2,1,0:T(8,128)S(1)}, f32[5,64,128]{2,1,0:T(8,128)S(1)}, u32[]{:S(2)}, u32[]{:S(2)}) collective-permute-start(f32[5,64,128]{2,1,0:T(8,128)S(1)} %bitcast_add_fusion.7), channel_id=1, source_target_pairs={{1,0},{2,1},{3,2},{4,3},{5,4},{6,5},{7,6},{8,7},{9,8},{10,9},{11,1... | collective-permute-start | bytes 491528 | tf_op jit(solution)/shard_map/while/body/eval_jaxpr/ppermute | solution.py:14
  353.6 7.5 %collective-permute-start.1 = (f32[5,64,128]{2,1,0:T(8,128)S(1)}, f32[5,64,128]{2,1,0:T(8,128)S(1)}, u32[]{:S(2)}, u32[]{:S(2)}) collective-permute-start(f32[5,64,128]{2,1,0:T(8,128)S(1)} %bitcast_add_fusion.7), channel_id=1, source_target_pairs={{1,0},{2,1},{3,2},{4,3},{5,4},{6,5},{7,6},{8,7},{9,8},{10,9},{11,1... | collective-permute-start | bytes 491528 | tf_op jit(solution)/shard_map/while/body/eval_jaxpr/ppermute | solution.py:14
  362.2 7.5 %collective-permute-start.1 = (f32[5,64,128]{2,1,0:T(8,128)S(1)}, f32[5,64,128]{2,1,0:T(8,128)S(1)}, u32[]{:S(2)}, u32[]{:S(2)}) collective-permute-start(f32[5,64,128]{2,1,0:T(8,128)S(1)} %bitcast_add_fusion.7), channel_id=1, source_target_pairs={{1,0},{2,1},{3,2},{4,3},{5,4},{6,5},{7,6},{8,7},{9,8},{10,9},{11,1... | collective-permute-start | bytes 491528 | tf_op jit(solution)/shard_map/while/body/eval_jaxpr/ppermute | solution.py:14
  370.8 7.5 %collective-permute-start.1 = (f32[5,64,128]{2,1,0:T(8,128)S(1)}, f32[5,64,128]{2,1,0:T(8,128)S(1)}, u32[]{:S(2)}, u32[]{:S(2)}) collective-permute-start(f32[5,64,128]{2,1,0:T(8,128)S(1)} %bitcast_add_fusion.7), channel_id=1, source_target_pairs={{1,0},{2,1},{3,2},{4,3},{5,4},{6,5},{7,6},{8,7},{9,8},{10,9},{11,1... | collective-permute-start | bytes 491528 | tf_op jit(solution)/shard_map/while/body/eval_jaxpr/ppermute | solution.py:14
  379.4 7.5 %collective-permute-start.1 = (f32[5,64,128]{2,1,0:T(8,128)S(1)}, f32[5,64,128]{2,1,0:T(8,128)S(1)}, u32[]{:S(2)}, u32[]{:S(2)}) collective-permute-start(f32[5,64,128]{2,1,0:T(8,128)S(1)} %bitcast_add_fusion.7), channel_id=1, source_target_pairs={{1,0},{2,1},{3,2},{4,3},{5,4},{6,5},{7,6},{8,7},{9,8},{10,9},{11,1... | collective-permute-start | bytes 491528 | tf_op jit(solution)/shard_map/while/body/eval_jaxpr/ppermute | solution.py:14
  388.0 7.5 %collective-permute-start.1 = (f32[5,64,128]{2,1,0:T(8,128)S(1)}, f32[5,64,128]{2,1,0:T(8,128)S(1)}, u32[]{:S(2)}, u32[]{:S(2)}) collective-permute-start(f32[5,64,128]{2,1,0:T(8,128)S(1)} %bitcast_add_fusion.7), channel_id=1, source_target_pairs={{1,0},{2,1},{3,2},{4,3},{5,4},{6,5},{7,6},{8,7},{9,8},{10,9},{11,1... | collective-permute-start | bytes 491528 | tf_op jit(solution)/shard_map/while/body/eval_jaxpr/ppermute | solution.py:14
  396.6 7.5 %collective-permute-start.1 = (f32[5,64,128]{2,1,0:T(8,128)S(1)}, f32[5,64,128]{2,1,0:T(8,128)S(1)}, u32[]{:S(2)}, u32[]{:S(2)}) collective-permute-start(f32[5,64,128]{2,1,0:T(8,128)S(1)} %bitcast_add_fusion.7), channel_id=1, source_target_pairs={{1,0},{2,1},{3,2},{4,3},{5,4},{6,5},{7,6},{8,7},{9,8},{10,9},{11,1... | collective-permute-start | bytes 491528 | tf_op jit(solution)/shard_map/while/body/eval_jaxpr/ppermute | solution.py:14
  405.2 7.5 %collective-permute-start.1 = (f32[5,64,128]{2,1,0:T(8,128)S(1)}, f32[5,64,128]{2,1,0:T(8,128)S(1)}, u32[]{:S(2)}, u32[]{:S(2)}) collective-permute-start(f32[5,64,128]{2,1,0:T(8,128)S(1)} %bitcast_add_fusion.7), channel_id=1, source_target_pairs={{1,0},{2,1},{3,2},{4,3},{5,4},{6,5},{7,6},{8,7},{9,8},{10,9},{11,1... | collective-permute-start | bytes 491528 | tf_op jit(solution)/shard_map/while/body/eval_jaxpr/ppermute | solution.py:14
  413.8 7.5 %collective-permute-start.1 = (f32[5,64,128]{2,1,0:T(8,128)S(1)}, f32[5,64,128]{2,1,0:T(8,128)S(1)}, u32[]{:S(2)}, u32[]{:S(2)}) collective-permute-start(f32[5,64,128]{2,1,0:T(8,128)S(1)} %bitcast_add_fusion.7), channel_id=1, source_target_pairs={{1,0},{2,1},{3,2},{4,3},{5,4},{6,5},{7,6},{8,7},{9,8},{10,9},{11,1... | collective-permute-start | bytes 491528 | tf_op jit(solution)/shard_map/while/body/eval_jaxpr/ppermute | solution.py:14
  422.4 7.5 %collective-permute-start.1 = (f32[5,64,128]{2,1,0:T(8,128)S(1)}, f32[5,64,128]{2,1,0:T(8,128)S(1)}, u32[]{:S(2)}, u32[]{:S(2)}) collective-permute-start(f32[5,64,128]{2,1,0:T(8,128)S(1)} %bitcast_add_fusion.7), channel_id=1, source_target_pairs={{1,0},{2,1},{3,2},{4,3},{5,4},{6,5},{7,6},{8,7},{9,8},{10,9},{11,1... | collective-permute-start | bytes 491528 | tf_op jit(solution)/shard_map/while/body/eval_jaxpr/ppermute | solution.py:14
  431.0 7.5 %collective-permute-start.1 = (f32[5,64,128]{2,1,0:T(8,128)S(1)}, f32[5,64,128]{2,1,0:T(8,128)S(1)}, u32[]{:S(2)}, u32[]{:S(2)}) collective-permute-start(f32[5,64,128]{2,1,0:T(8,128)S(1)} %bitcast_add_fusion.7), channel_id=1, source_target_pairs={{1,0},{2,1},{3,2},{4,3},{5,4},{6,5},{7,6},{8,7},{9,8},{10,9},{11,1... | collective-permute-start | bytes 491528 | tf_op jit(solution)/shard_map/while/body/eval_jaxpr/ppermute | solution.py:14
  439.6 7.5 %collective-permute-start.1 = (f32[5,64,128]{2,1,0:T(8,128)S(1)}, f32[5,64,128]{2,1,0:T(8,128)S(1)}, u32[]{:S(2)}, u32[]{:S(2)}) collective-permute-start(f32[5,64,128]{2,1,0:T(8,128)S(1)} %bitcast_add_fusion.7), channel_id=1, source_target_pairs={{1,0},{2,1},{3,2},{4,3},{5,4},{6,5},{7,6},{8,7},{9,8},{10,9},{11,1... | collective-permute-start | bytes 491528 | tf_op jit(solution)/shard_map/while/body/eval_jaxpr/ppermute | solution.py:14
  448.2 7.5 %collective-permute-start.1 = (f32[5,64,128]{2,1,0:T(8,128)S(1)}, f32[5,64,128]{2,1,0:T(8,128)S(1)}, u32[]{:S(2)}, u32[]{:S(2)}) collective-permute-start(f32[5,64,128]{2,1,0:T(8,128)S(1)} %bitcast_add_fusion.7), channel_id=1, source_target_pairs={{1,0},{2,1},{3,2},{4,3},{5,4},{6,5},{7,6},{8,7},{9,8},{10,9},{11,1... | collective-permute-start | bytes 491528 | tf_op jit(solution)/shard_map/while/body/eval_jaxpr/ppermute | solution.py:14
  456.8 7.5 %collective-permute-start.1 = (f32[5,64,128]{2,1,0:T(8,128)S(1)}, f32[5,64,128]{2,1,0:T(8,128)S(1)}, u32[]{:S(2)}, u32[]{:S(2)}) collective-permute-start(f32[5,64,128]{2,1,0:T(8,128)S(1)} %bitcast_add_fusion.7), channel_id=1, source_target_pairs={{1,0},{2,1},{3,2},{4,3},{5,4},{6,5},{7,6},{8,7},{9,8},{10,9},{11,1... | collective-permute-start | bytes 491528 | tf_op jit(solution)/shard_map/while/body/eval_jaxpr/ppermute | solution.py:14
  465.4 7.5 %collective-permute-start.1 = (f32[5,64,128]{2,1,0:T(8,128)S(1)}, f32[5,64,128]{2,1,0:T(8,128)S(1)}, u32[]{:S(2)}, u32[]{:S(2)}) collective-permute-start(f32[5,64,128]{2,1,0:T(8,128)S(1)} %bitcast_add_fusion.7), channel_id=1, source_target_pairs={{1,0},{2,1},{3,2},{4,3},{5,4},{6,5},{7,6},{8,7},{9,8},{10,9},{11,1... | collective-permute-start | bytes 491528 | tf_op jit(solution)/shard_map/while/body/eval_jaxpr/ppermute | solution.py:14
  474.0 7.5 %collective-permute-start.1 = (f32[5,64,128]{2,1,0:T(8,128)S(1)}, f32[5,64,128]{2,1,0:T(8,128)S(1)}, u32[]{:S(2)}, u32[]{:S(2)}) collective-permute-start(f32[5,64,128]{2,1,0:T(8,128)S(1)} %bitcast_add_fusion.7), channel_id=1, source_target_pairs={{1,0},{2,1},{3,2},{4,3},{5,4},{6,5},{7,6},{8,7},{9,8},{10,9},{11,1... | collective-permute-start | bytes 491528 | tf_op jit(solution)/shard_map/while/body/eval_jaxpr/ppermute | solution.py:14
  482.6 7.5 %collective-permute-start.1 = (f32[5,64,128]{2,1,0:T(8,128)S(1)}, f32[5,64,128]{2,1,0:T(8,128)S(1)}, u32[]{:S(2)}, u32[]{:S(2)}) collective-permute-start(f32[5,64,128]{2,1,0:T(8,128)S(1)} %bitcast_add_fusion.7), channel_id=1, source_target_pairs={{1,0},{2,1},{3,2},{4,3},{5,4},{6,5},{7,6},{8,7},{9,8},{10,9},{11,1... | collective-permute-start | bytes 491528 | tf_op jit(solution)/shard_map/while/body/eval_jaxpr/ppermute | solution.py:14
  491.2 7.5 %collective-permute-start.1 = (f32[5,64,128]{2,1,0:T(8,128)S(1)}, f32[5,64,128]{2,1,0:T(8,128)S(1)}, u32[]{:S(2)}, u32[]{:S(2)}) collective-permute-start(f32[5,64,128]{2,1,0:T(8,128)S(1)} %bitcast_add_fusion.7), channel_id=1, source_target_pairs={{1,0},{2,1},{3,2},{4,3},{5,4},{6,5},{7,6},{8,7},{9,8},{10,9},{11,1... | collective-permute-start | bytes 491528 | tf_op jit(solution)/shard_map/while/body/eval_jaxpr/ppermute | solution.py:14
  499.8 7.5 %collective-permute-start.1 = (f32[5,64,128]{2,1,0:T(8,128)S(1)}, f32[5,64,128]{2,1,0:T(8,128)S(1)}, u32[]{:S(2)}, u32[]{:S(2)}) collective-permute-start(f32[5,64,128]{2,1,0:T(8,128)S(1)} %bitcast_add_fusion.7), channel_id=1, source_target_pairs={{1,0},{2,1},{3,2},{4,3},{5,4},{6,5},{7,6},{8,7},{9,8},{10,9},{11,1... | collective-permute-start | bytes 491528 | tf_op jit(solution)/shard_map/while/body/eval_jaxpr/ppermute | solution.py:14
  508.4 7.5 %collective-permute-start.1 = (f32[5,64,128]{2,1,0:T(8,128)S(1)}, f32[5,64,128]{2,1,0:T(8,128)S(1)}, u32[]{:S(2)}, u32[]{:S(2)}) collective-permute-start(f32[5,64,128]{2,1,0:T(8,128)S(1)} %bitcast_add_fusion.7), channel_id=1, source_target_pairs={{1,0},{2,1},{3,2},{4,3},{5,4},{6,5},{7,6},{8,7},{9,8},{10,9},{11,1... | collective-permute-start | bytes 491528 | tf_op jit(solution)/shard_map/while/body/eval_jaxpr/ppermute | solution.py:14
  517.0 7.5 %collective-permute-start.1 = (f32[5,64,128]{2,1,0:T(8,128)S(1)}, f32[5,64,128]{2,1,0:T(8,128)S(1)}, u32[]{:S(2)}, u32[]{:S(2)}) collective-permute-start(f32[5,64,128]{2,1,0:T(8,128)S(1)} %bitcast_add_fusion.7), channel_id=1, source_target_pairs={{1,0},{2,1},{3,2},{4,3},{5,4},{6,5},{7,6},{8,7},{9,8},{10,9},{11,1... | collective-permute-start | bytes 491528 | tf_op jit(solution)/shard_map/while/body/eval_jaxpr/ppermute | solution.py:14
  525.6 7.5 %collective-permute-start.1 = (f32[5,64,128]{2,1,0:T(8,128)S(1)}, f32[5,64,128]{2,1,0:T(8,128)S(1)}, u32[]{:S(2)}, u32[]{:S(2)}) collective-permute-start(f32[5,64,128]{2,1,0:T(8,128)S(1)} %bitcast_add_fusion.7), channel_id=1, source_target_pairs={{1,0},{2,1},{3,2},{4,3},{5,4},{6,5},{7,6},{8,7},{9,8},{10,9},{11,1... | collective-permute-start | bytes 491528 | tf_op jit(solution)/shard_map/while/body/eval_jaxpr/ppermute | solution.py:14
  534.2 7.5 %collective-permute-start.1 = (f32[5,64,128]{2,1,0:T(8,128)S(1)}, f32[5,64,128]{2,1,0:T(8,128)S(1)}, u32[]{:S(2)}, u32[]{:S(2)}) collective-permute-start(f32[5,64,128]{2,1,0:T(8,128)S(1)} %bitcast_add_fusion.7), channel_id=1, source_target_pairs={{1,0},{2,1},{3,2},{4,3},{5,4},{6,5},{7,6},{8,7},{9,8},{10,9},{11,1... | collective-permute-start | bytes 491528 | tf_op jit(solution)/shard_map/while/body/eval_jaxpr/ppermute | solution.py:14
  567.3 33.4 %copy-start.14 = (f32[2,40,256]{2,1,0:T(8,128)}, f32[2,40,256]{2,1,0:T(8,128)S(1)}, u32[]{:S(2)}) copy-start(f32[2,40,256]{2,1,0:T(8,128)S(1)} %get-tuple-element.2360) | copy-start | bytes 245764 | tf_op jit(solution)/shard_map/transpose(jvp())/while
  646.9 33.4 %copy-start.14 = (f32[2,40,256]{2,1,0:T(8,128)}, f32[2,40,256]{2,1,0:T(8,128)S(1)}, u32[]{:S(2)}) copy-start(f32[2,40,256]{2,1,0:T(8,128)S(1)} %get-tuple-element.2360) | copy-start | bytes 245764 | tf_op jit(solution)/shard_map/transpose(jvp())/while
  (58 other events, 361.9 us)
where the time goes:
time: 757 us; the launch traced here: 746 us
  waiting for transfers between devices  178 us (24%)
  starting transfers between devices  164 us (22%)
  matrix products  154 us (20%)
  other arithmetic  113 us (15%)
  local copies, waits for them, and re-layouts  110 us (15%)
  loops' own time  25.7 us (3%)
    ppermute x46, waiting for transfers between devices, from_behind(): lax.ppermute(value, axis, [(source, source + steps) for source in range(f...  178 us
    ppermute x46, starting transfers between devices, from_behind(): lax.ppermute(value, axis, [(source, source + steps) for source in range(f...  164 us
    dot_general x6, matrix products, advance(): jnp.einsum('hts,shp->thp', mixing, values, precision=lax.Precision.HIGHEST)  89.3 us
    unnamed x17, local copies, waits for them, and re-layouts  35.6 us
    dynamic_update_slice x8, other arithmetic, block_pass(): lax.scan(advance, start_state, (shaped, decays, writes, reads))  34.5 us
    dot_general x6, matrix products, advance(): jnp.einsum('shp,sn->hpn', values * tail_weight[:, :, None], write_block,...  29.8 us
    add x23, other arithmetic, forward_turn(): outgoing = own_retain[:, None, None] * incoming + own_state  23.1 us
    add x23, other arithmetic, backward_turn(): outgoing = own_retain[:, None, None] * incoming + own_grad  23.1 us
  transfers between devices with their start and end apart: 46, of which 46 were waited for; matrix products, arithmetic and copies ran while one was open for 0% of the time, Pallas kernels for 0%

commit v1 on v0

v1 whole, which is shorter than its diff:
```python
import functools

import jax
import jax.numpy as jnp
from jax import lax
from jax.experimental import pallas as pl
from jax.experimental.pallas import tpu as pltpu
from jax.sharding import PartitionSpec as P

CHUNK = 128
LANES = 512
GROUPS = (3, 2)
F32 = jnp.float32
BF16 = jnp.bfloat16


def dot(a, b):
    return lax.dot_general(a, b, (((1,), (0,)), ((), ())), preferred_element_type=F32)


def dot_nt(a, b):
    return lax.dot_general(a, b, (((1,), (1,)), ((), ())), preferred_element_type=F32)


def split(x):
    high = x.astype(BF16)
    return high, (x - high.astype(F32)).astype(BF16)


def split3(x):
    high = x.astype(BF16)
    rest = x - high.astype(F32)
    middle = rest.astype(BF16)
    return high, middle, (rest - middle.astype(F32)).astype(BF16)


def three(product, a, b):
    return product(a[0], b[0]) + product(a[0], b[1]) + product(a[1], b[0])


def iota(shape, axis):
    return lax.broadcasted_iota(jnp.int32, shape, axis)


def fold3(x, heads):
    high, middle, low = split3(x)
    column = iota(x.shape, 1)
    chosen = jnp.where(
        column < heads,
        high.astype(F32),
        jnp.where(column < 2 * heads, middle.astype(F32), low.astype(F32)),
    )
    return chosen.astype(BF16)


def spread_matrix(rows, lanes, first, heads, width):
    row, lane = iota((rows, lanes), 0), iota((rows, lanes), 1)
    hit = None
    for copy in range(3):
        start = (row - (first + copy * heads)) * width
        one = jnp.logical_and(lane >= start, lane < start + width)
        hit = one if hit is None else jnp.logical_or(hit, one)
    return jnp.where(hit, 1.0, 0.0).astype(BF16)


def pack_decay(packed, decay_ref, heads):
    packed[...] = jnp.zeros_like(packed)
    for copy in range(3):
        packed[copy * heads : (copy + 1) * heads, :] = decay_ref[...]


def state_kernel(
    slot_ref, decay_ref, write_ref, read_ref, x_ref, g_ref, keep_ref, send_ref,
    packed, tail, lead, write_t, read_t, stage, *, first_head, heads, width
):
    step = pl.program_id(0)
    rows, lanes = x_ref.shape
    state = write_ref.shape[1]
    quarter = state // 4

    @pl.when(step == 0)
    def _():
        pack_decay(packed, decay_ref, heads)
        parts = split3(packed[...])
        t, u = iota((rows, rows), 0), iota((rows, rows), 1)
        before = jnp.where(u <= t, 1.0, 0.0).astype(BF16)
        after = jnp.where(u > t, 1.0, 0.0).astype(BF16)
        lead[...] = fold3(jnp.exp(sum(dot_nt(before, p) for p in parts)), heads)
        tail[...] = fold3(jnp.exp(sum(dot_nt(after, p) for p in parts)), heads)
        write_t[0], write_t[1] = split(write_ref[...].T)
        read_t[0], read_t[1] = split(read_ref[...].T)

    first = first_head + step * (lanes // width)
    spread = spread_matrix(packed.shape[0], lanes, first, heads, width)
    slot = slot_ref[0]
    for which, (value_ref, weight, factor) in enumerate(
        ((x_ref, tail, write_t), (g_ref, lead, read_t))
    ):
        scaled = split(value_ref[...] * dot(weight[...], spread))
        stage[which] = three(dot, (factor[0], factor[1]), scaled)
        for relative in range(4):
            start = pl.multiple_of((slot ^ relative) * quarter, quarter)
            target = keep_ref if relative < 2 else send_ref
            target[which, relative % 2] = stage[which, pl.ds(start, quarter), :]


def block_kernel(
    slot_ref, decay_ref, write_ref, read_ref, skip_ref, x_ref, g_ref, mine_ref, other_ref,
    *refs, first_head, heads, width, chained
):
    if chained:
        _, _, old_decay, old_write, old_read, *refs = refs
    (
        y_ref, dx_ref, gd_ref, gw_ref, gr_ref,
        packed, up, down, edges, left_y, left_x, write_t, read_t,
        row_sums, acc_read, acc_write, state_in, grad_in, ups, downs, right_h, right_l, held, inner
    ) = refs
    step, last = pl.program_id(0), pl.num_programs(0) - 1
    rows, lanes = x_ref.shape
    state = write_ref.shape[1]
    quarter = state // 4
    count = rows // CHUNK
    middle = CHUNK // 2 - 1
    span = [slice(i * CHUNK, (i + 1) * CHUNK) for i in range(count)]

    @pl.when(step == 0)
    def _():
        pack_decay(packed, decay_ref, heads)
        t, u = iota((CHUNK, CHUNK), 0), iota((CHUNK, CHUNK), 1)
        ahead = jnp.logical_and(u > middle, u <= t)
        behind = jnp.logical_and(u <= middle, u > t)
        signed = jnp.where(ahead, 1.0, jnp.where(behind, -1.0, 0.0)).astype(BF16)
        row, column = iota((16, CHUNK), 0), iota((16, CHUNK), 1)
        half = jnp.where((row == 0) == (column <= middle), 1.0, 0.0).astype(BF16)
        for i in range(count):
            parts = split3(packed[:, span[i]])
            gap = sum(dot_nt(signed, p) for p in parts)
            up[span[i], :] = fold3(jnp.exp(gap), heads)
            down[span[i], :] = fold3(jnp.exp(-gap), heads)
            edges[i] = fold3(jnp.exp(sum(dot_nt(half, p) for p in parts)), heads)
            write, read = write_ref[span[i], :], read_ref[span[i], :]
            write_p, read_p = split(write), split(read)
            scores = jnp.where(u <= t, three(dot_nt, read_p, write_p), 0.0)
            left_y[0, i], left_y[1, i] = split(jnp.concatenate([scores, read], 1))
            scores = jnp.where(u >= t, three(dot_nt, write_p, read_p), 0.0)
            left_x[0, i], left_x[1, i] = split(jnp.concatenate([scores, write], 1))
            write_t[i] = jnp.concatenate(split(write.T), 1)
            read_t[i] = jnp.concatenate(split(read.T), 1)
        row_sums[...] = jnp.zeros_like(row_sums)
        acc_read[...] = jnp.zeros_like(acc_read)
        acc_write[...] = jnp.zeros_like(acc_write)

    first = first_head + step * (lanes // width)
    spread = spread_matrix(packed.shape[0], lanes, first, heads, width)
    ups[...] = dot(up[...], spread)
    downs[...] = dot(down[...], spread)
    edge = [dot(edges[i], spread) for i in range(count)]
    skip = skip_ref[...]
    slot = slot_ref[0]
    for relative in range(4):
        start = pl.multiple_of((slot ^ relative) * quarter, quarter)
        source = mine_ref if relative < 2 else other_ref
        state_in[pl.ds(start, quarter), :] = source[0, relative % 2]
        grad_in[pl.ds(start, quarter), :] = source[1, relative % 2]

    carried = edge[0][0:1] * state_in[...]
    for i in range(count):
        x = x_ref[span[i], :]
        xh, xl = split(x * downs[span[i], :])
        ph, pl_ = split(carried)
        right_h[i] = jnp.concatenate([xh, ph], 0)
        right_l[i] = jnp.concatenate([xl, pl_], 0)
        made = three(dot, (left_y[0, i], left_y[1, i]), (right_h[i], right_l[i]))
        made = made * ups[span[i], :]
        y_ref[span[i], :] = made + skip * x
        inner[span[i], :] = made * g_ref[span[i], :]
        gained = dot(write_t[i], jnp.concatenate([xh, xh], 0)) + dot(write_t[i, :, :CHUNK], xl)
        total = carried + gained
        held[i] = total
        if i + 1 < count:
            carried = edge[i + 1][0:1] * (edge[i][1:2] * total)

    row, lane = iota((lanes, packed.shape[0]), 0), iota((lanes, packed.shape[0]), 1)
    begin = (lane - first) * width
    gather = jnp.where(jnp.logical_and(row >= begin, row < begin + width), 1.0, 0.0).astype(BF16)
    bottom = iota((CHUNK, 1), 0) == CHUNK - 1
    carried = edge[count - 1][1:2] * grad_in[...]
    for i in reversed(range(count)):
        g = g_ref[span[i], :]
        x = x_ref[span[i], :]
        gh, gl = split(g * ups[span[i], :])
        qh, ql = split(carried)
        right = (jnp.concatenate([gh, qh], 0), jnp.concatenate([gl, ql], 0))
        made = three(dot, (left_x[0, i], left_x[1, i]), right) * downs[span[i], :]
        dx_ref[span[i], :] = made + skip * g
        flow = jnp.sum(held[i] * carried, axis=0, keepdims=True)
        change = inner[span[i], :] - x * made + jnp.where(bottom, flow, 0.0)
        ch, cl = split(change)
        row_sums[span[i], :] += dot(ch, gather) + dot(cl, gather)
        acc_read[i] += three(dot_nt, (gh, gl), (right_h[i], right_l[i]))
        acc_write[i] += dot_nt(right_h[i, :CHUNK], jnp.concatenate([qh, ql], 0))
        acc_write[i, :, :state] += dot_nt(right_l[i, :CHUNK], qh)
        if i > 0:
            gained = dot(read_t[i], jnp.concatenate([gh, gh], 0)) + dot(read_t[i, :, :CHUNK], gl)
            carried = edge[i - 1][1:2] * (edge[i][0:1] * (carried + gained))

    @pl.when(step == last)
    def _():
        t, u = iota((CHUNK, CHUNK), 0), iota((CHUNK, CHUNK), 1)
        until = jnp.where(t >= u, 1.0, 0.0).astype(BF16)
        for i in range(count):
            scores = jnp.where(u <= t, acc_read[i, :, :CHUNK], 0.0)
            write, read = split(write_ref[span[i], :]), split(read_ref[span[i], :])
            grad_read = acc_read[i, :, CHUNK:] + three(dot, split(scores), write)
            grad_write = acc_write[i, :, :state] + acc_write[i, :, state:]
            grad_write = grad_write + three(dot, split(scores.T), read)
            parts = split3(row_sums[span[i], :].T)
            decay = sum(dot(p, until) for p in parts)[:heads]
            if chained:
                grad_read = grad_read + old_read[span[i], :]
                grad_write = grad_write + old_write[span[i], :]
                decay = decay + old_decay[:, span[i]]
            gr_ref[span[i], :] = grad_read
            gw_ref[span[i], :] = grad_write
            gd_ref[:, span[i]] = decay


def whole(shape):
    return pl.BlockSpec(shape, lambda *_: (0,) * len(shape))


def make_states(slot, log_decay, state_write, state_read, inputs, grad_output, first, blocks):
    rows, columns = inputs.shape
    heads, state = log_decay.shape[0], state_write.shape[1]
    quarter = state // 4
    pack = 128
    wide = pl.BlockSpec((rows, LANES), lambda j, _: (0, first + j))
    part = pl.BlockSpec((2, 2, quarter, LANES), lambda j, _: (0, 0, 0, j))
    shape = jax.ShapeDtypeStruct((2, 2, quarter, blocks * LANES), F32)
    width = columns // heads
    return pl.pallas_call(
        functools.partial(state_kernel, first_head=first * LANES // width, heads=heads, width=width),
        out_shape=(shape, shape),
        grid_spec=pltpu.PrefetchScalarGridSpec(
            num_scalar_prefetch=1,
            grid=(blocks,),
            in_specs=[
                whole((heads, rows)), whole((rows, state)), whole((rows, state)), wide, wide
            ],
            out_specs=(part, part),
            scratch_shapes=[
                pltpu.VMEM((pack, rows), F32),
                pltpu.VMEM((rows, pack), BF16),
                pltpu.VMEM((rows, pack), BF16),
                pltpu.VMEM((2, state, rows), BF16),
                pltpu.VMEM((2, state, rows), BF16),
                pltpu.VMEM((2, state, LANES), F32),
            ],
        ),
        compiler_params=pltpu.CompilerParams(vmem_limit_bytes=40 << 20),
        cost_estimate=pl.CostEstimate(
            flops=12 * rows * state * blocks * LANES,
            bytes_accessed=8 * rows * blocks * LANES,
            transcendentals=0,
        ),
    )(slot, log_decay, state_write, state_read, inputs, grad_output)


def make_outputs(
    slot, log_decay, state_write, state_read, skip, inputs, grad_output, mine, other, first, blocks,
    earlier
):
    rows, columns = inputs.shape
    heads, state = log_decay.shape[0], state_write.shape[1]
    quarter, count = state // 4, rows // CHUNK
    pack = 128
    wide = pl.BlockSpec((rows, LANES), lambda j, _: (0, first + j))
    part = pl.BlockSpec((2, 2, quarter, LANES), lambda j, _: (0, 0, 0, j))
    line = pl.BlockSpec((1, LANES), lambda j, _: (0, first + j))
    small = [whole((heads, rows)), whole((rows, state)), whole((rows, state))]
    in_specs = [*small, line, wide, wide, part, part]
    operands = [log_decay, state_write, state_read, skip, inputs, grad_output, mine, other]
    aliases = {}
    if earlier is not None:
        aliases = {9: 0, 10: 1}
        in_specs += [pl.BlockSpec(memory_space=pl.ANY)] * 2 + small
        operands += earlier
    width = columns // heads
    large = jax.ShapeDtypeStruct((rows, columns), F32)
    side = jax.ShapeDtypeStruct((rows, state), F32)
    return pl.pallas_call(
        functools.partial(
            block_kernel,
            first_head=first * LANES // width,
            heads=heads,
            width=width,
            chained=earlier is not None,
        ),
        out_shape=(large, large, jax.ShapeDtypeStruct((heads, rows), F32), side, side),
        grid_spec=pltpu.PrefetchScalarGridSpec(
            num_scalar_prefetch=1,
            grid=(blocks,),
            in_specs=in_specs,
            out_specs=(wide, wide, *small),
            scratch_shapes=[
                pltpu.VMEM((pack, rows), F32),
                pltpu.VMEM((rows, pack), BF16),
                pltpu.VMEM((rows, pack), BF16),
                pltpu.VMEM((count, 16, pack), BF16),
                pltpu.VMEM((2, count, CHUNK, CHUNK + state), BF16),
                pltpu.VMEM((2, count, CHUNK, CHUNK + state), BF16),
                pltpu.VMEM((count, state, 2 * CHUNK), BF16),
                pltpu.VMEM((count, state, 2 * CHUNK), BF16),
                pltpu.VMEM((rows, pack), F32),
                pltpu.VMEM((count, CHUNK, CHUNK + state), F32),
                pltpu.VMEM((count, CHUNK, 2 * state), F32),
                pltpu.VMEM((state, LANES), F32),
                pltpu.VMEM((state, LANES), F32),
                pltpu.VMEM((rows, LANES), F32),
                pltpu.VMEM((rows, LANES), F32),
                pltpu.VMEM((count, CHUNK + state, LANES), BF16),
                pltpu.VMEM((count, CHUNK + state, LANES), BF16),
                pltpu.VMEM((count, state, LANES), F32),
                pltpu.VMEM((rows, LANES), F32),
            ],
        ),
        input_output_aliases=aliases,
        compiler_params=pltpu.CompilerParams(vmem_limit_bytes=48 << 20),
        cost_estimate=pl.CostEstimate(
            flops=48 * rows * state * blocks * LANES,
            bytes_accessed=16 * rows * blocks * LANES,
            transcendentals=0,
        ),
    )(slot, *operands)


def local(inputs, log_decay, state_write, state_read, skip_gain, grad_output):
    heads = log_decay.shape[0]
    rows, columns = inputs.shape
    width = columns // heads
    devices, position = lax.axis_size("seq"), lax.axis_index("seq")
    planes = devices // 4
    core, chip, plane = position % 2, (position // 2) % 2, position // 4
    slot = (core * 2 + chip).astype(jnp.int32).reshape(1)
    swap_core = [(i, i ^ 1) for i in range(devices)]
    swap_chip = [(i, i ^ 2) for i in range(devices)]

    total = jnp.sum(log_decay, axis=1)
    twin = lax.ppermute(total, "seq", swap_core)
    here = total + twin
    beside = lax.ppermute(here, "seq", swap_chip)
    is_c0, is_y0 = core == 0, chip == 0
    logs = jnp.stack(
        [
            jnp.where(is_c0, total, twin),
            jnp.where(is_c0, twin, total),
            jnp.where(is_y0, here, beside),
            jnp.where(is_y0, beside, here),
            here + beside,
        ]
    )
    keepers = jnp.repeat(jnp.exp(logs), width, axis=1)
    one = jnp.ones((columns,), F32)
    skip = jnp.repeat(skip_gain, width).reshape(1, columns)

    def travel(first, blocks):
        lanes = slice(first * LANES, (first + blocks) * LANES)
        c0, c1, y0, y1, whole_plane = keepers[:, lanes]
        ones = one[lanes]
        keep, send = make_states(
            slot, log_decay, state_write, state_read, inputs, grad_output, first, blocks
        )
        near_core = lax.ppermute(send, "seq", swap_core)
        chip_f = jnp.where(is_c0, c1, ones) * keep[0] + jnp.where(is_c0, ones, c1) * near_core[0]
        chip_b = jnp.where(is_c0, ones, c0) * keep[1] + jnp.where(is_c0, c0, ones) * near_core[1]
        near_chip = lax.ppermute(jnp.stack([chip_f[1], chip_b[1]]), "seq", swap_chip)
        plane_f = jnp.where(is_y0, y1, ones) * chip_f[0] + jnp.where(is_y0, ones, y1) * near_chip[0]
        plane_b = jnp.where(is_y0, ones, y0) * chip_b[0] + jnp.where(is_y0, y0, ones) * near_chip[1]
        ahead = jnp.zeros_like(plane_f)
        back = jnp.zeros_like(plane_b)
        for hop in range(planes - 1):
            mirror = planes - 1 - hop
            going = jnp.where(
                plane == hop, whole_plane * ahead + plane_f, whole_plane * back + plane_b
            )
            pairs = [
                (source * 4 + i, target * 4 + i)
                for source, target in ((hop, hop + 1), (mirror, mirror - 1))
                for i in range(4)
            ]
            came = lax.ppermute(going, "seq", pairs)
            ahead = jnp.where(plane == hop + 1, came, ahead)
            back = jnp.where(plane == mirror - 1, came, back)
        mine = jnp.stack(
            [
                jnp.where(is_y0, ahead, y0 * ahead + near_chip[0]),
                jnp.where(is_y0, y1 * back + near_chip[1], back),
            ]
        )
        theirs = jnp.stack(
            [
                jnp.where(is_y0, y0 * ahead + chip_f[0], ahead),
                jnp.where(is_y0, back, y1 * back + chip_b[0]),
            ]
        )
        came = lax.ppermute(theirs, "seq", swap_chip)
        into_f = jnp.stack([mine[0], came[0]])
        into_b = jnp.stack([mine[1], came[1]])
        mine = jnp.stack(
            [
                jnp.where(is_c0, into_f, c0 * into_f + near_core[0]),
                jnp.where(is_c0, c1 * into_b + near_core[1], into_b),
            ]
        )
        theirs = jnp.stack(
            [
                jnp.where(is_c0, c0 * into_f + keep[0], into_f),
                jnp.where(is_c0, into_b, c1 * into_b + keep[1]),
            ]
        )
        return mine, lax.ppermute(theirs, "seq", swap_core)

    states = []
    first = 0
    for blocks in GROUPS:
        states.append((first, blocks, travel(first, blocks)))
        first += blocks
    results = None
    for first, blocks, (mine, other) in states:
        results = make_outputs(
            slot, log_decay, state_write, state_read, skip, inputs, grad_output, mine, other, first,
            blocks, results
        )
    outputs, grad_inputs, grad_decay, grad_write, grad_read = results
    return (outputs, grad_inputs, grad_decay, grad_write, grad_read)


def solution(mesh):
    in_specs = (
        P(("group", "seq"), None),
        P(None, ("group", "seq")),
        P(("group", "seq"), None),
        P(("group", "seq"), None),
        P(),
        P(("group", "seq"), None),
    )
    out_specs = (
        P(("group", "seq"), None),
        P(("group", "seq"), None),
        P(None, ("group", "seq")),
        P(("group", "seq"), None),
        P(("group", "seq"), None),
    )
    return jax.shard_map(local, mesh=mesh, in_specs=in_specs, out_specs=out_specs, check_vma=False)
```

time: 757 us -> 114 us (0.15)
  the two profiles are of different devices: /device:TPU:13 before, /device:TPU:1 now
where the time goes in v1:
time: 114 us; the launch traced here: 112 us
  Pallas kernels  43.8 us (38%)
  starting transfers between devices  25.8 us (23%)
  waiting for transfers between devices  19.9 us (17%)
  local copies, waits for them, and re-layouts  11.2 us (10%)
  other arithmetic  10.4 us (9%)
  between operations  1.22 us (1%)
    pallas_call x2, Pallas kernels, make_outputs(): pl.pallas_call(functools.partial(block_kernel, first_head=first * LANES /...  34.3 us
    ppermute x6, starting transfers between devices, travel(): came = lax.ppermute(going, 'seq', pairs)  10.2 us
    pallas_call x2, Pallas kernels, make_states(): pl.pallas_call(functools.partial(state_kernel, first_head=first * LANES /...  9.51 us
    ppermute x2, waiting for transfers between devices, travel(): lax.ppermute(jnp.stack([chip_f[1], chip_b[1]]), 'seq', swap_chip)  9.2 us
    ppermute x6, waiting for transfers between devices, travel(): came = lax.ppermute(going, 'seq', pairs)  8.07 us
    ppermute x2, starting transfers between devices, travel(): return (mine, lax.ppermute(theirs, 'seq', swap_core))  8.01 us
    unnamed x26, local copies, waits for them, and re-layouts  7.8 us
    another operation x2, other arithmetic, travel(): c0, c1, y0, y1, whole_plane = keepers[:, lanes]  2.79 us
  transfers between devices with their start and end apart: 16, of which 7 were waited for; matrix products, arithmetic and copies ran while one was open for 11% of the time, Pallas kernels for 26%

profile of v1, /device:TPU:1, one launch (start us, length us, event | category | flops | bytes accessed | tf_op | source)
XLA Modules:
  0.0 112.5 jit_solution(10643407156386019419)
XLA Ops:
  0.6 1.0 reduce_sum.9
  1.6 0.1 collective-permute-start
  1.8 2.5 %copy-done = f32[512,2560]{1,0:T(8,128)S(1)} copy-done((f32[512,2560]{1,0:T(8,128)S(1)}, f32[512,2560]{1,0:T(8,128)}, u32[]{:S(2)}) %copy-start) | copy-done | bytes 5242904
  4.2 2.5 %copy-done.1 = f32[512,2560]{1,0:T(8,128)S(1)} copy-done((f32[512,2560]{1,0:T(8,128)S(1)}, f32[512,2560]{1,0:T(8,128)}, u32[]{:S(2)}) %copy-start.1) | copy-done | bytes 5242904
  6.7 0.9 copy-done.2
  7.7 0.9 copy-done.4
  8.6 0.9 copy-done.6
  9.5 4.0 %shard_map.101 = (f32[2,2,32,1024]{3,2,1,0:T(8,128)S(1)}, f32[2,2,32,1024]{3,2,1,0:T(8,128)S(1)}) custom-call(s32[1]{0:T(128)} %bitcast.slot_ref, f32[40,512]{1,0:T(8,128)S(1)} %copy-done.6, f32[512,128]{1,0:T(8,128)S(1)} %copy-done.2, f32[512,128]{1,0:T(8,128)S(1)} %copy-done.4, f32[512,2560]{1,0:T(8,128)S(1)} %copy-done, f32[512,2560]{1,0:T(8,128)S(1)} %copy-done.1), custom_call_target="tpu_custom_call" | custom-call | flops 805306368 | bytes 4194304 | tf_op jit(solution)/shard_map/pallas_call | solution.py:241
  13.5 0.5 collective-permute-start.2
  14.1 5.5 %shard_map.102 = (f32[2,2,32,1536]{3,2,1,0:T(8,128)S(1)}, f32[2,2,32,1536]{3,2,1,0:T(8,128)S(1)}) custom-call(s32[1]{0:T(128)} %bitcast.slot_ref, f32[40,512]{1,0:T(8,128)S(1)} %copy-done.6, f32[512,128]{1,0:T(8,128)S(1)} %copy-done.2, f32[512,128]{1,0:T(8,128)S(1)} %copy-done.4, f32[512,2560]{1,0:T(8,128)S(1)} %copy-done, f32[512,2560]{1,0:T(8,128)S(1)} %copy-done.1), custom_call_target="tpu_custom_call" | custom-call | flops 1207959552 | bytes 6291456 | tf_op jit(solution)/shard_map/pallas_call | solution.py:241
  19.6 0.1 collective-permute-start.9
  19.7 2.7 %collective-permute-start.1 = (f32[40]{0:T(128)S(1)}, f32[40]{0:T(128)S(1)}, u32[]{:S(2)}, u32[]{:S(2)}) collective-permute-start(f32[40]{0:T(128)S(1)} %get-tuple-element.92), channel_id=1, source_target_pairs={{0,2},{1,3},{2,0},{3,1},{4,6},{5,7},{6,4},{7,5},{8,10},{9,11},{10,... | collective-permute-start | bytes 488 | tf_op jit(solution)/shard_map/ppermute | solution.py:351
  22.4 0.9 collective-permute-done.1
  23.3 0.1 broadcast_in_dim.5
  23.4 0.7 reshape.193
  24.2 1.1 %slice_reduce_fusion.3 = (f32[1536]{0:T(1024)S(1)}, f32[1536]{0:T(1024)S(1)}, f32[1536]{0:T(1024)S(1)}, f32[1536]{0:T(1024)S(1)}, f32[1536]{0:T(1024)S(1)}, /*in...) fusion(f32[5,2560]{1,0:T(8,128)} %reshape.193, pred[]{:T(512)S(6)} %eq.16), kind=kLoop, calls=%fused_computation.104 | loop fusion | flops 6144 | bytes 86017 | tf_op jit(solution)/shard_map/unstack | solution.py:368
  25.4 1.6 %fusion.12 = (f32[1,1024]{1,0:T(1,128)}, f32[1,1024]{1,0:T(1,128)S(1)}, f32[1,1024]{1,0:T(1,128)S(1)}, f32[1,1024]{1,0:T(1,128)S(1)}, f32[1,1024]{1,0:T(1,128)S(...) fusion(f32[5,2560]{1,0:T(8,128)} %reshape.193, pred[]{:T(512)S(6)} %eq.16), kind=kLoop, calls=%fused_computation.106 | loop fusion | flops 4096 | bytes 57345 | tf_op jit(solution)/shard_map/unstack | solution.py:368
  27.0 0.1 fusion.1
  27.3 1.5 %collective-permute-start.10 = (f32[2,32,1536]{2,1,0:T(8,128)S(1)}, f32[2,32,1536]{2,1,0:T(8,128)S(1)}, u32[]{:S(2)}, u32[]{:S(2)}) collective-permute-start(f32[2,32,1536]{2,1,0:T(8,128)S(1)} %pad_maximum_fusion.4), channel_id=1, source_target_pairs={{0,2},{1,3},{2,0},{3,1},{4,6},{5,7},{6,4},{7,5},{8,10},{9,11},{10,... | collective-permute-start | bytes 1179656 | tf_op jit(solution)/shard_map/ppermute | solution.py:376
  28.8 1.1 fusion.3
  30.0 0.1 collective-permute-start.3
  30.1 6.8 %collective-permute-done.10 = f32[2,32,1536]{2,1,0:T(8,128)S(1)} collective-permute-done((f32[2,32,1536]{2,1,0:T(8,128)S(1)}, f32[2,32,1536]{2,1,0:T(8,128)S(1)}, u32[]{:S(2)}, u32[]{:S(2)}) %collective-permute-start.10) | collective-permute-done | bytes 393248 | tf_op jit(solution)/shard_map/ppermute | solution.py:376
  37.0 3.2 %collective-permute-start.11 = (f32[32,1536]{1,0:T(8,128)S(1)}, f32[32,1536]{1,0:T(8,128)S(1)}, u32[]{:S(2)}, u32[]{:S(2)}) collective-permute-start(f32[32,1536]{1,0:T(8,128)S(1)} %get-tuple-element.35), channel_id=1, source_target_pairs={{0,4},{1,5},{2,6},{3,7},{12,8},{13,9},{14,10},{15,11},{16,20},{17,... | collective-permute-start | bytes 589832 | tf_op jit(solution)/shard_map/ppermute | solution.py:391
  40.2 2.4 %collective-permute-done.3 = f32[2,32,1024]{2,1,0:T(8,128)S(1)} collective-permute-done((f32[2,32,1024]{2,1,0:T(8,128)S(1)}, f32[2,32,1024]{2,1,0:T(8,128)S(1)}, u32[]{:S(2)}, u32[]{:S(2)}) %collective-permute-start.3) | collective-permute-done | bytes 262176 | tf_op jit(solution)/shard_map/ppermute | solution.py:376
  42.6 3.2 %collective-permute-start.4 = (f32[32,1024]{1,0:T(8,128)S(1)}, f32[32,1024]{1,0:T(8,128)S(1)}, u32[]{:S(2)}, u32[]{:S(2)}) collective-permute-start(f32[32,1024]{1,0:T(8,128)S(1)} %get-tuple-element.41), channel_id=1, source_target_pairs={{0,4},{1,5},{2,6},{3,7},{12,8},{13,9},{14,10},{15,11},{16,20},{17,... | collective-permute-start | bytes 393224 | tf_op jit(solution)/shard_map/ppermute | solution.py:391
  45.8 0.7 collective-permute-start.12
  46.5 2.2 %collective-permute-done.4 = f32[32,1024]{1,0:T(8,128)S(1)} collective-permute-done((f32[32,1024]{1,0:T(8,128)S(1)}, f32[32,1024]{1,0:T(8,128)S(1)}, u32[]{:S(2)}, u32[]{:S(2)}) %collective-permute-start.4) | collective-permute-done | bytes 131104 | tf_op jit(solution)/shard_map/ppermute | solution.py:391
  48.7 0.7 collective-permute-start.5
  49.5 1.3 %collective-permute-start.13 = (f32[32,1536]{1,0:T(8,128)S(1)}, f32[32,1536]{1,0:T(8,128)S(1)}, u32[]{:S(2)}, u32[]{:S(2)}) collective-permute-start(f32[32,1536]{1,0:T(8,128)S(1)} %get-tuple-element.32), channel_id=1, source_target_pairs={{8,12},{9,13},{10,14},{11,15},{4,0},{5,1},{6,2},{7,3},{24,28},{25,... | collective-permute-start | bytes 589832 | tf_op jit(solution)/shard_map/ppermute | solution.py:391
  50.8 0.7 add_select_fusion.11
  51.5 1.3 %collective-permute-start.6 = (f32[32,1024]{1,0:T(8,128)}, f32[32,1024]{1,0:T(8,128)}, u32[]{:S(2)}, u32[]{:S(2)}) collective-permute-start(f32[32,1024]{1,0:T(8,128)} %get-tuple-element.38), channel_id=1, source_target_pairs={{8,12},{9,13},{10,14},{11,15},{4,0},{5,1},{6,2},{7,3},{24,28},{25,... | collective-permute-start | bytes 393224 | tf_op jit(solution)/shard_map/ppermute | solution.py:391
  52.8 5.5 %collective-permute-done.13 = f32[32,1536]{1,0:T(8,128)S(1)} collective-permute-done((f32[32,1536]{1,0:T(8,128)S(1)}, f32[32,1536]{1,0:T(8,128)S(1)}, u32[]{:S(2)}, u32[]{:S(2)}) %collective-permute-start.13) | collective-permute-done | bytes 196640 | tf_op jit(solution)/shard_map/ppermute | solution.py:391
  58.3 0.1 select_bitcast_fusion.3
  58.4 0.8 pad_maximum_fusion.5
  59.1 1.2 %collective-permute-start.14 = (f32[2,32,1536]{2,1,0:T(8,128)}, f32[2,32,1536]{2,1,0:T(8,128)}, u32[]{:S(2)}, u32[]{:S(2)}) collective-permute-start(f32[2,32,1536]{2,1,0:T(8,128)} %pad_maximum_fusion.5), channel_id=1, source_target_pairs={{0,2},{1,3},{2,0},{3,1},{4,6},{5,7},{6,4},{7,5},{8,10},{9,11},{10,... | collective-permute-start | bytes 1179656 | tf_op jit(solution)/shard_map/ppermute | solution.py:406
  60.4 0.7 broadcast_in_dim.4
  61.1 0.8 reshape_reshape.3.skip_ref
  61.9 0.4 collective-permute-done.6
  62.3 1.0 select_bitcast_fusion.7
  63.3 1.3 %collective-permute-start.7 = (f32[2,32,1024]{2,1,0:T(8,128)S(1)}, f32[2,32,1024]{2,1,0:T(8,128)S(1)}, u32[]{:S(2)}, u32[]{:S(2)}) collective-permute-start(f32[2,32,1024]{2,1,0:T(8,128)S(1)} %pad_maximum_fusion.9), channel_id=1, source_target_pairs={{0,2},{1,3},{2,0},{3,1},{4,6},{5,7},{6,4},{7,5},{8,10},{9,11},{10,... | collective-permute-start | bytes 786440 | tf_op jit(solution)/shard_map/ppermute | solution.py:406
  64.7 1.7 %collective-permute-done.14 = f32[2,32,1536]{2,1,0:T(8,128)} collective-permute-done((f32[2,32,1536]{2,1,0:T(8,128)}, f32[2,32,1536]{2,1,0:T(8,128)}, u32[]{:S(2)}, u32[]{:S(2)}) %collective-permute-start.14) | collective-permute-done | bytes 393248 | tf_op jit(solution)/shard_map/ppermute | solution.py:406
  66.4 1.0 slice_bitcast_fusion.1
  67.5 1.0 add_select_fusion.3
  68.6 7.5 %collective-permute-start.15 = (f32[2,2,32,1536]{3,2,1,0:T(8,128)S(1)}, f32[2,2,32,1536]{3,2,1,0:T(8,128)S(1)}, u32[]{:S(2)}, u32[]{:S(2)}) collective-permute-start(f32[2,2,32,1536]{3,2,1,0:T(8,128)S(1)} %pad_maximum_fusion.1), channel_id=1, source_target_pairs={{0,1},{1,0},{2,3},{3,2},{4,5},{5,4},{6,7},{7,6},{8,9},{9,8},{10,11... | collective-permute-start | bytes 2359304 | tf_op jit(solution)/shard_map/ppermute | solution.py:421
  76.1 1.2 %add_select_fusion.7 = (f32[1,2,32,1024]{3,2,1,0:T(8,128)S(1)}, f32[1,2,32,1024]{3,2,1,0:T(8,128)S(1)}, f32[1,2,32,1024]{3,2,1,0:T(8,128)S(1)}, f32[1,2,32,1024]{3,2,1,0:T(8,128)S(1)}) fusion(f32[2,2,32,1024]{3,2,1,0:T(8,128)} %collective-permute-done.2, f32[1,1,32,1024]{3,2,1,0:T(8,128)S(1)} %get-tuple-element.70, ...), kind=kLoop, calls=%fused_computation.31 | loop fusion | flops 786432 | bytes 2629633 | tf_op jit(solution)/shard_map/jit(_where)/select_n | solution.py:411
  77.3 0.5 collective-permute-start.8
  78.0 19.7 %shard_map.103 = (f32[512,2560]{1,0:T(8,128)}, f32[512,2560]{1,0:T(8,128)}, f32[40,512]{1,0:T(8,128)S(1)}, f32[512,128]{1,0:T(8,128)S(1)}, f32[512,128]{1,0:T(8,128)S(1)}) custom-call(s32[1]{0:T(128)} %bitcast.slot_ref, f32[40,512]{1,0:T(8,128)S(1)} %copy-done.7, f32[512,128]{1,0:T(8,128)S(1)} %copy-done.3, f32[512,128]{1,0:T(8,128)S(1)} %copy-done.5, ...), custom_call_target="tpu_custom_call" | custom-call | flops 4831838208 | bytes 12582912 | tf_op jit(solution)/shard_map/pallas_call | solution.py:291
  97.6 14.7 %shard_map.104 = (f32[512,2560]{1,0:T(8,128)}, f32[512,2560]{1,0:T(8,128)}, f32[40,512]{1,0:T(8,128)}, f32[512,128]{1,0:T(8,128)}, f32[512,128]{1,0:T(8,128)}) custom-call(s32[1]{0:T(128)} %bitcast.slot_ref, f32[40,512]{1,0:T(8,128)S(1)} %copy-done.7, f32[512,128]{1,0:T(8,128)S(1)} %copy-done.3, ...), custom_call_target="tpu_custom_call", output_to_operand_aliasing={{0}: (9, {}), {1}: (10, {})} | custom-call | flops 3221225472 | bytes 8388608 | tf_op jit(solution)/shard_map/pallas_call | solution.py:291
  (55 shorter events, 0.7 us)
Async XLA Ops:
  1.6 18.0 %collective-permute-start = (f32[40]{0:T(128)S(1)}, f32[40]{0:T(128)S(1)}, u32[]{:S(2)}, u32[]{:S(2)}) collective-permute-start(f32[40]{0:T(128)S(1)} %reduce_sum.9), channel_id=1, source_target_pairs={{0,1},{1,0},{2,3},{3,2},{4,5},{5,4},{6,7},{7,6},{8,9},{9,8},{10,11... | collective-permute-start | bytes 488 | tf_op jit(solution)/shard_map/ppermute | solution.py:349
  1.8 2.5 %copy-start = (f32[512,2560]{1,0:T(8,128)S(1)}, f32[512,2560]{1,0:T(8,128)}, u32[]{:S(2)}) copy-start(f32[512,2560]{1,0:T(8,128)} %x_ref.7) | copy-start | bytes 15728644
  4.2 2.5 %copy-start.1 = (f32[512,2560]{1,0:T(8,128)S(1)}, f32[512,2560]{1,0:T(8,128)}, u32[]{:S(2)}) copy-start(f32[512,2560]{1,0:T(8,128)} %g_ref.7) | copy-start | bytes 15728644
  6.7 0.9 copy-start.2
  7.7 0.9 copy-start.4
  8.6 0.9 copy-start.6
  13.5 15.3 %collective-permute-start.2 = (f32[2,2,32,1024]{3,2,1,0:T(8,128)S(1)}, f32[2,2,32,1024]{3,2,1,0:T(8,128)}, u32[]{:S(2)}, u32[]{:S(2)}) collective-permute-start(f32[2,2,32,1024]{3,2,1,0:T(8,128)S(1)} %get-tuple-element.15), channel_id=1, source_target_pairs={{0,1},{1,0},{2,3},{3,2},{4,5},{5,4},{6,7},{7,6},{8,9},{9,8},{10,11... | collective-permute-start | bytes 1572872 | tf_op jit(solution)/shard_map/ppermute | solution.py:373
  19.6 7.5 %collective-permute-start.9 = (f32[2,2,32,1536]{3,2,1,0:T(8,128)S(1)}, f32[2,2,32,1536]{3,2,1,0:T(8,128)S(1)}, u32[]{:S(2)}, u32[]{:S(2)}) collective-permute-start(f32[2,2,32,1536]{3,2,1,0:T(8,128)S(1)} %get-tuple-element.17), channel_id=1, source_target_pairs={{0,1},{1,0},{2,3},{3,2},{4,5},{5,4},{6,7},{7,6},{8,9},{9,8},{10,11... | collective-permute-start | bytes 2359304 | tf_op jit(solution)/shard_map/ppermute | solution.py:373
  19.7 3.6 %collective-permute-start.1 = (f32[40]{0:T(128)S(1)}, f32[40]{0:T(128)S(1)}, u32[]{:S(2)}, u32[]{:S(2)}) collective-permute-start(f32[40]{0:T(128)S(1)} %get-tuple-element.92), channel_id=1, source_target_pairs={{0,2},{1,3},{2,0},{3,1},{4,6},{5,7},{6,4},{7,5},{8,10},{9,11},{10,... | collective-permute-start | bytes 488 | tf_op jit(solution)/shard_map/ppermute | solution.py:351
  25.3 1.7 %copy-start.8 = (f32[1536]{0:T(1024)}, f32[1536]{0:T(1024)S(1)}, u32[]{:S(2)}) copy-start(f32[1536]{0:T(1024)S(1)} %get-tuple-element.28) | copy-start | bytes 18436
  25.3 1.7 %copy-start.9 = (f32[1536]{0:T(1024)}, f32[1536]{0:T(1024)S(1)}, u32[]{:S(2)}) copy-start(f32[1536]{0:T(1024)S(1)} %get-tuple-element.29) | copy-start | bytes 18436
  27.0 22.5 %copy-start.10 = (f32[1,1024]{1,0:T(1,128)}, f32[1,1024]{1,0:T(1,128)S(1)}, u32[]{:S(2)}) copy-start(f32[1,1024]{1,0:T(1,128)S(1)} %get-tuple-element.78) | copy-start | bytes 12292
  27.3 9.7 %collective-permute-start.10 = (f32[2,32,1536]{2,1,0:T(8,128)S(1)}, f32[2,32,1536]{2,1,0:T(8,128)S(1)}, u32[]{:S(2)}, u32[]{:S(2)}) collective-permute-start(f32[2,32,1536]{2,1,0:T(8,128)S(1)} %pad_maximum_fusion.4), channel_id=1, source_target_pairs={{0,2},{1,3},{2,0},{3,1},{4,6},{5,7},{6,4},{7,5},{8,10},{9,11},{10,... | collective-permute-start | bytes 1179656 | tf_op jit(solution)/shard_map/ppermute | solution.py:376
  29.9 30.5 %copy-start.12 = (f32[40]{0:T(128)S(1)}, f32[40]{0:T(128)}, u32[]{:S(2)}) copy-start(f32[40]{0:T(128)} %param.10) | copy-start | bytes 484
  30.0 12.5 %collective-permute-start.3 = (f32[2,32,1024]{2,1,0:T(8,128)S(1)}, f32[2,32,1024]{2,1,0:T(8,128)S(1)}, u32[]{:S(2)}, u32[]{:S(2)}) collective-permute-start(f32[2,32,1024]{2,1,0:T(8,128)S(1)} %pad_maximum_fusion.8), channel_id=1, source_target_pairs={{0,2},{1,3},{2,0},{3,1},{4,6},{5,7},{6,4},{7,5},{8,10},{9,11},{10,... | collective-permute-start | bytes 786440 | tf_op jit(solution)/shard_map/ppermute | solution.py:376
  37.0 8.8 %collective-permute-start.11 = (f32[32,1536]{1,0:T(8,128)S(1)}, f32[32,1536]{1,0:T(8,128)S(1)}, u32[]{:S(2)}, u32[]{:S(2)}) collective-permute-start(f32[32,1536]{1,0:T(8,128)S(1)} %get-tuple-element.35), channel_id=1, source_target_pairs={{0,4},{1,5},{2,6},{3,7},{12,8},{13,9},{14,10},{15,11},{16,20},{17,... | collective-permute-start | bytes 589832 | tf_op jit(solution)/shard_map/ppermute | solution.py:391
  42.6 6.1 %collective-permute-start.4 = (f32[32,1024]{1,0:T(8,128)S(1)}, f32[32,1024]{1,0:T(8,128)S(1)}, u32[]{:S(2)}, u32[]{:S(2)}) collective-permute-start(f32[32,1024]{1,0:T(8,128)S(1)} %get-tuple-element.41), channel_id=1, source_target_pairs={{0,4},{1,5},{2,6},{3,7},{12,8},{13,9},{14,10},{15,11},{16,20},{17,... | collective-permute-start | bytes 393224 | tf_op jit(solution)/shard_map/ppermute | solution.py:391
  45.8 3.6 %collective-permute-start.12 = (f32[32,1536]{1,0:T(8,128)S(1)}, f32[32,1536]{1,0:T(8,128)S(1)}, u32[]{:S(2)}, u32[]{:S(2)}) collective-permute-start(f32[32,1536]{1,0:T(8,128)S(1)} %add_select_fusion.9), channel_id=1, source_target_pairs={{4,8},{5,9},{6,10},{7,11},{8,4},{9,5},{10,6},{11,7},{20,24},{21,25... | collective-permute-start | bytes 589832 | tf_op jit(solution)/shard_map/ppermute | solution.py:391
  48.7 2.1 %collective-permute-start.5 = (f32[32,1024]{1,0:T(8,128)S(1)}, f32[32,1024]{1,0:T(8,128)S(1)}, u32[]{:S(2)}, u32[]{:S(2)}) collective-permute-start(f32[32,1024]{1,0:T(8,128)S(1)} %add_select_fusion.12), channel_id=1, source_target_pairs={{4,8},{5,9},{6,10},{7,11},{8,4},{9,5},{10,6},{11,7},{20,24},{21,25... | collective-permute-start | bytes 393224 | tf_op jit(solution)/shard_map/ppermute | solution.py:391
  49.5 8.8 %collective-permute-start.13 = (f32[32,1536]{1,0:T(8,128)S(1)}, f32[32,1536]{1,0:T(8,128)S(1)}, u32[]{:S(2)}, u32[]{:S(2)}) collective-permute-start(f32[32,1536]{1,0:T(8,128)S(1)} %get-tuple-element.32), channel_id=1, source_target_pairs={{8,12},{9,13},{10,14},{11,15},{4,0},{5,1},{6,2},{7,3},{24,28},{25,... | collective-permute-start | bytes 589832 | tf_op jit(solution)/shard_map/ppermute | solution.py:391
  51.5 10.8 %collective-permute-start.6 = (f32[32,1024]{1,0:T(8,128)}, f32[32,1024]{1,0:T(8,128)}, u32[]{:S(2)}, u32[]{:S(2)}) collective-permute-start(f32[32,1024]{1,0:T(8,128)} %get-tuple-element.38), channel_id=1, source_target_pairs={{8,12},{9,13},{10,14},{11,15},{4,0},{5,1},{6,2},{7,3},{24,28},{25,... | collective-permute-start | bytes 393224 | tf_op jit(solution)/shard_map/ppermute | solution.py:391
  59.1 7.2 %collective-permute-start.14 = (f32[2,32,1536]{2,1,0:T(8,128)}, f32[2,32,1536]{2,1,0:T(8,128)}, u32[]{:S(2)}, u32[]{:S(2)}) collective-permute-start(f32[2,32,1536]{2,1,0:T(8,128)} %pad_maximum_fusion.5), channel_id=1, source_target_pairs={{0,2},{1,3},{2,0},{3,1},{4,6},{5,7},{6,4},{7,5},{8,10},{9,11},{10,... | collective-permute-start | bytes 1179656 | tf_op jit(solution)/shard_map/ppermute | solution.py:406
  61.9 14.2 %copy-start.11 = (f32[1,1024]{1,0:T(1,128)S(1)}, f32[1,1024]{1,0:T(1,128)}, u32[]{:S(2)}) copy-start(f32[1,1024]{1,0:T(1,128)} %copy-done.10) | copy-start | bytes 12292
  63.3 12.7 %collective-permute-start.7 = (f32[2,32,1024]{2,1,0:T(8,128)S(1)}, f32[2,32,1024]{2,1,0:T(8,128)S(1)}, u32[]{:S(2)}, u32[]{:S(2)}) collective-permute-start(f32[2,32,1024]{2,1,0:T(8,128)S(1)} %pad_maximum_fusion.9), channel_id=1, source_target_pairs={{0,2},{1,3},{2,0},{3,1},{4,6},{5,7},{6,4},{7,5},{8,10},{9,11},{10,... | collective-permute-start | bytes 786440 | tf_op jit(solution)/shard_map/ppermute | solution.py:406
  67.4 10.5 %copy-start.3 = (f32[512,128]{1,0:T(8,128)S(1)}, f32[512,128]{1,0:T(8,128)}, u32[]{:S(2)}) copy-start(f32[512,128]{1,0:T(8,128)} %write_ref.7) | copy-start | bytes 786436
  67.4 10.5 %copy-start.5 = (f32[512,128]{1,0:T(8,128)S(1)}, f32[512,128]{1,0:T(8,128)}, u32[]{:S(2)}) copy-start(f32[512,128]{1,0:T(8,128)} %read_ref.7) | copy-start | bytes 786436
  67.5 10.5 %copy-start.7 = (f32[40,512]{1,0:T(8,128)S(1)}, f32[40,512]{1,0:T(8,128)}, u32[]{:S(2)}) copy-start(f32[40,512]{1,0:T(8,128)} %decay_ref.7) | copy-start | bytes 245764
  68.6 9.4 %collective-permute-start.15 = (f32[2,2,32,1536]{3,2,1,0:T(8,128)S(1)}, f32[2,2,32,1536]{3,2,1,0:T(8,128)S(1)}, u32[]{:S(2)}, u32[]{:S(2)}) collective-permute-start(f32[2,2,32,1536]{3,2,1,0:T(8,128)S(1)} %pad_maximum_fusion.1), channel_id=1, source_target_pairs={{0,1},{1,0},{2,3},{3,2},{4,5},{5,4},{6,7},{7,6},{8,9},{9,8},{10,11... | collective-permute-start | bytes 2359304 | tf_op jit(solution)/shard_map/ppermute | solution.py:421
  77.3 20.3 %collective-permute-start.8 = (f32[2,2,32,1024]{3,2,1,0:T(8,128)S(1)}, f32[2,2,32,1024]{3,2,1,0:T(8,128)S(1)}, u32[]{:S(2)}, u32[]{:S(2)}) collective-permute-start(f32[2,2,32,1024]{3,2,1,0:T(8,128)S(1)} %pad_maximum_fusion.3), channel_id=1, source_target_pairs={{0,1},{1,0},{2,3},{3,2},{4,5},{5,4},{6,7},{7,6},{8,9},{9,8},{10,11... | collective-permute-start | bytes 1572872 | tf_op jit(solution)/shard_map/ppermute | solution.py:421

commit v2 on v1

v2 whole, which is shorter than its diff:
```python
import functools
import math

import jax
import jax.numpy as jnp
from jax import lax
from jax.experimental import pallas as pl
from jax.experimental.pallas import tpu as pltpu
from jax.sharding import PartitionSpec as P

CHUNK = 128
LANES = 512
PACK = 128
GROUPS = (3, 2)
VMEM = 24 << 20
ANYWHERE = pl.BlockSpec(memory_space=pl.ANY)
F32 = jnp.float32
BF16 = jnp.bfloat16


def dot(a, b):
    return lax.dot_general(a, b, (((1,), (0,)), ((), ())), preferred_element_type=F32)


def dot_nt(a, b):
    return lax.dot_general(a, b, (((1,), (1,)), ((), ())), preferred_element_type=F32)


def split(x):
    high = x.astype(BF16)
    return high, (x - high.astype(F32)).astype(BF16)


def split3(x):
    high = x.astype(BF16)
    rest = x - high.astype(F32)
    middle = rest.astype(BF16)
    return high, middle, (rest - middle.astype(F32)).astype(BF16)


def three(product, a, b):
    return product(a[0], b[0]) + product(a[0], b[1]) + product(a[1], b[0])


def left3(x):
    high, low = split(x)
    return jnp.concatenate([high, high, low], 1)


def dot3(left, high, low):
    return dot(left, jnp.concatenate([high, low, high], 0))


def dot3_nt(a, high, low):
    return dot_nt(jnp.concatenate([a[0], a[0], a[1]], 1), jnp.concatenate([high, low, high], 1))


def iota(shape, axis):
    return lax.broadcasted_iota(jnp.int32, shape, axis)


def fold3(x, heads):
    high, middle, low = split3(x)
    column = iota(x.shape, 1)
    chosen = jnp.where(
        column < heads,
        high.astype(F32),
        jnp.where(column < 2 * heads, middle.astype(F32), low.astype(F32)),
    )
    return chosen.astype(BF16)


def spread_matrix(rows, lanes, first, heads, width):
    row, lane = iota((rows, lanes), 0), iota((rows, lanes), 1)
    hit = None
    for copy in range(3):
        start = (row - (first + copy * heads)) * width
        one = jnp.logical_and(lane >= start, lane < start + width)
        hit = one if hit is None else jnp.logical_or(hit, one)
    return jnp.where(hit, 1.0, 0.0).astype(BF16)


def pack_decay(packed, decay_ref, heads):
    packed[...] = jnp.zeros_like(packed)
    for copy in range(3):
        packed[copy * heads : (copy + 1) * heads, :] = decay_ref[...]


def state_kernel(
    slot_ref, decay_ref, write_ref, read_ref, x_ref, g_ref, *refs, groups, heads, width
):
    *out_refs, packed, tail, lead, write_t, read_t, stage = refs
    step = pl.program_id(0)
    rows, lanes = x_ref.shape
    state = write_ref.shape[1]
    quarter = state // 4

    @pl.when(step == 0)
    def _():
        pack_decay(packed, decay_ref, heads)
        parts = split3(packed[...])
        t, u = iota((rows, rows), 0), iota((rows, rows), 1)
        before = jnp.where(u <= t, 1.0, 0.0).astype(BF16)
        after = jnp.where(u > t, 1.0, 0.0).astype(BF16)
        lead[...] = fold3(jnp.exp(sum(dot_nt(before, p) for p in parts)), heads)
        tail[...] = fold3(jnp.exp(sum(dot_nt(after, p) for p in parts)), heads)
        write_t[...] = left3(write_ref[...].T)
        read_t[...] = left3(read_ref[...].T)

    first = step * (lanes // width)
    spread = spread_matrix(packed.shape[0], lanes, first, heads, width)
    slot = slot_ref[0]
    for which, (value_ref, weight, factor) in enumerate(
        ((x_ref, tail, write_t), (g_ref, lead, read_t))
    ):
        scaled = split(value_ref[...] * dot(weight[...], spread))
        stage[which] = dot3(factor[...], *scaled)
    begin = 0
    for k, blocks in enumerate(groups):

        @pl.when(jnp.logical_and(step >= begin, step < begin + blocks))
        def _(k=k):
            for which in range(2):
                for relative in range(4):
                    start = pl.multiple_of((slot ^ relative) * quarter, quarter)
                    target = out_refs[2 * k + relative // 2]
                    target[which, relative % 2] = stage[which, pl.ds(start, quarter), :]

        begin += blocks


def prepare_kernel(
    _early, _late, decay_ref, write_ref, read_ref, left_y, left_x, left_c, left_b, up, down, edges,
    packed
):
    heads, rows = decay_ref.shape
    middle = CHUNK // 2 - 1
    pack_decay(packed, decay_ref, heads)
    t, u = iota((CHUNK, CHUNK), 0), iota((CHUNK, CHUNK), 1)
    ahead = jnp.logical_and(u > middle, u <= t)
    behind = jnp.logical_and(u <= middle, u > t)
    signed = jnp.where(ahead, 1.0, jnp.where(behind, -1.0, 0.0)).astype(BF16)
    row, column = iota((16, CHUNK), 0), iota((16, CHUNK), 1)
    half = jnp.where((row == 0) == (column <= middle), 1.0, 0.0).astype(BF16)
    for i in range(rows // CHUNK):
        span = slice(i * CHUNK, (i + 1) * CHUNK)
        parts = split3(packed[:, span])
        gap = sum(dot_nt(signed, p) for p in parts)
        up[span, :] = fold3(jnp.exp(gap), heads)
        down[span, :] = fold3(jnp.exp(-gap), heads)
        edges[i] = fold3(jnp.exp(sum(dot_nt(half, p) for p in parts)), heads)
        write, read = write_ref[span, :], read_ref[span, :]
        write_p, read_p = split(write), split(read)
        scores = jnp.where(u <= t, three(dot_nt, read_p, write_p), 0.0)
        left_y[i] = left3(jnp.concatenate([scores, write.T], 0))
        scores = jnp.where(u >= t, three(dot_nt, write_p, read_p), 0.0)
        left_x[i] = left3(jnp.concatenate([scores, read.T], 0))
        left_c[i] = left3(read)
        left_b[i] = left3(write)


def block_kernel(
    slot_ref, left_y, left_x, left_c, left_b, up, down, edges, write_ref, read_ref, skip_ref,
    x_ref, g_ref, mine_ref, other_ref, *refs, first_head, heads, width, chained, closing
):
    if chained:
        _, _, old_read, old_write, old_sums, *refs = refs
    y_ref, dx_ref, acc_read, acc_write, sums, *refs = refs
    if closing:
        gd_ref, gw_ref, gr_ref, *refs = refs
    state_in, grad_in, ups, downs, right_h, right_l, held, inner = refs
    step, last = pl.program_id(0), pl.num_programs(0) - 1
    rows, lanes = x_ref.shape
    state = state_in.shape[0]
    quarter = state // 4
    count = rows // CHUNK
    span = [slice(i * CHUNK, (i + 1) * CHUNK) for i in range(count)]

    @pl.when(step == 0)
    def _():
        acc_read[...] = old_read[...] if chained else jnp.zeros_like(acc_read)
        acc_write[...] = old_write[...] if chained else jnp.zeros_like(acc_write)
        sums[...] = old_sums[...] if chained else jnp.zeros_like(sums)

    first = first_head + step * (lanes // width)
    spread = spread_matrix(PACK, lanes, first, heads, width)
    edge = [dot(edges[i], spread) for i in range(count)]
    skip = skip_ref[...]
    ups[...] = dot(up[...], spread)
    downs[...] = dot(down[...], spread)
    slot = slot_ref[0]
    for relative in range(4):
        start = pl.multiple_of((slot ^ relative) * quarter, quarter)
        source = mine_ref if relative < 2 else other_ref
        state_in[pl.ds(start, quarter), :] = source[0, relative % 2]
        grad_in[pl.ds(start, quarter), :] = source[1, relative % 2]

    carried = edge[0][0:1] * state_in[...]
    for i in range(count):
        x = x_ref[span[i], :]
        xh, xl = split(x * downs[span[i], :])
        ph, pl_ = split(carried)
        right_h[i, :CHUNK], right_l[i, :CHUNK] = xh, xl
        right_h[i, CHUNK:], right_l[i, CHUNK:] = ph, pl_
        both = dot3(left_y[i], xh, xl)
        made = (both[:CHUNK] + dot3(left_c[i], ph, pl_)) * ups[span[i], :]
        y_ref[span[i], :] = made + skip * x
        inner[span[i], :] = made * g_ref[span[i], :]
        total = carried + both[CHUNK:]
        held[i] = total
        if i + 1 < count:
            carried = edge[i + 1][0:1] * (edge[i][1:2] * total)

    row, lane = iota((lanes, PACK), 0), iota((lanes, PACK), 1)
    begin = (lane - first) * width
    gather = jnp.where(jnp.logical_and(row >= begin, row < begin + width), 1.0, 0.0).astype(BF16)
    bottom = iota((CHUNK, 1), 0) == CHUNK - 1
    carried = edge[count - 1][1:2] * grad_in[...]
    for i in reversed(range(count)):
        g, x = g_ref[span[i], :], x_ref[span[i], :]
        gh, gl = split(g * ups[span[i], :])
        qh, ql = split(carried)
        both = dot3(left_x[i] if i > 0 else left_x[i, :CHUNK], gh, gl)
        made = (both[:CHUNK] + dot3(left_b[i], qh, ql)) * downs[span[i], :]
        dx_ref[span[i], :] = made + skip * g
        flow = jnp.sum(held[i] * carried, axis=0, keepdims=True)
        ch, cl = split(inner[span[i], :] - x * made + jnp.where(bottom, flow, 0.0))
        sums[span[i], :] += dot(ch, gather) + dot(cl, gather)
        acc_read[i] += dot3_nt((right_h[i], right_l[i]), gh, gl)
        acc_write[i] += dot3_nt((right_h[i, :CHUNK], right_l[i, :CHUNK]), qh, ql)
        if i > 0:
            carried = edge[i - 1][1:2] * (edge[i][0:1] * (carried + both[CHUNK:]))

    if closing:

        @pl.when(step == last)
        def _():
            s, t = iota((CHUNK, CHUNK), 0), iota((CHUNK, CHUNK), 1)
            until = jnp.where(s >= t, 1.0, 0.0).astype(BF16)
            for i in range(count):
                scores = jnp.where(s <= t, acc_read[i, :CHUNK], 0.0)
                write, read = split(write_ref[span[i], :]), split(read_ref[span[i], :])
                gr_ref[span[i], :] = acc_read[i, CHUNK:].T + three(dot, split(scores.T), write)
                gw_ref[span[i], :] = acc_write[i] + three(dot, split(scores), read)
                parts = split3(sums[span[i], :].T)
                gd_ref[:, span[i]] = sum(dot(p, until) for p in parts)[:heads]


def whole(shape):
    return pl.BlockSpec(shape, lambda *_: (0,) * len(shape))


def make_states(slot, log_decay, state_write, state_read, inputs, grad_output, groups):
    rows, columns = inputs.shape
    heads, state = log_decay.shape[0], state_write.shape[1]
    quarter = state // 4
    wide = pl.BlockSpec((rows, LANES), lambda j, _: (0, j))
    shapes, specs, begin = [], [], 0
    for count in groups:
        shape = jax.ShapeDtypeStruct((2, 2, quarter, count * LANES), F32)
        spec = pl.BlockSpec(
            (2, 2, quarter, LANES),
            lambda j, _, begin=begin, count=count: (0, 0, 0, jnp.clip(j - begin, 0, count - 1)),
        )
        shapes += [shape, shape]
        specs += [spec, spec]
        begin += count
    blocks = begin
    width = columns // heads
    return pl.pallas_call(
        functools.partial(state_kernel, groups=groups, heads=heads, width=width),
        out_shape=tuple(shapes),
        grid_spec=pltpu.PrefetchScalarGridSpec(
            num_scalar_prefetch=1,
            grid=(blocks,),
            in_specs=[
                whole((heads, rows)), whole((rows, state)), whole((rows, state)), wide, wide
            ],
            out_specs=tuple(specs),
            scratch_shapes=[
                pltpu.VMEM((PACK, rows), F32),
                pltpu.VMEM((rows, PACK), BF16),
                pltpu.VMEM((rows, PACK), BF16),
                pltpu.VMEM((state, 3 * rows), BF16),
                pltpu.VMEM((state, 3 * rows), BF16),
                pltpu.VMEM((2, state, LANES), F32),
            ],
        ),
        compiler_params=pltpu.CompilerParams(vmem_limit_bytes=VMEM),
        cost_estimate=pl.CostEstimate(
            flops=12 * rows * state * blocks * LANES,
            bytes_accessed=8 * rows * blocks * LANES,
            transcendentals=0,
        ),
    )(slot, log_decay, state_write, state_read, inputs, grad_output)


def prepare(log_decay, state_write, state_read, early, late):
    heads, rows = log_decay.shape
    state = state_write.shape[1]
    count = rows // CHUNK
    left = jax.ShapeDtypeStruct((count, CHUNK + state, 3 * CHUNK), BF16)
    side = jax.ShapeDtypeStruct((count, CHUNK, 3 * state), BF16)
    column = jax.ShapeDtypeStruct((rows, PACK), BF16)
    edges = jax.ShapeDtypeStruct((count, 16, PACK), BF16)
    small = [whole((heads, rows)), whole((rows, state)), whole((rows, state))]
    return pl.pallas_call(
        prepare_kernel,
        in_specs=[ANYWHERE, ANYWHERE, *small],
        out_shape=(left, left, side, side, column, column, edges),
        scratch_shapes=[pltpu.VMEM((PACK, rows), F32)],
        cost_estimate=pl.CostEstimate(flops=1 << 30, bytes_accessed=6 << 20, transcendentals=0),
    )(early, late, log_decay, state_write, state_read)


def make_outputs(
    slot, prepared, skip, inputs, grad_output, pieces, heads, first, blocks, earlier, closing
):
    rows, columns = inputs.shape
    state = prepared[7].shape[1]
    quarter, count = state // 4, rows // CHUNK
    width = columns // heads
    wide = pl.BlockSpec((rows, LANES), lambda j, _: (0, first + j))
    part = pl.BlockSpec((2, 2, quarter, LANES), lambda j, _: (0, 0, 0, j))
    line = pl.BlockSpec((1, LANES), lambda j, _: (0, first + j))
    totals = [(count, CHUNK + state, CHUNK), (count, CHUNK, state), (rows, PACK)]
    in_specs = [*(whole(a.shape) for a in prepared), line, wide, wide, part, part]
    operands = [*prepared, skip, inputs, grad_output, *pieces]
    aliases = {}
    if earlier is not None:
        aliases = {len(operands) + 1: 0, len(operands) + 2: 1}
        in_specs += [ANYWHERE] * 2 + [whole(s) for s in totals]
        operands += earlier
    shapes = [(rows, columns)] * 2 + totals
    out_specs = [wide, wide, *(whole(s) for s in totals)]
    if closing:
        sides = [(heads, rows), (rows, state), (rows, state)]
        shapes += sides
        out_specs += [whole(s) for s in sides]
    return pl.pallas_call(
        functools.partial(
            block_kernel,
            first_head=first * LANES // width,
            heads=heads,
            width=width,
            chained=earlier is not None,
            closing=closing,
        ),
        out_shape=tuple(jax.ShapeDtypeStruct(s, F32) for s in shapes),
        grid_spec=pltpu.PrefetchScalarGridSpec(
            num_scalar_prefetch=1,
            grid=(blocks,),
            in_specs=in_specs,
            out_specs=tuple(out_specs),
            scratch_shapes=[
                pltpu.VMEM((state, LANES), F32),
                pltpu.VMEM((state, LANES), F32),
                pltpu.VMEM((rows, LANES), F32),
                pltpu.VMEM((rows, LANES), F32),
                pltpu.VMEM((count, CHUNK + state, LANES), BF16),
                pltpu.VMEM((count, CHUNK + state, LANES), BF16),
                pltpu.VMEM((count, state, LANES), F32),
                pltpu.VMEM((rows, LANES), F32),
            ],
        ),
        input_output_aliases=aliases,
        compiler_params=pltpu.CompilerParams(vmem_limit_bytes=28 << 20),
        cost_estimate=pl.CostEstimate(
            flops=140 * rows * state * blocks * LANES,
            bytes_accessed=16 * rows * blocks * LANES,
            transcendentals=0,
        ),
    )(slot, *operands)


def local(inputs, log_decay, state_write, state_read, skip_gain, grad_output):
    hbm = functools.partial(pltpu.with_memory_space_constraint, memory_space=pltpu.HBM)
    inputs, grad_output = hbm(inputs), hbm(grad_output)
    state_write, state_read = hbm(state_write), hbm(state_read)
    heads = log_decay.shape[0]
    rows, columns = inputs.shape
    width = columns // heads
    devices, position = lax.axis_size("seq"), lax.axis_index("seq")
    planes = devices // 4
    core, chip, plane = position % 2, (position // 2) % 2, position // 4
    slot = (core * 2 + chip).astype(jnp.int32).reshape(1)
    swap_core = [(i, i ^ 1) for i in range(devices)]
    swap_chip = [(i, i ^ 2) for i in range(devices)]

    total = jnp.sum(log_decay, axis=1)
    twin, beside, across = (
        lax.ppermute(total, "seq", [(i, i ^ bits) for i in range(devices)]) for bits in (1, 2, 3)
    )
    here, there = total + twin, beside + across
    is_c0, is_y0 = core == 0, chip == 0
    logs = jnp.stack(
        [
            jnp.where(is_c0, total, twin),
            jnp.where(is_c0, twin, total),
            jnp.where(is_y0, here, there),
            jnp.where(is_y0, there, here),
            here + there,
        ]
    )
    keepers = jnp.repeat(jnp.exp(logs), width, axis=1)
    one = jnp.ones((columns,), F32)
    skip = jnp.repeat(skip_gain, width).reshape(1, columns)

    goings = []
    made = make_states(slot, log_decay, state_write, state_read, inputs, grad_output, GROUPS)

    def travel(first, blocks, keep, send):
        lanes = slice(first * LANES, (first + blocks) * LANES)
        c0, c1, y0, y1, whole_plane = keepers[:, lanes]
        ones = one[lanes]
        near_core = lax.ppermute(send, "seq", swap_core)
        chip_f = jnp.where(is_c0, c1, ones) * keep[0] + jnp.where(is_c0, ones, c1) * near_core[0]
        chip_b = jnp.where(is_c0, ones, c0) * keep[1] + jnp.where(is_c0, c0, ones) * near_core[1]
        going = jnp.stack([chip_f[1], chip_b[1]])
        near_chip = lax.ppermute(going, "seq", swap_chip)
        if not goings:
            goings.append(prepare(log_decay, state_write, state_read, skip, going))
            near_chip, _ = lax.optimization_barrier((near_chip, goings[0][-1]))
        plane_f = jnp.where(is_y0, y1, ones) * chip_f[0] + jnp.where(is_y0, ones, y1) * near_chip[0]
        plane_b = jnp.where(is_y0, ones, y0) * chip_b[0] + jnp.where(is_y0, y0, ones) * near_chip[1]
        ahead = jnp.zeros_like(plane_f)
        back = jnp.zeros_like(plane_b)
        for hop in range(planes - 1):
            mirror = planes - 1 - hop
            going = jnp.where(
                plane == hop, whole_plane * ahead + plane_f, whole_plane * back + plane_b
            )
            pairs = [
                (source * 4 + i, target * 4 + i)
                for source, target in ((hop, hop + 1), (mirror, mirror - 1))
                for i in range(4)
            ]
            came = lax.ppermute(going, "seq", pairs)
            ahead = jnp.where(plane == hop + 1, came, ahead)
            back = jnp.where(plane == mirror - 1, came, back)
        mine = jnp.stack(
            [
                jnp.where(is_y0, ahead, y0 * ahead + near_chip[0]),
                jnp.where(is_y0, y1 * back + near_chip[1], back),
            ]
        )
        theirs = jnp.stack(
            [
                jnp.where(is_y0, y0 * ahead + chip_f[0], ahead),
                jnp.where(is_y0, back, y1 * back + chip_b[0]),
            ]
        )
        came = lax.ppermute(theirs, "seq", swap_chip)
        into_f = jnp.stack([mine[0], came[0]])
        into_b = jnp.stack([mine[1], came[1]])
        mine = jnp.stack(
            [
                jnp.where(is_c0, into_f, c0 * into_f + near_core[0]),
                jnp.where(is_c0, c1 * into_b + near_core[1], into_b),
            ]
        )
        theirs = jnp.stack(
            [
                jnp.where(is_c0, c0 * into_f + keep[0], into_f),
                jnp.where(is_c0, into_b, c1 * into_b + keep[1]),
            ]
        )
        return mine, lax.ppermute(theirs, "seq", swap_core)

    travels = []
    first = 0
    for k, blocks in enumerate(GROUPS):
        pair = made[2 * k : 2 * k + 2]
        travels.append((first, blocks, travel(first, blocks, *pair)))
        first += blocks
    prepared = [*goings[0], state_write, state_read]
    results = None
    for k, (first, blocks, pieces) in enumerate(travels):
        results = make_outputs(
            slot, prepared, skip, inputs, grad_output, pieces, heads, first, blocks, results,
            k + 1 == len(travels)
        )
    outputs, grad_inputs, _, _, _, grad_decay, grad_write, grad_read = results
    return (outputs, grad_inputs, grad_decay, grad_write, grad_read)


def solution(mesh):
    in_specs = (
        P(("group", "seq"), None),
        P(None, ("group", "seq")),
        P(("group", "seq"), None),
        P(("group", "seq"), None),
        P(),
        P(("group", "seq"), None),
    )
    out_specs = (
        P(("group", "seq"), None),
        P(("group", "seq"), None),
        P(None, ("group", "seq")),
        P(("group", "seq"), None),
        P(("group", "seq"), None),
    )
    return jax.shard_map(local, mesh=mesh, in_specs=in_specs, out_specs=out_specs, check_vma=False)
```

time: 114 us -> 103 us (0.904); the launches traced: 112 us -> 103 us
  local copies, waits for them, and re-layouts: 11.2 us -> 2.62 us
  waiting for transfers between devices: 19.9 us -> 16.3 us
  other arithmetic: 10.4 us -> 12.1 us
  starting transfers between devices: 25.8 us -> 27.5 us
    unnamed x26 -> x20, local copies, waits for them, and re-layouts: 7.8 us -> 0.93 us
    pallas_call x2, Pallas kernels: 34.3 us -> 29.6 us  [make_outputs(): pl.pallas_call(functools.partial(block_kernel, first_head=first * LANES /...]
    ppermute x4 -> x5, waiting for transfers between devices: 10.1 us -> 5.71 us  [the longest x2 5.7 us: travel(): near_chip = lax.ppermute(going, 'seq', swap_chip)]
    pallas_call x2, Pallas kernels: 9.51 us -> 13.5 us  [the longest x1 9.99 us: make_states(): pl.pallas_call(functools.partial(state_kernel, groups=groups, heads=heads...]
    ppermute x2, starting transfers between devices: 8.01 us -> 10.1 us  [travel(): return (mine, lax.ppermute(theirs, 'seq', swap_core))]
    another operation x2, other arithmetic: 0.05 us -> 1.51 us  [travel(): going = jnp.stack([chip_f[1], chip_b[1]])]
    select_n x6, other arithmetic: 1 us -> 2.34 us  [travel(): jnp.where(plane == hop, whole_plane * ahead + plane_f, whole_plane * back...]
    ppermute x4 -> x5, starting transfers between devices: 4.42 us -> 4.64 us  [the longest x3 3.16 us: local(): lax.ppermute(total, 'seq', [(i, i ^ bits) for i in range(devices)])]
  transfers between devices with their start and end apart: 16 -> 17, of which waited for: 7 -> 6; matrix products, arithmetic and copies ran while one was open for 11% -> 12% of each run, Pallas kernels for 26% -> 29%
where the time goes in v2:
time: 103 us
  Pallas kernels  43.1 us (42%)
  starting transfers between devices  27.5 us (27%)
  waiting for transfers between devices  16.3 us (16%)
  other arithmetic  12.1 us (12%)
  local copies, waits for them, and re-layouts  2.62 us (3%)
  between operations  1.23 us (1%)
    pallas_call x2, Pallas kernels, make_outputs(): pl.pallas_call(functools.partial(block_kernel, first_head=first * LANES /...  29.6 us
    ppermute x2, starting transfers between devices, travel(): return (mine, lax.ppermute(theirs, 'seq', swap_core))  10.1 us
    pallas_call x1, Pallas kernels, make_states(): pl.pallas_call(functools.partial(state_kernel, groups=groups, heads=heads...  9.99 us
    ppermute x6, starting transfers between devices, travel(): came = lax.ppermute(going, 'seq', pairs)  9.96 us
    ppermute x6, waiting for transfers between devices, travel(): came = lax.ppermute(going, 'seq', pairs)  8.92 us
    ppermute x2, waiting for transfers between devices, travel(): near_chip = lax.ppermute(going, 'seq', swap_chip)  5.7 us
    pallas_call x1, Pallas kernels, prepare(): pl.pallas_call(prepare_kernel, in_specs=[ANYWHERE, ANYWHERE, *small], out...  3.51 us
    ppermute x3, starting transfers between devices, local(): lax.ppermute(total, 'seq', [(i, i ^ bits) for i in range(devices)])  3.16 us
  transfers between devices with their start and end apart: 17, of which 6 were waited for; matrix products, arithmetic and copies ran while one was open for 12% of the time, Pallas kernels for 29%

profile of v2, /device:TPU:1, one launch (start us, length us, event | category | flops | bytes accessed | tf_op | source)
XLA Modules:
  0.0 102.8 jit_solution(6842337158366867295)
XLA Ops:
  0.6 1.0 reduce_sum.9
  1.6 2.7 %collective-permute-start.2 = (f32[40]{0:T(128)S(1)}, f32[40]{0:T(128)S(1)}, u32[]{:S(2)}, u32[]{:S(2)}) collective-permute-start(f32[40]{0:T(128)S(1)} %reduce_sum.9), channel_id=1, source_target_pairs={{0,3},{1,2},{2,1},{3,0},{4,7},{5,6},{6,5},{7,4},{8,11},{9,10},{10,... | collective-permute-start | bytes 488 | tf_op jit(solution)/shard_map/ppermute | solution.py:392
  4.3 0.5 collective-permute-start
  4.8 0.9 copy-done
  5.7 10.0 %shard_map.101 = (f32[2,2,32,1536]{3,2,1,0:T(8,128)S(1)}, f32[2,2,32,1536]{3,2,1,0:T(8,128)S(1)}, f32[2,2,32,1024]{3,2,1,0:T(8,128)S(1)}, f32[2,2,32,1024]{3,2,1,0:T(8,128)S(1)}) custom-call(s32[1]{0:T(128)} %bitcast.slot_ref, f32[40,512]{1,0:T(8,128)S(1)} %copy-done, f32[512,128]{1,0:T(8,128)} %write_ref.7, f32[512,128]{1,0:T(8,128)} %read_ref.7, ...), custom_call_target="tpu_custom_call" | custom-call | flops 2013265920 | bytes 10485760 | tf_op jit(solution)/shard_map/pallas_call | solution.py:270
  15.7 0.1 collective-permute-start.4
  15.8 0.5 collective-permute-start.3
  16.3 0.1 broadcast_in_dim.4
  16.3 0.7 reshape_reshape.3._early.skip_ref
  17.1 0.1 broadcast_in_dim.5
  17.2 0.7 reshape.193
  17.9 1.0 fusion.20
  18.9 1.2 %slice_reduce_fusion.3 = (f32[1536]{0:T(1024)S(1)}, f32[1536]{0:T(1024)S(1)}, f32[1536]{0:T(1024)S(1)}, f32[1536]{0:T(1024)S(1)}, f32[1536]{0:T(1024)S(1)}, /*in...) fusion(f32[5,2560]{1,0:T(8,128)} %reshape.193, pred[]{:T(512)S(6)} %eq.16), kind=kLoop, calls=%fused_computation.108 | loop fusion | flops 6144 | bytes 86017 | tf_op jit(solution)/shard_map/unstack | solution.py:414
  20.2 0.1 fusion.1
  20.3 0.8 pad_maximum_fusion.4._late
  21.1 1.1 %collective-permute-start.11 = (f32[2,32,1536]{2,1,0:T(8,128)}, f32[2,32,1536]{2,1,0:T(8,128)}, u32[]{:S(2)}, u32[]{:S(2)}) collective-permute-start(f32[2,32,1536]{2,1,0:T(8,128)} %pad_maximum_fusion.4._late), channel_id=1, source_target_pairs={{0,2},{1,3},{2,0},{3,1},{4,6},{5,7},{6,4},{7,5},{8,10},{9,11},{10,... | collective-permute-start | bytes 1179656 | tf_op jit(solution)/shard_map/ppermute | solution.py:420
  22.2 1.1 %fusion.3 = (f32[2,32,1024]{2,1,0:T(8,128)S(1)}, f32[2,32,1024]{2,1,0:T(8,128)S(1)}) fusion(f32[2,2,32,1024]{3,2,1,0:T(8,128)} %collective-permute-done.4, f32[2,2,32,1024]{3,2,1,0:T(8,128)S(1)} %get-tuple-element.36, f32[1024]{0:T(1024)S(1)} %get-tuple-element.122, f32[1024]{0:T(1024)S(1)} %get-tuple-element.123, f32[1024]{0:T(1024)S(1)} %get-tuple-element.114, ...), kind=kLoop, calls=%fused_computation.26 | loop fusion | flops 393216 | bytes 1589248 | tf_op jit(solution)/shard_map/add | solution.py:417
  23.4 0.7 pad_maximum_fusion.8
  24.1 0.4 collective-permute-start.5
  24.5 3.5 %shard_map.102 = (bf16[4,256,384]{2,1,0:T(8,128)(2,1)}, bf16[4,256,384]{2,1,0:T(8,128)(2,1)}, bf16[4,128,384]{2,1,0:T(8,128)(2,1)}, bf16[4,128,384]{2,1,0:T(8,12...) custom-call(f32[1,2560]{1,0:T(1,128)} %reshape_reshape.3._early.skip_ref, ...), custom_call_target="tpu_custom_call" | custom-call | flops 1073741824 | bytes 6291456 | tf_op jit(solution)/shard_map/pallas_call | solution.py:307
  28.0 4.1 %collective-permute-done.11 = f32[2,32,1536]{2,1,0:T(8,128)} collective-permute-done((f32[2,32,1536]{2,1,0:T(8,128)}, f32[2,32,1536]{2,1,0:T(8,128)}, u32[]{:S(2)}, u32[]{:S(2)}) %collective-permute-start.11) | collective-permute-done | bytes 393248 | tf_op jit(solution)/shard_map/ppermute | solution.py:420
  32.1 1.1 %add_select_fusion.10 = (f32[32,1536]{1,0:T(8,128)S(1)}, f32[32,1536]{1,0:T(8,128)S(1)}, f32[32,1536]{1,0:T(8,128)S(1)}) fusion(f32[1536]{0:T(1024)S(1)} %broadcast_multiply_fusion, pred[]{:T(512)S(6)} %eq.20, f32[2,32,1536]{2,1,0:T(8,128)} %collective-permute-done.11, f32[1536]{0:T(1024)S(1)} %get-tuple-element.50, ...), kind=kLoop, calls=%fused_computation.50 | loop fusion | flops 442368 | bytes 1406977 | tf_op jit(solution)/shard_map/jit(_where)/select_n | solution.py:430
  33.2 2.9 %collective-permute-start.12 = (f32[32,1536]{1,0:T(8,128)S(1)}, f32[32,1536]{1,0:T(8,128)S(1)}, u32[]{:S(2)}, u32[]{:S(2)}) collective-permute-start(f32[32,1536]{1,0:T(8,128)S(1)} %get-tuple-element.61), channel_id=1, source_target_pairs={{0,4},{1,5},{2,6},{3,7},{12,8},{13,9},{14,10},{15,11},{16,20},{17,... | collective-permute-start | bytes 589832 | tf_op jit(solution)/shard_map/ppermute | solution.py:438
  36.2 1.6 %collective-permute-done.5 = f32[2,32,1024]{2,1,0:T(8,128)} collective-permute-done((f32[2,32,1024]{2,1,0:T(8,128)}, f32[2,32,1024]{2,1,0:T(8,128)}, u32[]{:S(2)}, u32[]{:S(2)}) %collective-permute-start.5) | collective-permute-done | bytes 262176 | tf_op jit(solution)/shard_map/ppermute | solution.py:420
  37.7 1.0 add_select_fusion.13
  38.8 2.9 %collective-permute-start.6 = (f32[32,1024]{1,0:T(8,128)S(1)}, f32[32,1024]{1,0:T(8,128)S(1)}, u32[]{:S(2)}, u32[]{:S(2)}) collective-permute-start(f32[32,1024]{1,0:T(8,128)S(1)} %get-tuple-element.67), channel_id=1, source_target_pairs={{0,4},{1,5},{2,6},{3,7},{12,8},{13,9},{14,10},{15,11},{16,20},{17,... | collective-permute-start | bytes 393224 | tf_op jit(solution)/shard_map/ppermute | solution.py:438
  41.7 0.1 add_select_fusion.9
  41.8 0.7 collective-permute-start.13
  42.5 1.2 %collective-permute-done.6 = f32[32,1024]{1,0:T(8,128)S(1)} collective-permute-done((f32[32,1024]{1,0:T(8,128)S(1)}, f32[32,1024]{1,0:T(8,128)S(1)}, u32[]{:S(2)}, u32[]{:S(2)}) %collective-permute-start.6) | collective-permute-done | bytes 131104 | tf_op jit(solution)/shard_map/ppermute | solution.py:438
  43.7 0.7 collective-permute-start.7
  44.4 0.1 add_select_fusion.8
  44.4 1.3 %collective-permute-start.14 = (f32[32,1536]{1,0:T(8,128)S(1)}, f32[32,1536]{1,0:T(8,128)S(1)}, u32[]{:S(2)}, u32[]{:S(2)}) collective-permute-start(f32[32,1536]{1,0:T(8,128)S(1)} %get-tuple-element.58), channel_id=1, source_target_pairs={{8,12},{9,13},{10,14},{11,15},{4,0},{5,1},{6,2},{7,3},{24,28},{25,... | collective-permute-start | bytes 589832 | tf_op jit(solution)/shard_map/ppermute | solution.py:438
  45.7 0.1 add_select_fusion.11
  45.8 1.5 %collective-permute-start.8 = (f32[32,1024]{1,0:T(8,128)S(1)}, f32[32,1024]{1,0:T(8,128)S(1)}, u32[]{:S(2)}, u32[]{:S(2)}) collective-permute-start(f32[32,1024]{1,0:T(8,128)S(1)} %get-tuple-element.64), channel_id=1, source_target_pairs={{8,12},{9,13},{10,14},{11,15},{4,0},{5,1},{6,2},{7,3},{24,28},{25,... | collective-permute-start | bytes 393224 | tf_op jit(solution)/shard_map/ppermute | solution.py:438
  47.3 5.9 %collective-permute-done.14 = f32[32,1536]{1,0:T(8,128)S(1)} collective-permute-done((f32[32,1536]{1,0:T(8,128)S(1)}, f32[32,1536]{1,0:T(8,128)S(1)}, u32[]{:S(2)}, u32[]{:S(2)}) %collective-permute-start.14) | collective-permute-done | bytes 196640 | tf_op jit(solution)/shard_map/ppermute | solution.py:438
  53.2 1.1 %fusion.9 = (f32[1,1,32,1536]{3,2,1,0:T(8,128)S(1)}, f32[1,1,32,1536]{3,2,1,0:T(8,128)S(1)}, f32[1,32,1536]{2,1,0:T(8,128)S(1)}, f32[1,32,1536]{2,1,0:T(8,128)S(1)}) fusion(f32[2,32,1536]{2,1,0:T(8,128)} %collective-permute-done.11, f32[1536]{0:T(1024)S(1)} %get-tuple-element.49, pred[]{:T(512)S(6)} %eq.16, f32[32,1536]{1,0:T(8,128)S(1)} %collective-permute-done.14, ...), kind=kLoop, calls=%fused_computation.45 | loop fusion | flops 589824 | bytes 2174979 | tf_op jit(solution)/shard_map/stack | solution.py:454
  54.4 1.0 collective-permute-start.15
  55.4 1.8 %collective-permute-done.8 = f32[32,1024]{1,0:T(8,128)S(1)} collective-permute-done((f32[32,1024]{1,0:T(8,128)S(1)}, f32[32,1024]{1,0:T(8,128)S(1)}, u32[]{:S(2)}, u32[]{:S(2)}) %collective-permute-start.8) | collective-permute-done | bytes 131104 | tf_op jit(solution)/shard_map/ppermute | solution.py:438
  57.2 1.0 %select_bitcast_fusion.5 = (f32[1,1,32,1024]{3,2,1,0:T(8,128)S(1)}, f32[1,1,32,1024]{3,2,1,0:T(8,128)S(1)}, f32[1,32,1024]{2,1,0:T(8,128)S(1)}, f32[1,32,1024]{2,1,0:T(8,128)S(1)}) fusion(f32[2,32,1024]{2,1,0:T(8,128)} %collective-permute-done.5, f32[1024]{0:T(1024)S(1)} %bitcast.145, pred[]{:T(512)S(6)} %eq.16, f32[32,1024]{1,0:T(8,128)S(1)} %collective-permute-done.8, ...), kind=kLoop, calls=%fused_computation.62 | loop fusion | flops 393216 | bytes 1449987 | tf_op jit(solution)/shard_map/stack | solution.py:454
  58.3 1.1 %collective-permute-start.9 = (f32[2,32,1024]{2,1,0:T(8,128)S(1)}, f32[2,32,1024]{2,1,0:T(8,128)S(1)}, u32[]{:S(2)}, u32[]{:S(2)}) collective-permute-start(f32[2,32,1024]{2,1,0:T(8,128)S(1)} %pad_maximum_fusion.9), channel_id=1, source_target_pairs={{0,2},{1,3},{2,0},{3,1},{4,6},{5,7},{6,4},{7,5},{8,10},{9,11},{10,... | collective-permute-start | bytes 786440 | tf_op jit(solution)/shard_map/ppermute | solution.py:453
  59.4 1.7 %collective-permute-done.15 = f32[2,32,1536]{2,1,0:T(8,128)S(1)} collective-permute-done((f32[2,32,1536]{2,1,0:T(8,128)S(1)}, f32[2,32,1536]{2,1,0:T(8,128)S(1)}, u32[]{:S(2)}, u32[]{:S(2)}) %collective-permute-start.15) | collective-permute-done | bytes 393248 | tf_op jit(solution)/shard_map/ppermute | solution.py:453
  61.2 0.2 add_select_fusion.3
  61.4 0.1 pad_maximum_fusion.1
  61.5 7.8 %collective-permute-start.16 = (f32[2,2,32,1536]{3,2,1,0:T(8,128)S(1)}, f32[2,2,32,1536]{3,2,1,0:T(8,128)S(1)}, u32[]{:S(2)}, u32[]{:S(2)}) collective-permute-start(f32[2,2,32,1536]{3,2,1,0:T(8,128)S(1)} %pad_maximum_fusion.1), channel_id=1, source_target_pairs={{0,1},{1,0},{2,3},{3,2},{4,5},{5,4},{6,7},{7,6},{8,9},{9,8},{10,11... | collective-permute-start | bytes 2359304 | tf_op jit(solution)/shard_map/ppermute | solution.py:468
  69.3 1.2 %add_select_fusion.7 = (f32[1,2,32,1024]{3,2,1,0:T(8,128)S(1)}, f32[1,2,32,1024]{3,2,1,0:T(8,128)S(1)}, f32[1,2,32,1024]{3,2,1,0:T(8,128)S(1)}, f32[1,2,32,1024]{3,2,1,0:T(8,128)S(1)}) fusion(f32[2,2,32,1024]{3,2,1,0:T(8,128)} %collective-permute-done.4, f32[1,1,32,1024]{3,2,1,0:T(8,128)S(1)} %get-tuple-element.96, ...), kind=kLoop, calls=%fused_computation.31 | loop fusion | flops 786432 | bytes 2629633 | tf_op jit(solution)/shard_map/jit(_where)/select_n | solution.py:458
  70.5 2.4 %collective-permute-start.10 = (f32[2,2,32,1024]{3,2,1,0:T(8,128)S(1)}, f32[2,2,32,1024]{3,2,1,0:T(8,128)S(1)}, u32[]{:S(2)}, u32[]{:S(2)}) collective-permute-start(f32[2,2,32,1024]{3,2,1,0:T(8,128)S(1)} %pad_maximum_fusion.3), channel_id=1, source_target_pairs={{0,1},{1,0},{2,3},{3,2},{4,5},{5,4},{6,7},{7,6},{8,9},{9,8},{10,11... | collective-permute-start | bytes 1572872 | tf_op jit(solution)/shard_map/ppermute | solution.py:468
  73.1 16.4 %shard_map.103 = (f32[512,2560]{1,0:T(8,128)}, f32[512,2560]{1,0:T(8,128)}, f32[4,256,128]{2,1,0:T(8,128)S(1)}, f32[4,128,128]{2,1,0:T(8,128)S(1)}, f32[512,128]{1,0:T(8,128)S(1)}) custom-call(s32[1]{0:T(128)} %bitcast.slot_ref, bf16[4,256,384]{2,1,0:T(8,128)(2,1)S(1)} %copy-done.2, bf16[4,256,384]{2,1,0:T(8,128)(2,1)S(1)} %copy-done.3, ...), custom_call_target="tpu_custom_call" | custom-call | flops 14092861440 | bytes 12582912 | tf_op jit(solution)/shard_map/pallas_call | solution.py:340
  89.5 13.2 %shard_map.104 = (f32[512,2560]{1,0:T(8,128)}, f32[512,2560]{1,0:T(8,128)}, f32[4,256,128]{2,1,0:T(8,128)}, f32[4,128,128]{2,1,0:T(8,128)}, f32[512,128]{1,0:T(8...) custom-call(s32[1]{0:T(128)} %bitcast.slot_ref, ...), custom_call_target="tpu_custom_call", output_to_operand_aliasing={{0}: (15, {}), {1}: (16, {})} | custom-call | flops 9395240960 | bytes 8388608 | tf_op jit(solution)/shard_map/pallas_call | solution.py:340
  (50 shorter events, 0.5 us)
Async XLA Ops:
  1.6 15.4 %collective-permute-start.2 = (f32[40]{0:T(128)S(1)}, f32[40]{0:T(128)S(1)}, u32[]{:S(2)}, u32[]{:S(2)}) collective-permute-start(f32[40]{0:T(128)S(1)} %reduce_sum.9), channel_id=1, source_target_pairs={{0,3},{1,2},{2,1},{3,0},{4,7},{5,6},{6,5},{7,4},{8,11},{9,10},{10,... | collective-permute-start | bytes 488 | tf_op jit(solution)/shard_map/ppermute | solution.py:392
  4.3 12.7 %collective-permute-start.1 = (f32[40]{0:T(128)S(1)}, f32[40]{0:T(128)S(1)}, u32[]{:S(2)}, u32[]{:S(2)}) collective-permute-start(f32[40]{0:T(128)S(1)} %reduce_sum.9), channel_id=1, source_target_pairs={{0,2},{1,3},{2,0},{3,1},{4,6},{5,7},{6,4},{7,5},{8,10},{9,11},{10,... | collective-permute-start | bytes 488 | tf_op jit(solution)/shard_map/ppermute | solution.py:392
  4.3 12.7 %collective-permute-start = (f32[40]{0:T(128)S(1)}, f32[40]{0:T(128)S(1)}, u32[]{:S(2)}, u32[]{:S(2)}) collective-permute-start(f32[40]{0:T(128)S(1)} %reduce_sum.9), channel_id=1, source_target_pairs={{0,1},{1,0},{2,3},{3,2},{4,5},{5,4},{6,7},{7,6},{8,9},{9,8},{10,11... | collective-permute-start | bytes 488 | tf_op jit(solution)/shard_map/ppermute | solution.py:392
  4.8 0.9 copy-start
  5.7 10.6 %copy-start.9 = (f32[40]{0:T(128)S(1)}, f32[40]{0:T(128)}, u32[]{:S(2)}) copy-start(f32[40]{0:T(128)} %param.10) | copy-start | bytes 484
  15.7 6.5 %collective-permute-start.4 = (f32[2,2,32,1024]{3,2,1,0:T(8,128)S(1)}, f32[2,2,32,1024]{3,2,1,0:T(8,128)}, u32[]{:S(2)}, u32[]{:S(2)}) collective-permute-start(f32[2,2,32,1024]{3,2,1,0:T(8,128)S(1)} %get-tuple-element.37), channel_id=1, source_target_pairs={{0,1},{1,0},{2,3},{3,2},{4,5},{5,4},{6,7},{7,6},{8,9},{9,8},{10,11... | collective-permute-start | bytes 1572872 | tf_op jit(solution)/shard_map/ppermute | solution.py:416
  15.8 4.4 %collective-permute-start.3 = (f32[2,2,32,1536]{3,2,1,0:T(8,128)S(1)}, f32[2,2,32,1536]{3,2,1,0:T(8,128)S(1)}, u32[]{:S(2)}, u32[]{:S(2)}) collective-permute-start(f32[2,2,32,1536]{3,2,1,0:T(8,128)S(1)} %get-tuple-element.28), channel_id=1, source_target_pairs={{0,1},{1,0},{2,3},{3,2},{4,5},{5,4},{6,7},{7,6},{8,9},{9,8},{10,11... | collective-permute-start | bytes 2359304 | tf_op jit(solution)/shard_map/ppermute | solution.py:416
  21.1 11.0 %collective-permute-start.11 = (f32[2,32,1536]{2,1,0:T(8,128)}, f32[2,32,1536]{2,1,0:T(8,128)}, u32[]{:S(2)}, u32[]{:S(2)}) collective-permute-start(f32[2,32,1536]{2,1,0:T(8,128)} %pad_maximum_fusion.4._late), channel_id=1, source_target_pairs={{0,2},{1,3},{2,0},{3,1},{4,6},{5,7},{6,4},{7,5},{8,10},{9,11},{10,... | collective-permute-start | bytes 1179656 | tf_op jit(solution)/shard_map/ppermute | solution.py:420
  24.1 13.7 %collective-permute-start.5 = (f32[2,32,1024]{2,1,0:T(8,128)}, f32[2,32,1024]{2,1,0:T(8,128)}, u32[]{:S(2)}, u32[]{:S(2)}) collective-permute-start(f32[2,32,1024]{2,1,0:T(8,128)} %pad_maximum_fusion.8), channel_id=1, source_target_pairs={{0,2},{1,3},{2,0},{3,1},{4,6},{5,7},{6,4},{7,5},{8,10},{9,11},{10,... | collective-permute-start | bytes 786440 | tf_op jit(solution)/shard_map/ppermute | solution.py:420
  33.2 8.5 %collective-permute-start.12 = (f32[32,1536]{1,0:T(8,128)S(1)}, f32[32,1536]{1,0:T(8,128)S(1)}, u32[]{:S(2)}, u32[]{:S(2)}) collective-permute-start(f32[32,1536]{1,0:T(8,128)S(1)} %get-tuple-element.61), channel_id=1, source_target_pairs={{0,4},{1,5},{2,6},{3,7},{12,8},{13,9},{14,10},{15,11},{16,20},{17,... | collective-permute-start | bytes 589832 | tf_op jit(solution)/shard_map/ppermute | solution.py:438
  38.8 4.9 %collective-permute-start.6 = (f32[32,1024]{1,0:T(8,128)S(1)}, f32[32,1024]{1,0:T(8,128)S(1)}, u32[]{:S(2)}, u32[]{:S(2)}) collective-permute-start(f32[32,1024]{1,0:T(8,128)S(1)} %get-tuple-element.67), channel_id=1, source_target_pairs={{0,4},{1,5},{2,6},{3,7},{12,8},{13,9},{14,10},{15,11},{16,20},{17,... | collective-permute-start | bytes 393224 | tf_op jit(solution)/shard_map/ppermute | solution.py:438
  41.8 2.6 %collective-permute-start.13 = (f32[32,1536]{1,0:T(8,128)S(1)}, f32[32,1536]{1,0:T(8,128)S(1)}, u32[]{:S(2)}, u32[]{:S(2)}) collective-permute-start(f32[32,1536]{1,0:T(8,128)S(1)} %add_select_fusion.9), channel_id=1, source_target_pairs={{4,8},{5,9},{6,10},{7,11},{8,4},{9,5},{10,6},{11,7},{20,24},{21,25... | collective-permute-start | bytes 589832 | tf_op jit(solution)/shard_map/ppermute | solution.py:438
  43.7 2.1 %collective-permute-start.7 = (f32[32,1024]{1,0:T(8,128)S(1)}, f32[32,1024]{1,0:T(8,128)S(1)}, u32[]{:S(2)}, u32[]{:S(2)}) collective-permute-start(f32[32,1024]{1,0:T(8,128)S(1)} %add_select_fusion.12), channel_id=1, source_target_pairs={{4,8},{5,9},{6,10},{7,11},{8,4},{9,5},{10,6},{11,7},{20,24},{21,25... | collective-permute-start | bytes 393224 | tf_op jit(solution)/shard_map/ppermute | solution.py:438
  44.4 8.8 %collective-permute-start.14 = (f32[32,1536]{1,0:T(8,128)S(1)}, f32[32,1536]{1,0:T(8,128)S(1)}, u32[]{:S(2)}, u32[]{:S(2)}) collective-permute-start(f32[32,1536]{1,0:T(8,128)S(1)} %get-tuple-element.58), channel_id=1, source_target_pairs={{8,12},{9,13},{10,14},{11,15},{4,0},{5,1},{6,2},{7,3},{24,28},{25,... | collective-permute-start | bytes 589832 | tf_op jit(solution)/shard_map/ppermute | solution.py:438
  45.8 11.4 %collective-permute-start.8 = (f32[32,1024]{1,0:T(8,128)S(1)}, f32[32,1024]{1,0:T(8,128)S(1)}, u32[]{:S(2)}, u32[]{:S(2)}) collective-permute-start(f32[32,1024]{1,0:T(8,128)S(1)} %get-tuple-element.64), channel_id=1, source_target_pairs={{8,12},{9,13},{10,14},{11,15},{4,0},{5,1},{6,2},{7,3},{24,28},{25,... | collective-permute-start | bytes 393224 | tf_op jit(solution)/shard_map/ppermute | solution.py:438
  54.4 6.7 %collective-permute-start.15 = (f32[2,32,1536]{2,1,0:T(8,128)S(1)}, f32[2,32,1536]{2,1,0:T(8,128)S(1)}, u32[]{:S(2)}, u32[]{:S(2)}) collective-permute-start(f32[2,32,1536]{2,1,0:T(8,128)S(1)} %pad_maximum_fusion.5), channel_id=1, source_target_pairs={{0,2},{1,3},{2,0},{3,1},{4,6},{5,7},{6,4},{7,5},{8,10},{9,11},{10,... | collective-permute-start | bytes 1179656 | tf_op jit(solution)/shard_map/ppermute | solution.py:453
  58.3 11.0 %collective-permute-start.9 = (f32[2,32,1024]{2,1,0:T(8,128)S(1)}, f32[2,32,1024]{2,1,0:T(8,128)S(1)}, u32[]{:S(2)}, u32[]{:S(2)}) collective-permute-start(f32[2,32,1024]{2,1,0:T(8,128)S(1)} %pad_maximum_fusion.9), channel_id=1, source_target_pairs={{0,2},{1,3},{2,0},{3,1},{4,6},{5,7},{6,4},{7,5},{8,10},{9,11},{10,... | collective-permute-start | bytes 786440 | tf_op jit(solution)/shard_map/ppermute | solution.py:453
  61.1 11.9 %copy-start.1 = (f32[1,2560]{1,0:T(1,128)S(1)}, f32[1,2560]{1,0:T(1,128)}, u32[]{:S(2)}) copy-start(f32[1,2560]{1,0:T(1,128)} %reshape_reshape.3._early.skip_ref) | copy-start | bytes 30724
  61.1 11.9 %copy-start.2 = (bf16[4,256,384]{2,1,0:T(8,128)(2,1)S(1)}, bf16[4,256,384]{2,1,0:T(8,128)(2,1)}, u32[]{:S(2)}) copy-start(bf16[4,256,384]{2,1,0:T(8,128)(2,1)} %get-tuple-element.29.left_y) | copy-start | bytes 2359300
  61.1 11.9 %copy-start.3 = (bf16[4,256,384]{2,1,0:T(8,128)(2,1)S(1)}, bf16[4,256,384]{2,1,0:T(8,128)(2,1)}, u32[]{:S(2)}) copy-start(bf16[4,256,384]{2,1,0:T(8,128)(2,1)} %get-tuple-element.30.left_x) | copy-start | bytes 2359300
  61.1 11.9 %copy-start.4 = (bf16[4,128,384]{2,1,0:T(8,128)(2,1)S(1)}, bf16[4,128,384]{2,1,0:T(8,128)(2,1)}, u32[]{:S(2)}) copy-start(bf16[4,128,384]{2,1,0:T(8,128)(2,1)} %get-tuple-element.31.left_c) | copy-start | bytes 1179652
  61.1 11.9 %copy-start.5 = (bf16[4,128,384]{2,1,0:T(8,128)(2,1)S(1)}, bf16[4,128,384]{2,1,0:T(8,128)(2,1)}, u32[]{:S(2)}) copy-start(bf16[4,128,384]{2,1,0:T(8,128)(2,1)} %get-tuple-element.32.left_b) | copy-start | bytes 1179652
  61.1 11.9 %copy-start.6 = (bf16[512,128]{1,0:T(8,128)(2,1)S(1)}, bf16[512,128]{1,0:T(8,128)(2,1)}, u32[]{:S(2)}) copy-start(bf16[512,128]{1,0:T(8,128)(2,1)} %get-tuple-element.33.up) | copy-start | bytes 393220
  61.2 11.9 %copy-start.7 = (bf16[512,128]{1,0:T(8,128)(2,1)S(1)}, bf16[512,128]{1,0:T(8,128)(2,1)}, u32[]{:S(2)}) copy-start(bf16[512,128]{1,0:T(8,128)(2,1)} %get-tuple-element.34.down) | copy-start | bytes 393220
  61.2 11.9 %copy-start.8 = (bf16[4,16,128]{2,1,0:T(8,128)(2,1)S(1)}, bf16[4,16,128]{2,1,0:T(8,128)(2,1)}, u32[]{:S(2)}) copy-start(bf16[4,16,128]{2,1,0:T(8,128)(2,1)} %get-tuple-element.35.edges) | copy-start | bytes 49156
  61.5 11.5 %collective-permute-start.16 = (f32[2,2,32,1536]{3,2,1,0:T(8,128)S(1)}, f32[2,2,32,1536]{3,2,1,0:T(8,128)S(1)}, u32[]{:S(2)}, u32[]{:S(2)}) collective-permute-start(f32[2,2,32,1536]{3,2,1,0:T(8,128)S(1)} %pad_maximum_fusion.1), channel_id=1, source_target_pairs={{0,1},{1,0},{2,3},{3,2},{4,5},{5,4},{6,7},{7,6},{8,9},{9,8},{10,11... | collective-permute-start | bytes 2359304 | tf_op jit(solution)/shard_map/ppermute | solution.py:468
  70.5 19.0 %collective-permute-start.10 = (f32[2,2,32,1024]{3,2,1,0:T(8,128)S(1)}, f32[2,2,32,1024]{3,2,1,0:T(8,128)S(1)}, u32[]{:S(2)}, u32[]{:S(2)}) collective-permute-start(f32[2,2,32,1024]{3,2,1,0:T(8,128)S(1)} %pad_maximum_fusion.3), channel_id=1, source_target_pairs={{0,1},{1,0},{2,3},{3,2},{4,5},{5,4},{6,7},{7,6},{8,9},{9,8},{10,11... | collective-permute-start | bytes 1572872 | tf_op jit(solution)/shard_map/ppermute | solution.py:468

commit v3 on v2

--- a/solution.py
+++ b/solution.py
@@ -48,11 +48,20 @@
 
 
 def dot3(left, high, low):
-    return dot(left, jnp.concatenate([high, low, high], 0))
+    depth = left.shape[1] // 3
+    a, b = left[:, :depth], left[:, 2 * depth :]
+    rows = left.shape[0]
+    both = dot(
+        jnp.concatenate([jnp.concatenate([a, a], 1), jnp.concatenate([b, b], 1)], 0),
+        jnp.concatenate([high, low], 0),
+    )
+    return both[:rows] + both[rows:]
 
 
 def dot3_nt(a, high, low):
-    return dot_nt(jnp.concatenate([a[0], a[0], a[1]], 1), jnp.concatenate([high, low, high], 1))
+    rows = a[0].shape[0]
+    both = dot_nt(jnp.concatenate([a[0], a[1]], 0), high)
+    return both[:rows] + both[rows:] + dot_nt(a[0], low)
 
 
 def iota(shape, axis):
@@ -159,6 +168,24 @@
         left_b[i] = left3(write)
 
 
+def fold_pair(a, b, size):
+    lower = iota(a.shape, 1) % (2 * size) < size
+    return jnp.where(
+        lower, a + pltpu.roll(a, PACK - size, 1), b + pltpu.roll(b, size, 1)
+    )
+
+
+def fold_heads(x):
+    tiles = [x[:, k * PACK : (k + 1) * PACK] for k in range(4)]
+    return fold_pair(fold_pair(tiles[0], tiles[1], 32), fold_pair(tiles[2], tiles[3], 32), 16)
+
+
+def gather_matrix(first):
+    lane, column = iota((2 * PACK, PACK), 0) % PACK, iota((2 * PACK, PACK), 1)
+    head = lane % 32 // 16 * 4 + lane % 64 // 32 * 2 + lane // 64
+    return jnp.where(column == first + head, 1.0, 0.0).astype(BF16)
+
+
 def block_kernel(
     slot_ref, left_y, left_x, left_c, left_b, up, down, edges, write_ref, read_ref, skip_ref,
     x_ref, g_ref, mine_ref, other_ref, *refs, first_head, heads, width, chained, closing
@@ -168,7 +195,10 @@
     y_ref, dx_ref, acc_read, acc_write, sums, *refs = refs
     if closing:
         gd_ref, gw_ref, gr_ref, *refs = refs
-    state_in, grad_in, ups, downs, right_h, right_l, held, inner = refs
+    (
+        state_in, grad_in, ups, downs, right_h, right_l, held, inner, folded, turned_h, turned_l,
+        ends, outer
+    ) = refs
     step, last = pl.program_id(0), pl.num_programs(0) - 1
     rows, lanes = x_ref.shape
     state = state_in.shape[0]
@@ -195,41 +225,48 @@
         state_in[pl.ds(start, quarter), :] = source[0, relative % 2]
         grad_in[pl.ds(start, quarter), :] = source[1, relative % 2]
 
-    carried = edge[0][0:1] * state_in[...]
+    ahead = edge[0][0:1] * state_in[...]
+    back = edge[count - 1][1:2] * grad_in[...]
     for i in range(count):
-        x = x_ref[span[i], :]
+        x, g = x_ref[span[i], :], g_ref[span[i], :]
         xh, xl = split(x * downs[span[i], :])
-        ph, pl_ = split(carried)
+        ph, pl_ = split(ahead)
         right_h[i, :CHUNK], right_l[i, :CHUNK] = xh, xl
         right_h[i, CHUNK:], right_l[i, CHUNK:] = ph, pl_
         both = dot3(left_y[i], xh, xl)
         made = (both[:CHUNK] + dot3(left_c[i], ph, pl_)) * ups[span[i], :]
         y_ref[span[i], :] = made + skip * x
-        inner[span[i], :] = made * g_ref[span[i], :]
-        total = carried + both[CHUNK:]
+        inner[span[i], :] = made * g
+        total = ahead + both[CHUNK:]
         held[i] = total
         if i + 1 < count:
-            carried = edge[i + 1][0:1] * (edge[i][1:2] * total)
-
-    row, lane = iota((lanes, PACK), 0), iota((lanes, PACK), 1)
-    begin = (lane - first) * width
-    gather = jnp.where(jnp.logical_and(row >= begin, row < begin + width), 1.0, 0.0).astype(BF16)
+            ahead = edge[i + 1][0:1] * (edge[i][1:2] * total)
+
+        j = count - 1 - i
+        x, g = x_ref[span[j], :], g_ref[span[j], :]
+        gh, gl = split(g * ups[span[j], :])
+        qh, ql = split(back)
+        turned_h[j, :CHUNK], turned_l[j, :CHUNK] = gh, gl
+        turned_h[j, CHUNK:], turned_l[j, CHUNK:] = qh, ql
+        both = dot3(left_x[j] if j > 0 else left_x[j, :CHUNK], gh, gl)
+        made = (both[:CHUNK] + dot3(left_b[j], qh, ql)) * downs[span[j], :]
+        dx_ref[span[j], :] = made + skip * g
+        outer[span[j], :] = x * made
+        ends[j] = back
+        if j > 0:
+            back = edge[j - 1][1:2] * (edge[j][0:1] * (back + both[CHUNK:]))
+
     bottom = iota((CHUNK, 1), 0) == CHUNK - 1
-    carried = edge[count - 1][1:2] * grad_in[...]
-    for i in reversed(range(count)):
-        g, x = g_ref[span[i], :], x_ref[span[i], :]
-        gh, gl = split(g * ups[span[i], :])
-        qh, ql = split(carried)
-        both = dot3(left_x[i] if i > 0 else left_x[i, :CHUNK], gh, gl)
-        made = (both[:CHUNK] + dot3(left_b[i], qh, ql)) * downs[span[i], :]
-        dx_ref[span[i], :] = made + skip * g
-        flow = jnp.sum(held[i] * carried, axis=0, keepdims=True)
-        ch, cl = split(inner[span[i], :] - x * made + jnp.where(bottom, flow, 0.0))
-        sums[span[i], :] += dot(ch, gather) + dot(cl, gather)
-        acc_read[i] += dot3_nt((right_h[i], right_l[i]), gh, gl)
-        acc_write[i] += dot3_nt((right_h[i, :CHUNK], right_l[i, :CHUNK]), qh, ql)
-        if i > 0:
-            carried = edge[i - 1][1:2] * (edge[i][0:1] * (carried + both[CHUNK:]))
+    for i in range(count):
+        flow = jnp.sum(held[i] * ends[i], axis=0, keepdims=True)
+        change = inner[span[i], :] - outer[span[i], :] + jnp.where(bottom, flow, 0.0)
+        folded[span[i], :] = fold_heads(change)
+        pairs = dot3_nt((right_h[i], right_l[i]), turned_h[i], turned_l[i])
+        acc_read[i] += pairs[:, :CHUNK]
+        acc_write[i] += pairs[:CHUNK, CHUNK:]
+
+    ch, cl = split(folded[...])
+    sums[...] += dot(jnp.concatenate([ch, cl], 1), gather_matrix(first))
 
     if closing:
 
@@ -361,10 +398,15 @@
                 pltpu.VMEM((count, CHUNK + state, LANES), BF16),
                 pltpu.VMEM((count, state, LANES), F32),
                 pltpu.VMEM((rows, LANES), F32),
+                pltpu.VMEM((rows, PACK), F32),
+                pltpu.VMEM((count, CHUNK + state, LANES), BF16),
+                pltpu.VMEM((count, CHUNK + state, LANES), BF16),
+                pltpu.VMEM((count, state, LANES), F32),
+                pltpu.VMEM((rows, LANES), F32),
             ],
         ),
         input_output_aliases=aliases,
-        compiler_params=pltpu.CompilerParams(vmem_limit_bytes=28 << 20),
+        compiler_params=pltpu.CompilerParams(vmem_limit_bytes=32 << 20),
         cost_estimate=pl.CostEstimate(
             flops=140 * rows * state * blocks * LANES,
             bytes_accessed=16 * rows * blocks * LANES,

time: 103 us -> 97.1 us (0.943)
  Pallas kernels: 43.1 us -> 36.7 us
    pallas_call x2, Pallas kernels: 29.6 us -> 23.1 us  [make_outputs(): pl.pallas_call(functools.partial(block_kernel, first_head=first * LANES /...]
  transfers between devices with their start and end apart: 17 -> 17, of which waited for: 6 -> 6; matrix products, arithmetic and copies ran while one was open for 12% -> 13% of each run, Pallas kernels for 29% -> 27%
where the time goes in v3:
time: 97.1 us; the launch traced here: 96.4 us
  Pallas kernels  36.7 us (38%)
  starting transfers between devices  27.5 us (28%)
  waiting for transfers between devices  16.2 us (17%)
  other arithmetic  12.1 us (12%)
  local copies, waits for them, and re-layouts  2.62 us (3%)
  between operations  1.23 us (1%)
    pallas_call x2, Pallas kernels, make_outputs(): pl.pallas_call(functools.partial(block_kernel, first_head=first * LANES /...  23.1 us
    ppermute x2, starting transfers between devices, travel(): return (mine, lax.ppermute(theirs, 'seq', swap_core))  10.1 us
    pallas_call x1, Pallas kernels, make_states(): pl.pallas_call(functools.partial(state_kernel, groups=groups, heads=heads...  10.1 us
    ppermute x6, starting transfers between devices, travel(): came = lax.ppermute(going, 'seq', pairs)  10 us
    ppermute x6, waiting for transfers between devices, travel(): came = lax.ppermute(going, 'seq', pairs)  8.9 us
    ppermute x2, waiting for transfers between devices, travel(): near_chip = lax.ppermute(going, 'seq', swap_chip)  5.66 us
    pallas_call x1, Pallas kernels, prepare(): pl.pallas_call(prepare_kernel, in_specs=[ANYWHERE, ANYWHERE, *small], out...  3.52 us
    ppermute x3, starting transfers between devices, local(): lax.ppermute(total, 'seq', [(i, i ^ bits) for i in range(devices)])  3.16 us
  transfers between devices with their start and end apart: 17, of which 6 were waited for; matrix products, arithmetic and copies ran while one was open for 13% of the time, Pallas kernels for 27%

profile of v3, /device:TPU:1, one launch (start us, length us, event | category | flops | bytes accessed | tf_op | source)
XLA Modules:
  0.0 96.4 jit_solution(3772584569944765754)
XLA Ops:
  0.6 1.0 %reduce_sum.9 = f32[40]{0:T(128)S(1)} reduce(f32[40,512]{1,0:T(8,128)} %decay_ref.3, f32[]{:T(128)} %constant.49.clone.1), dimensions={1}, to_apply=%region_0.1 | reduce | flops 20440 | bytes 82084 | tf_op jit(solution)/shard_map/reduce_sum | solution.py:432
  1.6 2.7 %collective-permute-start.2 = (f32[40]{0:T(128)S(1)}, f32[40]{0:T(128)S(1)}, u32[]{:S(2)}, u32[]{:S(2)}) collective-permute-start(f32[40]{0:T(128)S(1)} %reduce_sum.9), channel_id=1, source_target_pairs={{0,3},{1,2},{2,1},{3,0},{4,7},{5,6},{6,5},{7,4},{8,11},{9,10},{10,... | collective-permute-start | bytes 488 | tf_op jit(solution)/shard_map/ppermute | solution.py:434
  4.3 0.5 collective-permute-start
  4.8 0.9 copy-done
  5.7 10.1 %shard_map.101 = (f32[2,2,32,1536]{3,2,1,0:T(8,128)S(1)}, f32[2,2,32,1536]{3,2,1,0:T(8,128)S(1)}, f32[2,2,32,1024]{3,2,1,0:T(8,128)S(1)}, f32[2,2,32,1024]{3,2,1,0:T(8,128)S(1)}) custom-call(s32[1]{0:T(128)} %bitcast.slot_ref, f32[40,512]{1,0:T(8,128)S(1)} %copy-done, f32[512,128]{1,0:T(8,128)} %write_ref.7, f32[512,128]{1,0:T(8,128)} %read_ref.7, ...), custom_call_target="tpu_custom_call" | custom-call | flops 2013265920 | bytes 10485760 | tf_op jit(solution)/shard_map/pallas_call | solution.py:307
  15.8 0.1 collective-permute-start.4
  15.9 0.5 collective-permute-start.3
  16.4 0.1 broadcast_in_dim.4
  16.4 0.7 reshape_reshape.3._early.skip_ref
  17.2 0.1 broadcast_in_dim.5
  17.3 0.7 reshape.193
  18.0 1.0 %fusion.20 = (f32[1,1024]{1,0:T(1,128)S(1)}, f32[1,1024]{1,0:T(1,128)S(1)}, f32[1,1024]{1,0:T(1,128)S(1)}, f32[1,1024]{1,0:T(1,128)S(1)}, f32[1,1024]{1,0:T(1,12...) fusion(f32[5,2560]{1,0:T(8,128)} %reshape.193, pred[]{:T(512)S(6)} %eq.16), kind=kLoop, calls=%fused_computation.110 | loop fusion | flops 4096 | bytes 57345 | tf_op jit(solution)/shard_map/unstack | solution.py:456
  19.1 1.2 %slice_reduce_fusion.3 = (f32[1536]{0:T(1024)S(1)}, f32[1536]{0:T(1024)S(1)}, f32[1536]{0:T(1024)S(1)}, f32[1536]{0:T(1024)S(1)}, f32[1536]{0:T(1024)S(1)}, /*in...) fusion(f32[5,2560]{1,0:T(8,128)} %reshape.193, pred[]{:T(512)S(6)} %eq.16), kind=kLoop, calls=%fused_computation.108 | loop fusion | flops 6144 | bytes 86017 | tf_op jit(solution)/shard_map/unstack | solution.py:456
  20.3 0.1 fusion.1
  20.4 0.8 pad_maximum_fusion.4._late
  21.2 1.1 %collective-permute-start.11 = (f32[2,32,1536]{2,1,0:T(8,128)}, f32[2,32,1536]{2,1,0:T(8,128)}, u32[]{:S(2)}, u32[]{:S(2)}) collective-permute-start(f32[2,32,1536]{2,1,0:T(8,128)} %pad_maximum_fusion.4._late), channel_id=1, source_target_pairs={{0,2},{1,3},{2,0},{3,1},{4,6},{5,7},{6,4},{7,5},{8,10},{9,11},{10,... | collective-permute-start | bytes 1179656 | tf_op jit(solution)/shard_map/ppermute | solution.py:462
  22.3 1.1 %fusion.3 = (f32[2,32,1024]{2,1,0:T(8,128)S(1)}, f32[2,32,1024]{2,1,0:T(8,128)S(1)}) fusion(f32[2,2,32,1024]{3,2,1,0:T(8,128)} %collective-permute-done.4, f32[2,2,32,1024]{3,2,1,0:T(8,128)S(1)} %get-tuple-element.36, f32[1024]{0:T(1024)S(1)} %get-tuple-element.122, f32[1024]{0:T(1024)S(1)} %get-tuple-element.123, f32[1024]{0:T(1024)S(1)} %get-tuple-element.114, ...), kind=kLoop, calls=%fused_computation.26 | loop fusion | flops 393216 | bytes 1589248 | tf_op jit(solution)/shard_map/add | solution.py:459
  23.5 0.7 pad_maximum_fusion.8
  24.2 0.4 collective-permute-start.5
  24.6 3.5 %shard_map.102 = (bf16[4,256,384]{2,1,0:T(8,128)(2,1)}, bf16[4,256,384]{2,1,0:T(8,128)(2,1)}, bf16[4,128,384]{2,1,0:T(8,128)(2,1)}, bf16[4,128,384]{2,1,0:T(8,12...) custom-call(f32[1,2560]{1,0:T(1,128)} %reshape_reshape.3._early.skip_ref, ...), custom_call_target="tpu_custom_call" | custom-call | flops 1073741824 | bytes 6291456 | tf_op jit(solution)/shard_map/pallas_call | solution.py:344
  28.1 4.1 %collective-permute-done.11 = f32[2,32,1536]{2,1,0:T(8,128)} collective-permute-done((f32[2,32,1536]{2,1,0:T(8,128)}, f32[2,32,1536]{2,1,0:T(8,128)}, u32[]{:S(2)}, u32[]{:S(2)}) %collective-permute-start.11) | collective-permute-done | bytes 393248 | tf_op jit(solution)/shard_map/ppermute | solution.py:462
  32.2 1.1 %add_select_fusion.10 = (f32[32,1536]{1,0:T(8,128)S(1)}, f32[32,1536]{1,0:T(8,128)S(1)}, f32[32,1536]{1,0:T(8,128)S(1)}) fusion(f32[1536]{0:T(1024)S(1)} %broadcast_multiply_fusion, pred[]{:T(512)S(6)} %eq.20, f32[2,32,1536]{2,1,0:T(8,128)} %collective-permute-done.11, f32[1536]{0:T(1024)S(1)} %get-tuple-element.50, ...), kind=kLoop, calls=%fused_computation.50 | loop fusion | flops 442368 | bytes 1406977 | tf_op jit(solution)/shard_map/jit(_where)/select_n | solution.py:472
  33.4 3.0 %collective-permute-start.12 = (f32[32,1536]{1,0:T(8,128)S(1)}, f32[32,1536]{1,0:T(8,128)S(1)}, u32[]{:S(2)}, u32[]{:S(2)}) collective-permute-start(f32[32,1536]{1,0:T(8,128)S(1)} %get-tuple-element.61), channel_id=1, source_target_pairs={{0,4},{1,5},{2,6},{3,7},{12,8},{13,9},{14,10},{15,11},{16,20},{17,... | collective-permute-start | bytes 589832 | tf_op jit(solution)/shard_map/ppermute | solution.py:480
  36.3 1.5 %collective-permute-done.5 = f32[2,32,1024]{2,1,0:T(8,128)} collective-permute-done((f32[2,32,1024]{2,1,0:T(8,128)}, f32[2,32,1024]{2,1,0:T(8,128)}, u32[]{:S(2)}, u32[]{:S(2)}) %collective-permute-start.5) | collective-permute-done | bytes 262176 | tf_op jit(solution)/shard_map/ppermute | solution.py:462
  37.9 1.0 %add_select_fusion.13 = (f32[32,1024]{1,0:T(8,128)S(1)}, f32[32,1024]{1,0:T(8,128)S(1)}, f32[32,1024]{1,0:T(8,128)S(1)}) fusion(f32[1024]{0:T(1024)S(1)} %broadcast_multiply_fusion.1, pred[]{:T(512)S(6)} %eq.20, f32[2,32,1024]{2,1,0:T(8,128)} %collective-permute-done.5, f32[1024]{0:T(1024)S(1)} %bitcast.149, f32[2,32,1024]{2,1,0:T(8,128)S(1)} %get-tuple-element.72, ...), kind=kLoop, calls=%fused_computation.65 | loop fusion | flops 294912 | bytes 937985 | tf_op jit(solution)/shard_map/jit(_where)/select_n | solution.py:472
  38.9 3.0 %collective-permute-start.6 = (f32[32,1024]{1,0:T(8,128)S(1)}, f32[32,1024]{1,0:T(8,128)S(1)}, u32[]{:S(2)}, u32[]{:S(2)}) collective-permute-start(f32[32,1024]{1,0:T(8,128)S(1)} %get-tuple-element.67), channel_id=1, source_target_pairs={{0,4},{1,5},{2,6},{3,7},{12,8},{13,9},{14,10},{15,11},{16,20},{17,... | collective-permute-start | bytes 393224 | tf_op jit(solution)/shard_map/ppermute | solution.py:480
  41.9 0.1 add_select_fusion.9
  41.9 0.7 collective-permute-start.13
  42.6 1.2 %collective-permute-done.6 = f32[32,1024]{1,0:T(8,128)S(1)} collective-permute-done((f32[32,1024]{1,0:T(8,128)S(1)}, f32[32,1024]{1,0:T(8,128)S(1)}, u32[]{:S(2)}, u32[]{:S(2)}) %collective-permute-start.6) | collective-permute-done | bytes 131104 | tf_op jit(solution)/shard_map/ppermute | solution.py:480
  43.8 0.7 collective-permute-start.7
  44.5 0.1 add_select_fusion.8
  44.6 1.3 %collective-permute-start.14 = (f32[32,1536]{1,0:T(8,128)S(1)}, f32[32,1536]{1,0:T(8,128)S(1)}, u32[]{:S(2)}, u32[]{:S(2)}) collective-permute-start(f32[32,1536]{1,0:T(8,128)S(1)} %get-tuple-element.58), channel_id=1, source_target_pairs={{8,12},{9,13},{10,14},{11,15},{4,0},{5,1},{6,2},{7,3},{24,28},{25,... | collective-permute-start | bytes 589832 | tf_op jit(solution)/shard_map/ppermute | solution.py:480
  45.9 0.1 add_select_fusion.11
  46.0 1.5 %collective-permute-start.8 = (f32[32,1024]{1,0:T(8,128)S(1)}, f32[32,1024]{1,0:T(8,128)S(1)}, u32[]{:S(2)}, u32[]{:S(2)}) collective-permute-start(f32[32,1024]{1,0:T(8,128)S(1)} %get-tuple-element.64), channel_id=1, source_target_pairs={{8,12},{9,13},{10,14},{11,15},{4,0},{5,1},{6,2},{7,3},{24,28},{25,... | collective-permute-start | bytes 393224 | tf_op jit(solution)/shard_map/ppermute | solution.py:480
  47.4 5.9 %collective-permute-done.14 = f32[32,1536]{1,0:T(8,128)S(1)} collective-permute-done((f32[32,1536]{1,0:T(8,128)S(1)}, f32[32,1536]{1,0:T(8,128)S(1)}, u32[]{:S(2)}, u32[]{:S(2)}) %collective-permute-start.14) | collective-permute-done | bytes 196640 | tf_op jit(solution)/shard_map/ppermute | solution.py:480
  53.3 1.1 %fusion.9 = (f32[1,1,32,1536]{3,2,1,0:T(8,128)S(1)}, f32[1,1,32,1536]{3,2,1,0:T(8,128)S(1)}, f32[1,32,1536]{2,1,0:T(8,128)S(1)}, f32[1,32,1536]{2,1,0:T(8,128)S(1)}) fusion(f32[2,32,1536]{2,1,0:T(8,128)} %collective-permute-done.11, f32[1536]{0:T(1024)S(1)} %get-tuple-element.49, pred[]{:T(512)S(6)} %eq.16, f32[32,1536]{1,0:T(8,128)S(1)} %collective-permute-done.14, ...), kind=kLoop, calls=%fused_computation.45 | loop fusion | flops 589824 | bytes 2174979 | tf_op jit(solution)/shard_map/stack | solution.py:496
  54.5 1.0 %collective-permute-start.15 = (f32[2,32,1536]{2,1,0:T(8,128)S(1)}, f32[2,32,1536]{2,1,0:T(8,128)S(1)}, u32[]{:S(2)}, u32[]{:S(2)}) collective-permute-start(f32[2,32,1536]{2,1,0:T(8,128)S(1)} %pad_maximum_fusion.5), channel_id=1, source_target_pairs={{0,2},{1,3},{2,0},{3,1},{4,6},{5,7},{6,4},{7,5},{8,10},{9,11},{10,... | collective-permute-start | bytes 1179656 | tf_op jit(solution)/shard_map/ppermute | solution.py:495
  55.5 1.8 %collective-permute-done.8 = f32[32,1024]{1,0:T(8,128)S(1)} collective-permute-done((f32[32,1024]{1,0:T(8,128)S(1)}, f32[32,1024]{1,0:T(8,128)S(1)}, u32[]{:S(2)}, u32[]{:S(2)}) %collective-permute-start.8) | collective-permute-done | bytes 131104 | tf_op jit(solution)/shard_map/ppermute | solution.py:480
  57.4 1.0 %select_bitcast_fusion.5 = (f32[1,1,32,1024]{3,2,1,0:T(8,128)S(1)}, f32[1,1,32,1024]{3,2,1,0:T(8,128)S(1)}, f32[1,32,1024]{2,1,0:T(8,128)S(1)}, f32[1,32,1024]{2,1,0:T(8,128)S(1)}) fusion(f32[2,32,1024]{2,1,0:T(8,128)} %collective-permute-done.5, f32[1024]{0:T(1024)S(1)} %bitcast.145, pred[]{:T(512)S(6)} %eq.16, f32[32,1024]{1,0:T(8,128)S(1)} %collective-permute-done.8, ...), kind=kLoop, calls=%fused_computation.62 | loop fusion | flops 393216 | bytes 1449987 | tf_op jit(solution)/shard_map/stack | solution.py:496
  58.4 1.1 %collective-permute-start.9 = (f32[2,32,1024]{2,1,0:T(8,128)S(1)}, f32[2,32,1024]{2,1,0:T(8,128)S(1)}, u32[]{:S(2)}, u32[]{:S(2)}) collective-permute-start(f32[2,32,1024]{2,1,0:T(8,128)S(1)} %pad_maximum_fusion.9), channel_id=1, source_target_pairs={{0,2},{1,3},{2,0},{3,1},{4,6},{5,7},{6,4},{7,5},{8,10},{9,11},{10,... | collective-permute-start | bytes 786440 | tf_op jit(solution)/shard_map/ppermute | solution.py:495
  59.5 1.6 %collective-permute-done.15 = f32[2,32,1536]{2,1,0:T(8,128)S(1)} collective-permute-done((f32[2,32,1536]{2,1,0:T(8,128)S(1)}, f32[2,32,1536]{2,1,0:T(8,128)S(1)}, u32[]{:S(2)}, u32[]{:S(2)}) %collective-permute-start.15) | collective-permute-done | bytes 393248 | tf_op jit(solution)/shard_map/ppermute | solution.py:495
  61.3 0.2 add_select_fusion.3
  61.5 0.1 pad_maximum_fusion.1
  61.6 7.8 %collective-permute-start.16 = (f32[2,2,32,1536]{3,2,1,0:T(8,128)S(1)}, f32[2,2,32,1536]{3,2,1,0:T(8,128)S(1)}, u32[]{:S(2)}, u32[]{:S(2)}) collective-permute-start(f32[2,2,32,1536]{3,2,1,0:T(8,128)S(1)} %pad_maximum_fusion.1), channel_id=1, source_target_pairs={{0,1},{1,0},{2,3},{3,2},{4,5},{5,4},{6,7},{7,6},{8,9},{9,8},{10,11... | collective-permute-start | bytes 2359304 | tf_op jit(solution)/shard_map/ppermute | solution.py:510
  69.4 1.2 %add_select_fusion.7 = (f32[1,2,32,1024]{3,2,1,0:T(8,128)S(1)}, f32[1,2,32,1024]{3,2,1,0:T(8,128)S(1)}, f32[1,2,32,1024]{3,2,1,0:T(8,128)S(1)}, f32[1,2,32,1024]{3,2,1,0:T(8,128)S(1)}) fusion(f32[2,2,32,1024]{3,2,1,0:T(8,128)} %collective-permute-done.4, f32[1,1,32,1024]{3,2,1,0:T(8,128)S(1)} %get-tuple-element.96, ...), kind=kLoop, calls=%fused_computation.31 | loop fusion | flops 786432 | bytes 2629633 | tf_op jit(solution)/shard_map/jit(_where)/select_n | solution.py:500
  70.6 2.4 %collective-permute-start.10 = (f32[2,2,32,1024]{3,2,1,0:T(8,128)S(1)}, f32[2,2,32,1024]{3,2,1,0:T(8,128)S(1)}, u32[]{:S(2)}, u32[]{:S(2)}) collective-permute-start(f32[2,2,32,1024]{3,2,1,0:T(8,128)S(1)} %pad_maximum_fusion.3), channel_id=1, source_target_pairs={{0,1},{1,0},{2,3},{3,2},{4,5},{5,4},{6,7},{7,6},{8,9},{9,8},{10,11... | collective-permute-start | bytes 1572872 | tf_op jit(solution)/shard_map/ppermute | solution.py:510
  73.2 12.4 %shard_map.103 = (f32[512,2560]{1,0:T(8,128)}, f32[512,2560]{1,0:T(8,128)}, f32[4,256,128]{2,1,0:T(8,128)S(1)}, f32[4,128,128]{2,1,0:T(8,128)S(1)}, f32[512,128]{1,0:T(8,128)S(1)}) custom-call(s32[1]{0:T(128)} %bitcast.slot_ref, bf16[4,256,384]{2,1,0:T(8,128)(2,1)S(1)} %copy-done.2, bf16[4,256,384]{2,1,0:T(8,128)(2,1)S(1)} %copy-done.3, ...), custom_call_target="tpu_custom_call" | custom-call | flops 14092861440 | bytes 12582912 | tf_op jit(solution)/shard_map/pallas_call | solution.py:377
  85.5 10.7 %shard_map.104 = (f32[512,2560]{1,0:T(8,128)}, f32[512,2560]{1,0:T(8,128)}, f32[4,256,128]{2,1,0:T(8,128)}, f32[4,128,128]{2,1,0:T(8,128)}, f32[512,128]{1,0:T(8...) custom-call(s32[1]{0:T(128)} %bitcast.slot_ref, ...), custom_call_target="tpu_custom_call", output_to_operand_aliasing={{0}: (15, {}), {1}: (16, {})} | custom-call | flops 9395240960 | bytes 8388608 | tf_op jit(solution)/shard_map/pallas_call | solution.py:377
  (50 shorter events, 0.5 us)
Async XLA Ops:
  1.6 15.5 %collective-permute-start.2 = (f32[40]{0:T(128)S(1)}, f32[40]{0:T(128)S(1)}, u32[]{:S(2)}, u32[]{:S(2)}) collective-permute-start(f32[40]{0:T(128)S(1)} %reduce_sum.9), channel_id=1, source_target_pairs={{0,3},{1,2},{2,1},{3,0},{4,7},{5,6},{6,5},{7,4},{8,11},{9,10},{10,... | collective-permute-start | bytes 488 | tf_op jit(solution)/shard_map/ppermute | solution.py:434
  4.3 12.8 %collective-permute-start.1 = (f32[40]{0:T(128)S(1)}, f32[40]{0:T(128)S(1)}, u32[]{:S(2)}, u32[]{:S(2)}) collective-permute-start(f32[40]{0:T(128)S(1)} %reduce_sum.9), channel_id=1, source_target_pairs={{0,2},{1,3},{2,0},{3,1},{4,6},{5,7},{6,4},{7,5},{8,10},{9,11},{10,... | collective-permute-start | bytes 488 | tf_op jit(solution)/shard_map/ppermute | solution.py:434
  4.3 12.8 %collective-permute-start = (f32[40]{0:T(128)S(1)}, f32[40]{0:T(128)S(1)}, u32[]{:S(2)}, u32[]{:S(2)}) collective-permute-start(f32[40]{0:T(128)S(1)} %reduce_sum.9), channel_id=1, source_target_pairs={{0,1},{1,0},{2,3},{3,2},{4,5},{5,4},{6,7},{7,6},{8,9},{9,8},{10,11... | collective-permute-start | bytes 488 | tf_op jit(solution)/shard_map/ppermute | solution.py:434
  4.8 0.9 copy-start
  5.7 10.7 %copy-start.9 = (f32[40]{0:T(128)S(1)}, f32[40]{0:T(128)}, u32[]{:S(2)}) copy-start(f32[40]{0:T(128)} %param.10) | copy-start | bytes 484
  15.8 6.6 %collective-permute-start.4 = (f32[2,2,32,1024]{3,2,1,0:T(8,128)S(1)}, f32[2,2,32,1024]{3,2,1,0:T(8,128)}, u32[]{:S(2)}, u32[]{:S(2)}) collective-permute-start(f32[2,2,32,1024]{3,2,1,0:T(8,128)S(1)} %get-tuple-element.37), channel_id=1, source_target_pairs={{0,1},{1,0},{2,3},{3,2},{4,5},{5,4},{6,7},{7,6},{8,9},{9,8},{10,11... | collective-permute-start | bytes 1572872 | tf_op jit(solution)/shard_map/ppermute | solution.py:458
  15.9 4.4 %collective-permute-start.3 = (f32[2,2,32,1536]{3,2,1,0:T(8,128)S(1)}, f32[2,2,32,1536]{3,2,1,0:T(8,128)S(1)}, u32[]{:S(2)}, u32[]{:S(2)}) collective-permute-start(f32[2,2,32,1536]{3,2,1,0:T(8,128)S(1)} %get-tuple-element.28), channel_id=1, source_target_pairs={{0,1},{1,0},{2,3},{3,2},{4,5},{5,4},{6,7},{7,6},{8,9},{9,8},{10,11... | collective-permute-start | bytes 2359304 | tf_op jit(solution)/shard_map/ppermute | solution.py:458
  21.2 11.0 %collective-permute-start.11 = (f32[2,32,1536]{2,1,0:T(8,128)}, f32[2,32,1536]{2,1,0:T(8,128)}, u32[]{:S(2)}, u32[]{:S(2)}) collective-permute-start(f32[2,32,1536]{2,1,0:T(8,128)} %pad_maximum_fusion.4._late), channel_id=1, source_target_pairs={{0,2},{1,3},{2,0},{3,1},{4,6},{5,7},{6,4},{7,5},{8,10},{9,11},{10,... | collective-permute-start | bytes 1179656 | tf_op jit(solution)/shard_map/ppermute | solution.py:462
  24.2 13.6 %collective-permute-start.5 = (f32[2,32,1024]{2,1,0:T(8,128)}, f32[2,32,1024]{2,1,0:T(8,128)}, u32[]{:S(2)}, u32[]{:S(2)}) collective-permute-start(f32[2,32,1024]{2,1,0:T(8,128)} %pad_maximum_fusion.8), channel_id=1, source_target_pairs={{0,2},{1,3},{2,0},{3,1},{4,6},{5,7},{6,4},{7,5},{8,10},{9,11},{10,... | collective-permute-start | bytes 786440 | tf_op jit(solution)/shard_map/ppermute | solution.py:462
  33.4 8.5 %collective-permute-start.12 = (f32[32,1536]{1,0:T(8,128)S(1)}, f32[32,1536]{1,0:T(8,128)S(1)}, u32[]{:S(2)}, u32[]{:S(2)}) collective-permute-start(f32[32,1536]{1,0:T(8,128)S(1)} %get-tuple-element.61), channel_id=1, source_target_pairs={{0,4},{1,5},{2,6},{3,7},{12,8},{13,9},{14,10},{15,11},{16,20},{17,... | collective-permute-start | bytes 589832 | tf_op jit(solution)/shard_map/ppermute | solution.py:480
  38.9 4.9 %collective-permute-start.6 = (f32[32,1024]{1,0:T(8,128)S(1)}, f32[32,1024]{1,0:T(8,128)S(1)}, u32[]{:S(2)}, u32[]{:S(2)}) collective-permute-start(f32[32,1024]{1,0:T(8,128)S(1)} %get-tuple-element.67), channel_id=1, source_target_pairs={{0,4},{1,5},{2,6},{3,7},{12,8},{13,9},{14,10},{15,11},{16,20},{17,... | collective-permute-start | bytes 393224 | tf_op jit(solution)/shard_map/ppermute | solution.py:480
  41.9 2.6 %collective-permute-start.13 = (f32[32,1536]{1,0:T(8,128)S(1)}, f32[32,1536]{1,0:T(8,128)S(1)}, u32[]{:S(2)}, u32[]{:S(2)}) collective-permute-start(f32[32,1536]{1,0:T(8,128)S(1)} %add_select_fusion.9), channel_id=1, source_target_pairs={{4,8},{5,9},{6,10},{7,11},{8,4},{9,5},{10,6},{11,7},{20,24},{21,25... | collective-permute-start | bytes 589832 | tf_op jit(solution)/shard_map/ppermute | solution.py:480
  43.8 2.1 %collective-permute-start.7 = (f32[32,1024]{1,0:T(8,128)S(1)}, f32[32,1024]{1,0:T(8,128)S(1)}, u32[]{:S(2)}, u32[]{:S(2)}) collective-permute-start(f32[32,1024]{1,0:T(8,128)S(1)} %add_select_fusion.12), channel_id=1, source_target_pairs={{4,8},{5,9},{6,10},{7,11},{8,4},{9,5},{10,6},{11,7},{20,24},{21,25... | collective-permute-start | bytes 393224 | tf_op jit(solution)/shard_map/ppermute | solution.py:480
  44.6 8.7 %collective-permute-start.14 = (f32[32,1536]{1,0:T(8,128)S(1)}, f32[32,1536]{1,0:T(8,128)S(1)}, u32[]{:S(2)}, u32[]{:S(2)}) collective-permute-start(f32[32,1536]{1,0:T(8,128)S(1)} %get-tuple-element.58), channel_id=1, source_target_pairs={{8,12},{9,13},{10,14},{11,15},{4,0},{5,1},{6,2},{7,3},{24,28},{25,... | collective-permute-start | bytes 589832 | tf_op jit(solution)/shard_map/ppermute | solution.py:480
  46.0 11.4 %collective-permute-start.8 = (f32[32,1024]{1,0:T(8,128)S(1)}, f32[32,1024]{1,0:T(8,128)S(1)}, u32[]{:S(2)}, u32[]{:S(2)}) collective-permute-start(f32[32,1024]{1,0:T(8,128)S(1)} %get-tuple-element.64), channel_id=1, source_target_pairs={{8,12},{9,13},{10,14},{11,15},{4,0},{5,1},{6,2},{7,3},{24,28},{25,... | collective-permute-start | bytes 393224 | tf_op jit(solution)/shard_map/ppermute | solution.py:480
  54.5 6.7 %collective-permute-start.15 = (f32[2,32,1536]{2,1,0:T(8,128)S(1)}, f32[2,32,1536]{2,1,0:T(8,128)S(1)}, u32[]{:S(2)}, u32[]{:S(2)}) collective-permute-start(f32[2,32,1536]{2,1,0:T(8,128)S(1)} %pad_maximum_fusion.5), channel_id=1, source_target_pairs={{0,2},{1,3},{2,0},{3,1},{4,6},{5,7},{6,4},{7,5},{8,10},{9,11},{10,... | collective-permute-start | bytes 1179656 | tf_op jit(solution)/shard_map/ppermute | solution.py:495
  58.4 10.9 %collective-permute-start.9 = (f32[2,32,1024]{2,1,0:T(8,128)S(1)}, f32[2,32,1024]{2,1,0:T(8,128)S(1)}, u32[]{:S(2)}, u32[]{:S(2)}) collective-permute-start(f32[2,32,1024]{2,1,0:T(8,128)S(1)} %pad_maximum_fusion.9), channel_id=1, source_target_pairs={{0,2},{1,3},{2,0},{3,1},{4,6},{5,7},{6,4},{7,5},{8,10},{9,11},{10,... | collective-permute-start | bytes 786440 | tf_op jit(solution)/shard_map/ppermute | solution.py:495
  61.2 11.9 %copy-start.1 = (f32[1,2560]{1,0:T(1,128)S(1)}, f32[1,2560]{1,0:T(1,128)}, u32[]{:S(2)}) copy-start(f32[1,2560]{1,0:T(1,128)} %reshape_reshape.3._early.skip_ref) | copy-start | bytes 30724
  61.2 11.9 %copy-start.2 = (bf16[4,256,384]{2,1,0:T(8,128)(2,1)S(1)}, bf16[4,256,384]{2,1,0:T(8,128)(2,1)}, u32[]{:S(2)}) copy-start(bf16[4,256,384]{2,1,0:T(8,128)(2,1)} %get-tuple-element.29.left_y) | copy-start | bytes 2359300
  61.2 11.9 %copy-start.3 = (bf16[4,256,384]{2,1,0:T(8,128)(2,1)S(1)}, bf16[4,256,384]{2,1,0:T(8,128)(2,1)}, u32[]{:S(2)}) copy-start(bf16[4,256,384]{2,1,0:T(8,128)(2,1)} %get-tuple-element.30.left_x) | copy-start | bytes 2359300
  61.2 11.9 %copy-start.4 = (bf16[4,128,384]{2,1,0:T(8,128)(2,1)S(1)}, bf16[4,128,384]{2,1,0:T(8,128)(2,1)}, u32[]{:S(2)}) copy-start(bf16[4,128,384]{2,1,0:T(8,128)(2,1)} %get-tuple-element.31.left_c) | copy-start | bytes 1179652
  61.2 11.9 %copy-start.5 = (bf16[4,128,384]{2,1,0:T(8,128)(2,1)S(1)}, bf16[4,128,384]{2,1,0:T(8,128)(2,1)}, u32[]{:S(2)}) copy-start(bf16[4,128,384]{2,1,0:T(8,128)(2,1)} %get-tuple-element.32.left_b) | copy-start | bytes 1179652
  61.3 11.9 %copy-start.6 = (bf16[512,128]{1,0:T(8,128)(2,1)S(1)}, bf16[512,128]{1,0:T(8,128)(2,1)}, u32[]{:S(2)}) copy-start(bf16[512,128]{1,0:T(8,128)(2,1)} %get-tuple-element.33.up) | copy-start | bytes 393220
  61.3 11.9 %copy-start.7 = (bf16[512,128]{1,0:T(8,128)(2,1)S(1)}, bf16[512,128]{1,0:T(8,128)(2,1)}, u32[]{:S(2)}) copy-start(bf16[512,128]{1,0:T(8,128)(2,1)} %get-tuple-element.34.down) | copy-start | bytes 393220
  61.3 11.9 %copy-start.8 = (bf16[4,16,128]{2,1,0:T(8,128)(2,1)S(1)}, bf16[4,16,128]{2,1,0:T(8,128)(2,1)}, u32[]{:S(2)}) copy-start(bf16[4,16,128]{2,1,0:T(8,128)(2,1)} %get-tuple-element.35.edges) | copy-start | bytes 49156
  61.6 11.5 %collective-permute-start.16 = (f32[2,2,32,1536]{3,2,1,0:T(8,128)S(1)}, f32[2,2,32,1536]{3,2,1,0:T(8,128)S(1)}, u32[]{:S(2)}, u32[]{:S(2)}) collective-permute-start(f32[2,2,32,1536]{3,2,1,0:T(8,128)S(1)} %pad_maximum_fusion.1), channel_id=1, source_target_pairs={{0,1},{1,0},{2,3},{3,2},{4,5},{5,4},{6,7},{7,6},{8,9},{9,8},{10,11... | collective-permute-start | bytes 2359304 | tf_op jit(solution)/shard_map/ppermute | solution.py:510
  70.6 14.9 %collective-permute-start.10 = (f32[2,2,32,1024]{3,2,1,0:T(8,128)S(1)}, f32[2,2,32,1024]{3,2,1,0:T(8,128)S(1)}, u32[]{:S(2)}, u32[]{:S(2)}) collective-permute-start(f32[2,2,32,1024]{3,2,1,0:T(8,128)S(1)} %pad_maximum_fusion.3), channel_id=1, source_target_pairs={{0,1},{1,0},{2,3},{3,2},{4,5},{5,4},{6,7},{7,6},{8,9},{9,8},{10,11... | collective-permute-start | bytes 1572872 | tf_op jit(solution)/shard_map/ppermute | solution.py:510

commit v4 on v3

--- a/solution.py
+++ b/solution.py
@@ -98,7 +98,7 @@
 def state_kernel(
     slot_ref, decay_ref, write_ref, read_ref, x_ref, g_ref, *refs, groups, heads, width
 ):
-    *out_refs, packed, tail, lead, write_t, read_t, stage = refs
+    *out_refs, decay_out, packed, tail, lead, write_t, read_t, stage = refs
     step = pl.program_id(0)
     rows, lanes = x_ref.shape
     state = write_ref.shape[1]
@@ -122,8 +122,10 @@
     for which, (value_ref, weight, factor) in enumerate(
         ((x_ref, tail, write_t), (g_ref, lead, read_t))
     ):
-        scaled = split(value_ref[...] * dot(weight[...], spread))
-        stage[which] = dot3(factor[...], *scaled)
+        scale = dot(weight[...], spread)
+        stage[which] = dot3(factor[...], *split(value_ref[...] * scale))
+        if which == 1:
+            decay_out[...] = jnp.broadcast_to(scale[rows - 1 :], decay_out.shape)
     begin = 0
     for k, blocks in enumerate(groups):
 
@@ -139,11 +141,18 @@
 
 
 def prepare_kernel(
-    _early, _late, decay_ref, write_ref, read_ref, left_y, left_x, left_c, left_b, up, down, edges,
-    packed
+    gain_ref, _late, decay_ref, write_ref, read_ref, left_y, left_x, left_c, left_b, up, down, edges,
+    skip_ref, packed
 ):
     heads, rows = decay_ref.shape
     middle = CHUNK // 2 - 1
+    columns = skip_ref.shape[1]
+    gains = jnp.broadcast_to(gain_ref[...], (16, heads))
+    head, lane = iota((heads, columns), 0), iota((heads, columns), 1)
+    start = head * (columns // heads)
+    hit = jnp.logical_and(lane >= start, lane < start + columns // heads)
+    spread = jnp.where(hit, 1.0, 0.0).astype(BF16)
+    skip_ref[...] = sum(dot(p, spread) for p in split3(gains))[:1]
     pack_decay(packed, decay_ref, heads)
     t, u = iota((CHUNK, CHUNK), 0), iota((CHUNK, CHUNK), 1)
     ahead = jnp.logical_and(u > middle, u <= t)
@@ -306,14 +315,14 @@
     width = columns // heads
     return pl.pallas_call(
         functools.partial(state_kernel, groups=groups, heads=heads, width=width),
-        out_shape=tuple(shapes),
+        out_shape=(*shapes, jax.ShapeDtypeStruct((8, columns), F32)),
         grid_spec=pltpu.PrefetchScalarGridSpec(
             num_scalar_prefetch=1,
             grid=(blocks,),
             in_specs=[
                 whole((heads, rows)), whole((rows, state)), whole((rows, state)), wide, wide
             ],
-            out_specs=tuple(specs),
+            out_specs=(*specs, pl.BlockSpec((8, LANES), lambda j, _: (0, j))),
             scratch_shapes=[
                 pltpu.VMEM((PACK, rows), F32),
                 pltpu.VMEM((rows, PACK), BF16),
@@ -332,7 +341,7 @@
     )(slot, log_decay, state_write, state_read, inputs, grad_output)
 
 
-def prepare(log_decay, state_write, state_read, early, late):
+def prepare(log_decay, state_write, state_read, gains, late, columns):
     heads, rows = log_decay.shape
     state = state_write.shape[1]
     count = rows // CHUNK
@@ -343,11 +352,13 @@
     small = [whole((heads, rows)), whole((rows, state)), whole((rows, state))]
     return pl.pallas_call(
         prepare_kernel,
-        in_specs=[ANYWHERE, ANYWHERE, *small],
-        out_shape=(left, left, side, side, column, column, edges),
+        in_specs=[whole((1, heads)), ANYWHERE, *small],
+        out_shape=(
+            left, left, side, side, column, column, edges, jax.ShapeDtypeStruct((1, columns), F32)
+        ),
         scratch_shapes=[pltpu.VMEM((PACK, rows), F32)],
         cost_estimate=pl.CostEstimate(flops=1 << 30, bytes_accessed=6 << 20, transcendentals=0),
-    )(early, late, log_decay, state_write, state_read)
+    )(gains, late, log_decay, state_write, state_read)
 
 
 def make_outputs(
@@ -418,7 +429,7 @@
 def local(inputs, log_decay, state_write, state_read, skip_gain, grad_output):
     hbm = functools.partial(pltpu.with_memory_space_constraint, memory_space=pltpu.HBM)
     inputs, grad_output = hbm(inputs), hbm(grad_output)
-    state_write, state_read = hbm(state_write), hbm(state_read)
+    state_write, state_read, log_decay = hbm(state_write), hbm(state_read), hbm(log_decay)
     heads = log_decay.shape[0]
     rows, columns = inputs.shape
     width = columns // heads
@@ -429,31 +440,23 @@
     swap_core = [(i, i ^ 1) for i in range(devices)]
     swap_chip = [(i, i ^ 2) for i in range(devices)]
 
-    total = jnp.sum(log_decay, axis=1)
-    twin, beside, across = (
-        lax.ppermute(total, "seq", [(i, i ^ bits) for i in range(devices)]) for bits in (1, 2, 3)
-    )
-    here, there = total + twin, beside + across
     is_c0, is_y0 = core == 0, chip == 0
-    logs = jnp.stack(
-        [
-            jnp.where(is_c0, total, twin),
-            jnp.where(is_c0, twin, total),
-            jnp.where(is_y0, here, there),
-            jnp.where(is_y0, there, here),
-            here + there,
-        ]
-    )
-    keepers = jnp.repeat(jnp.exp(logs), width, axis=1)
-    one = jnp.ones((columns,), F32)
-    skip = jnp.repeat(skip_gain, width).reshape(1, columns)
-
     goings = []
     made = make_states(slot, log_decay, state_write, state_read, inputs, grad_output, GROUPS)
+    own = made[-1][0]
+    twin, beside, across = (
+        lax.ppermute(own, "seq", [(i, i ^ bits) for i in range(devices)]) for bits in (1, 2, 3)
+    )
+    here, there = own * twin, beside * across
+    one = jnp.ones((columns,), F32)
 
     def travel(first, blocks, keep, send):
         lanes = slice(first * LANES, (first + blocks) * LANES)
-        c0, c1, y0, y1, whole_plane = keepers[:, lanes]
+        c0 = jnp.where(is_c0, own, twin)[lanes]
+        c1 = jnp.where(is_c0, twin, own)[lanes]
+        y0 = jnp.where(is_y0, here, there)[lanes]
+        y1 = jnp.where(is_y0, there, here)[lanes]
+        whole_plane = (here * there)[lanes]
         ones = one[lanes]
         near_core = lax.ppermute(send, "seq", swap_core)
         chip_f = jnp.where(is_c0, c1, ones) * keep[0] + jnp.where(is_c0, ones, c1) * near_core[0]
@@ -461,7 +464,9 @@
         going = jnp.stack([chip_f[1], chip_b[1]])
         near_chip = lax.ppermute(going, "seq", swap_chip)
         if not goings:
-            goings.append(prepare(log_decay, state_write, state_read, skip, going))
+            goings.append(prepare(
+                    log_decay, state_write, state_read, skip_gain.reshape(1, heads), going, columns
+                ))
             near_chip, _ = lax.optimization_barrier((near_chip, goings[0][-1]))
         plane_f = jnp.where(is_y0, y1, ones) * chip_f[0] + jnp.where(is_y0, ones, y1) * near_chip[0]
         plane_b = jnp.where(is_y0, ones, y0) * chip_b[0] + jnp.where(is_y0, y0, ones) * near_chip[1]
@@ -515,7 +520,8 @@
         pair = made[2 * k : 2 * k + 2]
         travels.append((first, blocks, travel(first, blocks, *pair)))
         first += blocks
-    prepared = [*goings[0], state_write, state_read]
+    *prepared, skip = goings[0]
+    prepared += [state_write, state_read]
     results = None
     for k, (first, blocks, pieces) in enumerate(travels):
         results = make_outputs(

time: 97.1 us -> 93.7 us (0.965)
  other arithmetic: 12.1 us -> 9.02 us
  local copies, waits for them, and re-layouts: 2.62 us -> 0.17 us
  waiting for transfers between devices: 16.2 us -> 18.2 us
    another operation x3 -> x0, other arithmetic: 2.2 us -> none  [the longest x2 2.19 us: travel(): c0, c1, y0, y1, whole_plane = keepers[:, lanes]]
    ppermute x3, waiting for transfers between devices: 0.01 us -> 1.56 us  [local(): lax.ppermute(own, 'seq', [(i, i ^ bits) for i in range(devices)])]
    reduce_sum x1 -> x0, other arithmetic: 1 us -> none  [local(): total = jnp.sum(log_decay, axis=1)]
  transfers between devices with their start and end apart: 17 -> 17, of which waited for: 6 -> 9; matrix products, arithmetic and copies ran while one was open for 13% -> 10% of each run, Pallas kernels for 27% -> 17%
where the time goes in v4:
time: 93.7 us; the launch traced here: 93.3 us
  Pallas kernels  36.9 us (39%)
  starting transfers between devices  27.7 us (30%)
  waiting for transfers between devices  18.2 us (19%)
  other arithmetic  9.02 us (10%)
  between operations  1.26 us (1%)
    pallas_call x2, Pallas kernels, make_outputs(): pl.pallas_call(functools.partial(block_kernel, first_head=first * LANES /...  23.1 us
    ppermute x6, starting transfers between devices, travel(): came = lax.ppermute(going, 'seq', pairs)  10.3 us
    ppermute x2, starting transfers between devices, travel(): return (mine, lax.ppermute(theirs, 'seq', swap_core))  10.1 us
    pallas_call x1, Pallas kernels, make_states(): pl.pallas_call(functools.partial(state_kernel, groups=groups, heads=heads...  10.1 us
    ppermute x6, waiting for transfers between devices, travel(): came = lax.ppermute(going, 'seq', pairs)  8.88 us
    ppermute x2, waiting for transfers between devices, travel(): near_chip = lax.ppermute(going, 'seq', swap_chip)  5.22 us
    pallas_call x1, Pallas kernels, prepare(): pl.pallas_call(prepare_kernel, in_specs=[whole((1, heads)), ANYWHERE, *sm...  3.74 us
    ppermute x3, starting transfers between devices, local(): lax.ppermute(own, 'seq', [(i, i ^ bits) for i in range(devices)])  3.16 us
  transfers between devices with their start and end apart: 17, of which 9 were waited for; matrix products, arithmetic and copies ran while one was open for 10% of the time, Pallas kernels for 17%

profile of v4, /device:TPU:1, one launch (start us, length us, event | category | flops | bytes accessed | tf_op | source)
XLA Modules:
  0.0 93.3 jit_solution(15626070945257060150)
XLA Ops:
  0.7 10.1 %shard_map.101 = (f32[2,2,32,1536]{3,2,1,0:T(8,128)S(1)}, f32[2,2,32,1536]{3,2,1,0:T(8,128)S(1)}, f32[2,2,32,1024]{3,2,1,0:T(8,128)S(1)}, f32[2,2,32,1024]{3,2,1,0:T(8,128)S(1)}, f32[8,2560]{1,0:T(8,128)S(1)}) custom-call(s32[1]{0:T(128)} %bitcast.slot_ref, f32[40,512]{1,0:T(8,128)} %decay_ref.3, f32[512,128]{1,0:T(8,128)} %write_ref.7, ...), custom_call_target="tpu_custom_call" | custom-call | flops 2013265920 | bytes 10485760 | tf_op jit(solution)/shard_map/pallas_call | solution.py:316
  10.8 2.7 %collective-permute-start.3 = (f32[2560]{0:T(1024)S(1)}, f32[2560]{0:T(1024)S(1)}, u32[]{:S(2)}, u32[]{:S(2)}) collective-permute-start(f32[2560]{0:T(1024)S(1)} %slice_reduce_fusion), channel_id=1, source_target_pairs={{0,3},{1,2},{2,1},{3,0},{4,7},{5,6},{6,5},{7,4},{8,11},{9,10},{10,... | collective-permute-start | bytes 30728 | tf_op jit(solution)/shard_map/ppermute | solution.py:448
  13.5 0.5 collective-permute-start
  14.0 0.0 collective-permute-start.4
  14.0 0.5 collective-permute-start.1
  14.5 0.4 collective-permute-done.3
  14.9 1.2 %collective-permute-done.2 = f32[2560]{0:T(1024)S(1)} collective-permute-done((f32[2560]{0:T(1024)S(1)}, f32[2560]{0:T(1024)S(1)}, u32[]{:S(2)}, u32[]{:S(2)}) %collective-permute-start.2) | collective-permute-done | bytes 10272 | tf_op jit(solution)/shard_map/ppermute | solution.py:448
  16.2 0.9 collective-permute-done.1
  17.0 0.1 fusion.1
  17.2 0.8 pad_maximum_fusion.4._late
  18.0 1.1 %collective-permute-start.11 = (f32[2,32,1536]{2,1,0:T(8,128)}, f32[2,32,1536]{2,1,0:T(8,128)}, u32[]{:S(2)}, u32[]{:S(2)}) collective-permute-start(f32[2,32,1536]{2,1,0:T(8,128)} %pad_maximum_fusion.4._late), channel_id=1, source_target_pairs={{0,2},{1,3},{2,0},{3,1},{4,6},{5,7},{6,4},{7,5},{8,10},{9,11},{10,... | collective-permute-start | bytes 1179656 | tf_op jit(solution)/shard_map/ppermute | solution.py:465
  19.2 1.1 %fusion.3 = (f32[2,32,1024]{2,1,0:T(8,128)S(1)}, f32[2,32,1024]{2,1,0:T(8,128)S(1)}) fusion(f32[2,2,32,1024]{3,2,1,0:T(8,128)} %collective-permute-done.4, f32[2,2,32,1024]{3,2,1,0:T(8,128)S(1)} %get-tuple-element.40, f32[1024]{0:T(1024)S(1)} %get-tuple-element.135, f32[1024]{0:T(1024)S(1)} %get-tuple-element.136, f32[1024]{0:T(1024)S(1)} %get-tuple-element.114, ...), kind=kLoop, calls=%fused_computation.26 | loop fusion | flops 393216 | bytes 1589248 | tf_op jit(solution)/shard_map/add | solution.py:462
  20.3 0.7 pad_maximum_fusion.8
  21.0 0.3 collective-permute-start.5
  21.4 3.7 %shard_map.102 = (bf16[4,256,384]{2,1,0:T(8,128)(2,1)}, bf16[4,256,384]{2,1,0:T(8,128)(2,1)}, bf16[4,128,384]{2,1,0:T(8,128)(2,1)}, bf16[4,128,384]{2,1,0:T(8,12...) custom-call(f32[1,40]{1,0:T(1,128)} %bitcast.120, ...), custom_call_target="tpu_custom_call" | custom-call | flops 1073741824 | bytes 6291456 | tf_op jit(solution)/shard_map/pallas_call | solution.py:353
  25.1 3.8 %collective-permute-done.11 = f32[2,32,1536]{2,1,0:T(8,128)} collective-permute-done((f32[2,32,1536]{2,1,0:T(8,128)}, f32[2,32,1536]{2,1,0:T(8,128)}, u32[]{:S(2)}, u32[]{:S(2)}) %collective-permute-start.11) | collective-permute-done | bytes 393248 | tf_op jit(solution)/shard_map/ppermute | solution.py:465
  28.9 1.1 %add_select_fusion.10 = (f32[32,1536]{1,0:T(8,128)S(1)}, f32[32,1536]{1,0:T(8,128)S(1)}, f32[32,1536]{1,0:T(8,128)S(1)}) fusion(f32[1536]{0:T(1024)S(1)} %get-tuple-element.108, pred[]{:T(512)S(6)} %eq.20, f32[2,32,1536]{2,1,0:T(8,128)} %collective-permute-done.11, f32[1536]{0:T(1024)S(1)} %get-tuple-element.111, f32[2,32,1536]{2,1,0:T(8,128)S(1)} %get-tuple-element.65, ...), kind=kLoop, calls=%fused_computation.50 | loop fusion | flops 442368 | bytes 1406977 | tf_op jit(solution)/shard_map/jit(_where)/select_n | solution.py:477
  30.0 3.1 %collective-permute-start.12 = (f32[32,1536]{1,0:T(8,128)S(1)}, f32[32,1536]{1,0:T(8,128)S(1)}, u32[]{:S(2)}, u32[]{:S(2)}) collective-permute-start(f32[32,1536]{1,0:T(8,128)S(1)} %get-tuple-element.56), channel_id=1, source_target_pairs={{0,4},{1,5},{2,6},{3,7},{12,8},{13,9},{14,10},{15,11},{16,20},{17,... | collective-permute-start | bytes 589832 | tf_op jit(solution)/shard_map/ppermute | solution.py:485
  33.1 1.4 %collective-permute-done.5 = f32[2,32,1024]{2,1,0:T(8,128)} collective-permute-done((f32[2,32,1024]{2,1,0:T(8,128)}, f32[2,32,1024]{2,1,0:T(8,128)}, u32[]{:S(2)}, u32[]{:S(2)}) %collective-permute-start.5) | collective-permute-done | bytes 262176 | tf_op jit(solution)/shard_map/ppermute | solution.py:465
  34.5 1.0 %add_select_fusion.13 = (f32[32,1024]{1,0:T(8,128)S(1)}, f32[32,1024]{1,0:T(8,128)S(1)}, f32[32,1024]{1,0:T(8,128)S(1)}) fusion(f32[1024]{0:T(1024)S(1)} %get-tuple-element.122, pred[]{:T(512)S(6)} %eq.20, f32[2,32,1024]{2,1,0:T(8,128)} %collective-permute-done.5, f32[1024]{0:T(1024)S(1)} %get-tuple-element.125, f32[2,32,1024]{2,1,0:T(8,128)S(1)} %get-tuple-element.67, ...), kind=kLoop, calls=%fused_computation.65 | loop fusion | flops 294912 | bytes 937985 | tf_op jit(solution)/shard_map/jit(_where)/select_n | solution.py:477
  35.6 3.1 %collective-permute-start.6 = (f32[32,1024]{1,0:T(8,128)S(1)}, f32[32,1024]{1,0:T(8,128)S(1)}, u32[]{:S(2)}, u32[]{:S(2)}) collective-permute-start(f32[32,1024]{1,0:T(8,128)S(1)} %get-tuple-element.62), channel_id=1, source_target_pairs={{0,4},{1,5},{2,6},{3,7},{12,8},{13,9},{14,10},{15,11},{16,20},{17,... | collective-permute-start | bytes 393224 | tf_op jit(solution)/shard_map/ppermute | solution.py:485
  38.7 0.1 add_select_fusion.9
  38.7 0.7 collective-permute-start.13
  39.4 1.2 %collective-permute-done.6 = f32[32,1024]{1,0:T(8,128)S(1)} collective-permute-done((f32[32,1024]{1,0:T(8,128)S(1)}, f32[32,1024]{1,0:T(8,128)S(1)}, u32[]{:S(2)}, u32[]{:S(2)}) %collective-permute-start.6) | collective-permute-done | bytes 131104 | tf_op jit(solution)/shard_map/ppermute | solution.py:485
  40.6 0.7 collective-permute-start.7
  41.3 0.1 add_select_fusion.8
  41.4 1.3 %collective-permute-start.14 = (f32[32,1536]{1,0:T(8,128)S(1)}, f32[32,1536]{1,0:T(8,128)S(1)}, u32[]{:S(2)}, u32[]{:S(2)}) collective-permute-start(f32[32,1536]{1,0:T(8,128)S(1)} %get-tuple-element.53), channel_id=1, source_target_pairs={{8,12},{9,13},{10,14},{11,15},{4,0},{5,1},{6,2},{7,3},{24,28},{25,... | collective-permute-start | bytes 589832 | tf_op jit(solution)/shard_map/ppermute | solution.py:485
  42.7 0.1 add_select_fusion.11
  42.8 1.5 %collective-permute-start.8 = (f32[32,1024]{1,0:T(8,128)S(1)}, f32[32,1024]{1,0:T(8,128)S(1)}, u32[]{:S(2)}, u32[]{:S(2)}) collective-permute-start(f32[32,1024]{1,0:T(8,128)S(1)} %get-tuple-element.59), channel_id=1, source_target_pairs={{8,12},{9,13},{10,14},{11,15},{4,0},{5,1},{6,2},{7,3},{24,28},{25,... | collective-permute-start | bytes 393224 | tf_op jit(solution)/shard_map/ppermute | solution.py:485
  44.2 5.9 %collective-permute-done.14 = f32[32,1536]{1,0:T(8,128)S(1)} collective-permute-done((f32[32,1536]{1,0:T(8,128)S(1)}, f32[32,1536]{1,0:T(8,128)S(1)}, u32[]{:S(2)}, u32[]{:S(2)}) %collective-permute-start.14) | collective-permute-done | bytes 196640 | tf_op jit(solution)/shard_map/ppermute | solution.py:485
  50.1 1.1 %fusion.9 = (f32[1,1,32,1536]{3,2,1,0:T(8,128)S(1)}, f32[1,1,32,1536]{3,2,1,0:T(8,128)S(1)}, f32[1,32,1536]{2,1,0:T(8,128)S(1)}, f32[1,32,1536]{2,1,0:T(8,128)S(1)}) fusion(f32[2,32,1536]{2,1,0:T(8,128)} %collective-permute-done.11, f32[1536]{0:T(1024)S(1)} %get-tuple-element.128, pred[]{:T(512)S(6)} %eq.16, f32[32,1536]{1,0:T(8,128)S(1)} %collective-permute-done.14, ...), kind=kLoop, calls=%fused_computation.45 | loop fusion | flops 589824 | bytes 2174979 | tf_op jit(solution)/shard_map/stack | solution.py:501
  51.3 1.1 %collective-permute-start.15 = (f32[2,32,1536]{2,1,0:T(8,128)S(1)}, f32[2,32,1536]{2,1,0:T(8,128)S(1)}, u32[]{:S(2)}, u32[]{:S(2)}) collective-permute-start(f32[2,32,1536]{2,1,0:T(8,128)S(1)} %pad_maximum_fusion.5), channel_id=1, source_target_pairs={{0,2},{1,3},{2,0},{3,1},{4,6},{5,7},{6,4},{7,5},{8,10},{9,11},{10,... | collective-permute-start | bytes 1179656 | tf_op jit(solution)/shard_map/ppermute | solution.py:500
  52.4 1.8 %collective-permute-done.8 = f32[32,1024]{1,0:T(8,128)S(1)} collective-permute-done((f32[32,1024]{1,0:T(8,128)S(1)}, f32[32,1024]{1,0:T(8,128)S(1)}, u32[]{:S(2)}, u32[]{:S(2)}) %collective-permute-start.8) | collective-permute-done | bytes 131104 | tf_op jit(solution)/shard_map/ppermute | solution.py:485
  54.2 1.0 %select_bitcast_fusion.5 = (f32[1,1,32,1024]{3,2,1,0:T(8,128)S(1)}, f32[1,1,32,1024]{3,2,1,0:T(8,128)S(1)}, f32[1,32,1024]{2,1,0:T(8,128)S(1)}, f32[1,32,1024]{2,1,0:T(8,128)S(1)}) fusion(f32[2,32,1024]{2,1,0:T(8,128)} %collective-permute-done.5, f32[1024]{0:T(1024)S(1)} %get-tuple-element.131, pred[]{:T(512)S(6)} %eq.16, ...), kind=kLoop, calls=%fused_computation.62 | loop fusion | flops 393216 | bytes 1449987 | tf_op jit(solution)/shard_map/stack | solution.py:501
  55.3 1.0 %collective-permute-start.9 = (f32[2,32,1024]{2,1,0:T(8,128)S(1)}, f32[2,32,1024]{2,1,0:T(8,128)S(1)}, u32[]{:S(2)}, u32[]{:S(2)}) collective-permute-start(f32[2,32,1024]{2,1,0:T(8,128)S(1)} %pad_maximum_fusion.9), channel_id=1, source_target_pairs={{0,2},{1,3},{2,0},{3,1},{4,6},{5,7},{6,4},{7,5},{8,10},{9,11},{10,... | collective-permute-start | bytes 786440 | tf_op jit(solution)/shard_map/ppermute | solution.py:500
  56.3 1.7 %collective-permute-done.15 = f32[2,32,1536]{2,1,0:T(8,128)S(1)} collective-permute-done((f32[2,32,1536]{2,1,0:T(8,128)S(1)}, f32[2,32,1536]{2,1,0:T(8,128)S(1)}, u32[]{:S(2)}, u32[]{:S(2)}) %collective-permute-start.15) | collective-permute-done | bytes 393248 | tf_op jit(solution)/shard_map/ppermute | solution.py:500
  58.0 0.0 copy-start
  58.0 0.0 copy-start.1
  58.0 0.0 copy-start.4
  58.1 0.0 copy-start.6
  58.1 0.3 add_select_fusion.3
  58.4 0.1 pad_maximum_fusion.1
  58.4 7.8 %collective-permute-start.16 = (f32[2,2,32,1536]{3,2,1,0:T(8,128)S(1)}, f32[2,2,32,1536]{3,2,1,0:T(8,128)S(1)}, u32[]{:S(2)}, u32[]{:S(2)}) collective-permute-start(f32[2,2,32,1536]{3,2,1,0:T(8,128)S(1)} %pad_maximum_fusion.1), channel_id=1, source_target_pairs={{0,1},{1,0},{2,3},{3,2},{4,5},{5,4},{6,7},{7,6},{8,9},{9,8},{10,11... | collective-permute-start | bytes 2359304 | tf_op jit(solution)/shard_map/ppermute | solution.py:515
  66.2 1.2 %add_select_fusion.7 = (f32[1,2,32,1024]{3,2,1,0:T(8,128)S(1)}, f32[1,2,32,1024]{3,2,1,0:T(8,128)S(1)}, f32[1,2,32,1024]{3,2,1,0:T(8,128)S(1)}, f32[1,2,32,1024]{3,2,1,0:T(8,128)S(1)}) fusion(f32[2,2,32,1024]{3,2,1,0:T(8,128)} %collective-permute-done.4, f32[1,1,32,1024]{3,2,1,0:T(8,128)S(1)} %get-tuple-element.91, ...), kind=kLoop, calls=%fused_computation.31 | loop fusion | flops 786432 | bytes 2629633 | tf_op jit(solution)/shard_map/jit(_where)/select_n | solution.py:505
  67.5 2.4 %collective-permute-start.10 = (f32[2,2,32,1024]{3,2,1,0:T(8,128)S(1)}, f32[2,2,32,1024]{3,2,1,0:T(8,128)S(1)}, u32[]{:S(2)}, u32[]{:S(2)}) collective-permute-start(f32[2,2,32,1024]{3,2,1,0:T(8,128)S(1)} %pad_maximum_fusion.3), channel_id=1, source_target_pairs={{0,1},{1,0},{2,3},{3,2},{4,5},{5,4},{6,7},{7,6},{8,9},{9,8},{10,11... | collective-permute-start | bytes 1572872 | tf_op jit(solution)/shard_map/ppermute | solution.py:515
  69.9 0.1 pad_maximum_fusion.mine_ref
  70.0 12.4 %shard_map.103 = (f32[512,2560]{1,0:T(8,128)}, f32[512,2560]{1,0:T(8,128)}, f32[4,256,128]{2,1,0:T(8,128)S(1)}, f32[4,128,128]{2,1,0:T(8,128)S(1)}, f32[512,128]{1,0:T(8,128)S(1)}) custom-call(s32[1]{0:T(128)} %bitcast.slot_ref, bf16[4,256,384]{2,1,0:T(8,128)(2,1)S(1)} %copy-done, bf16[4,256,384]{2,1,0:T(8,128)(2,1)S(1)} %copy-done.1, ...), custom_call_target="tpu_custom_call" | custom-call | flops 14092861440 | bytes 12582912 | tf_op jit(solution)/shard_map/pallas_call | solution.py:388
  82.4 10.7 %shard_map.104 = (f32[512,2560]{1,0:T(8,128)}, f32[512,2560]{1,0:T(8,128)}, f32[4,256,128]{2,1,0:T(8,128)}, f32[4,128,128]{2,1,0:T(8,128)}, f32[512,128]{1,0:T(8...) custom-call(s32[1]{0:T(128)} %bitcast.slot_ref, ...), custom_call_target="tpu_custom_call", output_to_operand_aliasing={{0}: (15, {}), {1}: (16, {})} | custom-call | flops 9395240960 | bytes 8388608 | tf_op jit(solution)/shard_map/pallas_call | solution.py:388
  (40 shorter events, 0.4 us)
Async XLA Ops:
  10.8 4.1 %collective-permute-start.3 = (f32[2560]{0:T(1024)S(1)}, f32[2560]{0:T(1024)S(1)}, u32[]{:S(2)}, u32[]{:S(2)}) collective-permute-start(f32[2560]{0:T(1024)S(1)} %slice_reduce_fusion), channel_id=1, source_target_pairs={{0,3},{1,2},{2,1},{3,0},{4,7},{5,6},{6,5},{7,4},{8,11},{9,10},{10,... | collective-permute-start | bytes 30728 | tf_op jit(solution)/shard_map/ppermute | solution.py:448
  13.5 2.5 %collective-permute-start.2 = (f32[2560]{0:T(1024)S(1)}, f32[2560]{0:T(1024)S(1)}, u32[]{:S(2)}, u32[]{:S(2)}) collective-permute-start(f32[2560]{0:T(1024)S(1)} %slice_reduce_fusion), channel_id=1, source_target_pairs={{0,2},{1,3},{2,0},{3,1},{4,6},{5,7},{6,4},{7,5},{8,10},{9,11},{10,... | collective-permute-start | bytes 30728 | tf_op jit(solution)/shard_map/ppermute | solution.py:448
  13.5 2.5 %collective-permute-start = (f32[2560]{0:T(1024)S(1)}, f32[2560]{0:T(1024)S(1)}, u32[]{:S(2)}, u32[]{:S(2)}) collective-permute-start(f32[2560]{0:T(1024)S(1)} %slice_reduce_fusion), channel_id=1, source_target_pairs={{0,1},{1,0},{2,3},{3,2},{4,5},{5,4},{6,7},{7,6},{8,9},{9,8},{10,11... | collective-permute-start | bytes 30728 | tf_op jit(solution)/shard_map/ppermute | solution.py:448
  14.0 5.1 %collective-permute-start.4 = (f32[2,2,32,1024]{3,2,1,0:T(8,128)S(1)}, f32[2,2,32,1024]{3,2,1,0:T(8,128)}, u32[]{:S(2)}, u32[]{:S(2)}) collective-permute-start(f32[2,2,32,1024]{3,2,1,0:T(8,128)S(1)} %get-tuple-element.41), channel_id=1, source_target_pairs={{0,1},{1,0},{2,3},{3,2},{4,5},{5,4},{6,7},{7,6},{8,9},{9,8},{10,11... | collective-permute-start | bytes 1572872 | tf_op jit(solution)/shard_map/ppermute | solution.py:461
  14.0 3.0 %collective-permute-start.1 = (f32[2,2,32,1536]{3,2,1,0:T(8,128)S(1)}, f32[2,2,32,1536]{3,2,1,0:T(8,128)S(1)}, u32[]{:S(2)}, u32[]{:S(2)}) collective-permute-start(f32[2,2,32,1536]{3,2,1,0:T(8,128)S(1)} %get-tuple-element.31), channel_id=1, source_target_pairs={{0,1},{1,0},{2,3},{3,2},{4,5},{5,4},{6,7},{7,6},{8,9},{9,8},{10,11... | collective-permute-start | bytes 2359304 | tf_op jit(solution)/shard_map/ppermute | solution.py:461
  18.0 10.9 %collective-permute-start.11 = (f32[2,32,1536]{2,1,0:T(8,128)}, f32[2,32,1536]{2,1,0:T(8,128)}, u32[]{:S(2)}, u32[]{:S(2)}) collective-permute-start(f32[2,32,1536]{2,1,0:T(8,128)} %pad_maximum_fusion.4._late), channel_id=1, source_target_pairs={{0,2},{1,3},{2,0},{3,1},{4,6},{5,7},{6,4},{7,5},{8,10},{9,11},{10,... | collective-permute-start | bytes 1179656 | tf_op jit(solution)/shard_map/ppermute | solution.py:465
  21.0 13.5 %collective-permute-start.5 = (f32[2,32,1024]{2,1,0:T(8,128)}, f32[2,32,1024]{2,1,0:T(8,128)}, u32[]{:S(2)}, u32[]{:S(2)}) collective-permute-start(f32[2,32,1024]{2,1,0:T(8,128)} %pad_maximum_fusion.8), channel_id=1, source_target_pairs={{0,2},{1,3},{2,0},{3,1},{4,6},{5,7},{6,4},{7,5},{8,10},{9,11},{10,... | collective-permute-start | bytes 786440 | tf_op jit(solution)/shard_map/ppermute | solution.py:465
  30.0 8.6 %collective-permute-start.12 = (f32[32,1536]{1,0:T(8,128)S(1)}, f32[32,1536]{1,0:T(8,128)S(1)}, u32[]{:S(2)}, u32[]{:S(2)}) collective-permute-start(f32[32,1536]{1,0:T(8,128)S(1)} %get-tuple-element.56), channel_id=1, source_target_pairs={{0,4},{1,5},{2,6},{3,7},{12,8},{13,9},{14,10},{15,11},{16,20},{17,... | collective-permute-start | bytes 589832 | tf_op jit(solution)/shard_map/ppermute | solution.py:485
  35.6 5.0 %collective-permute-start.6 = (f32[32,1024]{1,0:T(8,128)S(1)}, f32[32,1024]{1,0:T(8,128)S(1)}, u32[]{:S(2)}, u32[]{:S(2)}) collective-permute-start(f32[32,1024]{1,0:T(8,128)S(1)} %get-tuple-element.62), channel_id=1, source_target_pairs={{0,4},{1,5},{2,6},{3,7},{12,8},{13,9},{14,10},{15,11},{16,20},{17,... | collective-permute-start | bytes 393224 | tf_op jit(solution)/shard_map/ppermute | solution.py:485
  38.7 2.6 %collective-permute-start.13 = (f32[32,1536]{1,0:T(8,128)S(1)}, f32[32,1536]{1,0:T(8,128)S(1)}, u32[]{:S(2)}, u32[]{:S(2)}) collective-permute-start(f32[32,1536]{1,0:T(8,128)S(1)} %add_select_fusion.9), channel_id=1, source_target_pairs={{4,8},{5,9},{6,10},{7,11},{8,4},{9,5},{10,6},{11,7},{20,24},{21,25... | collective-permute-start | bytes 589832 | tf_op jit(solution)/shard_map/ppermute | solution.py:485
  40.6 2.1 %collective-permute-start.7 = (f32[32,1024]{1,0:T(8,128)S(1)}, f32[32,1024]{1,0:T(8,128)S(1)}, u32[]{:S(2)}, u32[]{:S(2)}) collective-permute-start(f32[32,1024]{1,0:T(8,128)S(1)} %add_select_fusion.12), channel_id=1, source_target_pairs={{4,8},{5,9},{6,10},{7,11},{8,4},{9,5},{10,6},{11,7},{20,24},{21,25... | collective-permute-start | bytes 393224 | tf_op jit(solution)/shard_map/ppermute | solution.py:485
  41.4 8.7 %collective-permute-start.14 = (f32[32,1536]{1,0:T(8,128)S(1)}, f32[32,1536]{1,0:T(8,128)S(1)}, u32[]{:S(2)}, u32[]{:S(2)}) collective-permute-start(f32[32,1536]{1,0:T(8,128)S(1)} %get-tuple-element.53), channel_id=1, source_target_pairs={{8,12},{9,13},{10,14},{11,15},{4,0},{5,1},{6,2},{7,3},{24,28},{25,... | collective-permute-start | bytes 589832 | tf_op jit(solution)/shard_map/ppermute | solution.py:485
  42.8 11.4 %collective-permute-start.8 = (f32[32,1024]{1,0:T(8,128)S(1)}, f32[32,1024]{1,0:T(8,128)S(1)}, u32[]{:S(2)}, u32[]{:S(2)}) collective-permute-start(f32[32,1024]{1,0:T(8,128)S(1)} %get-tuple-element.59), channel_id=1, source_target_pairs={{8,12},{9,13},{10,14},{11,15},{4,0},{5,1},{6,2},{7,3},{24,28},{25,... | collective-permute-start | bytes 393224 | tf_op jit(solution)/shard_map/ppermute | solution.py:485
  51.3 6.7 %collective-permute-start.15 = (f32[2,32,1536]{2,1,0:T(8,128)S(1)}, f32[2,32,1536]{2,1,0:T(8,128)S(1)}, u32[]{:S(2)}, u32[]{:S(2)}) collective-permute-start(f32[2,32,1536]{2,1,0:T(8,128)S(1)} %pad_maximum_fusion.5), channel_id=1, source_target_pairs={{0,2},{1,3},{2,0},{3,1},{4,6},{5,7},{6,4},{7,5},{8,10},{9,11},{10,... | collective-permute-start | bytes 1179656 | tf_op jit(solution)/shard_map/ppermute | solution.py:500
  55.3 10.9 %collective-permute-start.9 = (f32[2,32,1024]{2,1,0:T(8,128)S(1)}, f32[2,32,1024]{2,1,0:T(8,128)S(1)}, u32[]{:S(2)}, u32[]{:S(2)}) collective-permute-start(f32[2,32,1024]{2,1,0:T(8,128)S(1)} %pad_maximum_fusion.9), channel_id=1, source_target_pairs={{0,2},{1,3},{2,0},{3,1},{4,6},{5,7},{6,4},{7,5},{8,10},{9,11},{10,... | collective-permute-start | bytes 786440 | tf_op jit(solution)/shard_map/ppermute | solution.py:500
  58.0 11.9 %copy-start = (bf16[4,256,384]{2,1,0:T(8,128)(2,1)S(1)}, bf16[4,256,384]{2,1,0:T(8,128)(2,1)}, u32[]{:S(2)}) copy-start(bf16[4,256,384]{2,1,0:T(8,128)(2,1)} %get-tuple-element.32.left_y) | copy-start | bytes 2359300
  58.0 11.9 %copy-start.1 = (bf16[4,256,384]{2,1,0:T(8,128)(2,1)S(1)}, bf16[4,256,384]{2,1,0:T(8,128)(2,1)}, u32[]{:S(2)}) copy-start(bf16[4,256,384]{2,1,0:T(8,128)(2,1)} %get-tuple-element.33.left_x) | copy-start | bytes 2359300
  58.0 11.9 %copy-start.2 = (bf16[4,128,384]{2,1,0:T(8,128)(2,1)S(1)}, bf16[4,128,384]{2,1,0:T(8,128)(2,1)}, u32[]{:S(2)}) copy-start(bf16[4,128,384]{2,1,0:T(8,128)(2,1)} %get-tuple-element.34.left_c) | copy-start | bytes 1179652
  58.0 11.9 %copy-start.3 = (bf16[4,128,384]{2,1,0:T(8,128)(2,1)S(1)}, bf16[4,128,384]{2,1,0:T(8,128)(2,1)}, u32[]{:S(2)}) copy-start(bf16[4,128,384]{2,1,0:T(8,128)(2,1)} %get-tuple-element.35.left_b) | copy-start | bytes 1179652
  58.0 11.9 %copy-start.4 = (bf16[512,128]{1,0:T(8,128)(2,1)S(1)}, bf16[512,128]{1,0:T(8,128)(2,1)}, u32[]{:S(2)}) copy-start(bf16[512,128]{1,0:T(8,128)(2,1)} %get-tuple-element.36.up) | copy-start | bytes 393220
  58.1 11.9 %copy-start.5 = (bf16[512,128]{1,0:T(8,128)(2,1)S(1)}, bf16[512,128]{1,0:T(8,128)(2,1)}, u32[]{:S(2)}) copy-start(bf16[512,128]{1,0:T(8,128)(2,1)} %get-tuple-element.37.down) | copy-start | bytes 393220
  58.1 11.9 %copy-start.6 = (bf16[4,16,128]{2,1,0:T(8,128)(2,1)S(1)}, bf16[4,16,128]{2,1,0:T(8,128)(2,1)}, u32[]{:S(2)}) copy-start(bf16[4,16,128]{2,1,0:T(8,128)(2,1)} %get-tuple-element.38.edges) | copy-start | bytes 49156
  58.1 11.9 %copy-start.7 = (f32[1,2560]{1,0:T(1,128)S(1)}, f32[1,2560]{1,0:T(1,128)}, u32[]{:S(2)}) copy-start(f32[1,2560]{1,0:T(1,128)} %get-tuple-element.39.skip_ref) | copy-start | bytes 30724
  58.4 11.5 %collective-permute-start.16 = (f32[2,2,32,1536]{3,2,1,0:T(8,128)S(1)}, f32[2,2,32,1536]{3,2,1,0:T(8,128)S(1)}, u32[]{:S(2)}, u32[]{:S(2)}) collective-permute-start(f32[2,2,32,1536]{3,2,1,0:T(8,128)S(1)} %pad_maximum_fusion.1), channel_id=1, source_target_pairs={{0,1},{1,0},{2,3},{3,2},{4,5},{5,4},{6,7},{7,6},{8,9},{9,8},{10,11... | collective-permute-start | bytes 2359304 | tf_op jit(solution)/shard_map/ppermute | solution.py:515
  67.5 14.9 %collective-permute-start.10 = (f32[2,2,32,1024]{3,2,1,0:T(8,128)S(1)}, f32[2,2,32,1024]{3,2,1,0:T(8,128)S(1)}, u32[]{:S(2)}, u32[]{:S(2)}) collective-permute-start(f32[2,2,32,1024]{3,2,1,0:T(8,128)S(1)} %pad_maximum_fusion.3), channel_id=1, source_target_pairs={{0,1},{1,0},{2,3},{3,2},{4,5},{5,4},{6,7},{7,6},{8,9},{9,8},{10,11... | collective-permute-start | bytes 1572872 | tf_op jit(solution)/shard_map/ppermute | solution.py:515

commit v5 on v4

--- a/solution.py
+++ b/solution.py
@@ -123,7 +123,13 @@
         ((x_ref, tail, write_t), (g_ref, lead, read_t))
     ):
         scale = dot(weight[...], spread)
-        stage[which] = dot3(factor[...], *split(value_ref[...] * scale))
+        high, low = split(value_ref[...] * scale)
+        half = rows // 2
+        stage[which] = sum(
+            dot(factor[:, k * rows + h * half : k * rows + (h + 1) * half], part[h * half : (h + 1) * half])
+            for h in range(2)
+            for k, part in ((0, high), (1, low), (2, high))
+        )
         if which == 1:
             decay_out[...] = jnp.broadcast_to(scale[rows - 1 :], decay_out.shape)
     begin = 0

time: 93.7 us -> 93.3 us (level)
  no operation moved by 1% of the time
where the time goes in v5:
time: 93.3 us; the launch traced here: 92.9 us
  Pallas kernels  36.6 us (39%)
  starting transfers between devices  27.7 us (30%)
  waiting for transfers between devices  18.2 us (20%)
  other arithmetic  9.02 us (10%)
  between operations  1.26 us (1%)
    pallas_call x2, Pallas kernels, make_outputs(): pl.pallas_call(functools.partial(block_kernel, first_head=first * LANES /...  23.1 us
    ppermute x6, starting transfers between devices, travel(): came = lax.ppermute(going, 'seq', pairs)  10.3 us
    ppermute x2, starting transfers between devices, travel(): return (mine, lax.ppermute(theirs, 'seq', swap_core))  10.1 us
    pallas_call x1, Pallas kernels, make_states(): pl.pallas_call(functools.partial(state_kernel, groups=groups, heads=heads...  9.76 us
    ppermute x6, waiting for transfers between devices, travel(): came = lax.ppermute(going, 'seq', pairs)  8.88 us
    ppermute x2, waiting for transfers between devices, travel(): near_chip = lax.ppermute(going, 'seq', swap_chip)  5.21 us
    pallas_call x1, Pallas kernels, prepare(): pl.pallas_call(prepare_kernel, in_specs=[whole((1, heads)), ANYWHERE, *sm...  3.74 us
    ppermute x3, starting transfers between devices, local(): lax.ppermute(own, 'seq', [(i, i ^ bits) for i in range(devices)])  3.17 us
  transfers between devices with their start and end apart: 17, of which 9 were waited for; matrix products, arithmetic and copies ran while one was open for 10% of the time, Pallas kernels for 17%

profile of v5, /device:TPU:1, one launch (start us, length us, event | category | flops | bytes accessed | tf_op | source)
XLA Modules:
  0.0 92.9 jit_solution(9104331796345997433)
XLA Ops:
  0.7 9.8 %shard_map.101 = (f32[2,2,32,1536]{3,2,1,0:T(8,128)S(1)}, f32[2,2,32,1536]{3,2,1,0:T(8,128)S(1)}, f32[2,2,32,1024]{3,2,1,0:T(8,128)S(1)}, f32[2,2,32,1024]{3,2,1,0:T(8,128)S(1)}, f32[8,2560]{1,0:T(8,128)S(1)}) custom-call(s32[1]{0:T(128)} %bitcast.slot_ref, f32[40,512]{1,0:T(8,128)} %decay_ref.3, f32[512,128]{1,0:T(8,128)} %write_ref.7, ...), custom_call_target="tpu_custom_call" | custom-call | flops 2013265920 | bytes 10485760 | tf_op jit(solution)/shard_map/pallas_call | solution.py:322
  10.5 2.7 %collective-permute-start.3 = (f32[2560]{0:T(1024)S(1)}, f32[2560]{0:T(1024)S(1)}, u32[]{:S(2)}, u32[]{:S(2)}) collective-permute-start(f32[2560]{0:T(1024)S(1)} %slice_reduce_fusion), channel_id=1, source_target_pairs={{0,3},{1,2},{2,1},{3,0},{4,7},{5,6},{6,5},{7,4},{8,11},{9,10},{10,... | collective-permute-start | bytes 30728 | tf_op jit(solution)/shard_map/ppermute | solution.py:454
  13.2 0.5 collective-permute-start
  13.6 0.0 collective-permute-start.4
  13.7 0.5 collective-permute-start.1
  14.2 0.4 collective-permute-done.3
  14.5 1.2 %collective-permute-done.2 = f32[2560]{0:T(1024)S(1)} collective-permute-done((f32[2560]{0:T(1024)S(1)}, f32[2560]{0:T(1024)S(1)}, u32[]{:S(2)}, u32[]{:S(2)}) %collective-permute-start.2) | collective-permute-done | bytes 10272 | tf_op jit(solution)/shard_map/ppermute | solution.py:454
  15.8 0.9 collective-permute-done.1
  16.7 0.1 fusion.1
  16.9 0.8 pad_maximum_fusion.4._late
  17.7 1.1 %collective-permute-start.11 = (f32[2,32,1536]{2,1,0:T(8,128)}, f32[2,32,1536]{2,1,0:T(8,128)}, u32[]{:S(2)}, u32[]{:S(2)}) collective-permute-start(f32[2,32,1536]{2,1,0:T(8,128)} %pad_maximum_fusion.4._late), channel_id=1, source_target_pairs={{0,2},{1,3},{2,0},{3,1},{4,6},{5,7},{6,4},{7,5},{8,10},{9,11},{10,... | collective-permute-start | bytes 1179656 | tf_op jit(solution)/shard_map/ppermute | solution.py:471
  18.8 1.1 %fusion.3 = (f32[2,32,1024]{2,1,0:T(8,128)S(1)}, f32[2,32,1024]{2,1,0:T(8,128)S(1)}) fusion(f32[2,2,32,1024]{3,2,1,0:T(8,128)} %collective-permute-done.4, f32[2,2,32,1024]{3,2,1,0:T(8,128)S(1)} %get-tuple-element.40, f32[1024]{0:T(1024)S(1)} %get-tuple-element.135, f32[1024]{0:T(1024)S(1)} %get-tuple-element.136, f32[1024]{0:T(1024)S(1)} %get-tuple-element.114, ...), kind=kLoop, calls=%fused_computation.26 | loop fusion | flops 393216 | bytes 1589248 | tf_op jit(solution)/shard_map/add | solution.py:468
  20.0 0.7 pad_maximum_fusion.8
  20.7 0.3 collective-permute-start.5
  21.0 3.7 %shard_map.102 = (bf16[4,256,384]{2,1,0:T(8,128)(2,1)}, bf16[4,256,384]{2,1,0:T(8,128)(2,1)}, bf16[4,128,384]{2,1,0:T(8,128)(2,1)}, bf16[4,128,384]{2,1,0:T(8,12...) custom-call(f32[1,40]{1,0:T(1,128)} %bitcast.120, ...), custom_call_target="tpu_custom_call" | custom-call | flops 1073741824 | bytes 6291456 | tf_op jit(solution)/shard_map/pallas_call | solution.py:359
  24.7 3.8 %collective-permute-done.11 = f32[2,32,1536]{2,1,0:T(8,128)} collective-permute-done((f32[2,32,1536]{2,1,0:T(8,128)}, f32[2,32,1536]{2,1,0:T(8,128)}, u32[]{:S(2)}, u32[]{:S(2)}) %collective-permute-start.11) | collective-permute-done | bytes 393248 | tf_op jit(solution)/shard_map/ppermute | solution.py:471
  28.6 1.1 %add_select_fusion.10 = (f32[32,1536]{1,0:T(8,128)S(1)}, f32[32,1536]{1,0:T(8,128)S(1)}, f32[32,1536]{1,0:T(8,128)S(1)}) fusion(f32[1536]{0:T(1024)S(1)} %get-tuple-element.108, pred[]{:T(512)S(6)} %eq.20, f32[2,32,1536]{2,1,0:T(8,128)} %collective-permute-done.11, f32[1536]{0:T(1024)S(1)} %get-tuple-element.111, f32[2,32,1536]{2,1,0:T(8,128)S(1)} %get-tuple-element.65, ...), kind=kLoop, calls=%fused_computation.50 | loop fusion | flops 442368 | bytes 1406977 | tf_op jit(solution)/shard_map/jit(_where)/select_n | solution.py:483
  29.7 3.1 %collective-permute-start.12 = (f32[32,1536]{1,0:T(8,128)S(1)}, f32[32,1536]{1,0:T(8,128)S(1)}, u32[]{:S(2)}, u32[]{:S(2)}) collective-permute-start(f32[32,1536]{1,0:T(8,128)S(1)} %get-tuple-element.56), channel_id=1, source_target_pairs={{0,4},{1,5},{2,6},{3,7},{12,8},{13,9},{14,10},{15,11},{16,20},{17,... | collective-permute-start | bytes 589832 | tf_op jit(solution)/shard_map/ppermute | solution.py:491
  32.8 1.4 %collective-permute-done.5 = f32[2,32,1024]{2,1,0:T(8,128)} collective-permute-done((f32[2,32,1024]{2,1,0:T(8,128)}, f32[2,32,1024]{2,1,0:T(8,128)}, u32[]{:S(2)}, u32[]{:S(2)}) %collective-permute-start.5) | collective-permute-done | bytes 262176 | tf_op jit(solution)/shard_map/ppermute | solution.py:471
  34.2 1.0 %add_select_fusion.13 = (f32[32,1024]{1,0:T(8,128)S(1)}, f32[32,1024]{1,0:T(8,128)S(1)}, f32[32,1024]{1,0:T(8,128)S(1)}) fusion(f32[1024]{0:T(1024)S(1)} %get-tuple-element.122, pred[]{:T(512)S(6)} %eq.20, f32[2,32,1024]{2,1,0:T(8,128)} %collective-permute-done.5, f32[1024]{0:T(1024)S(1)} %get-tuple-element.125, f32[2,32,1024]{2,1,0:T(8,128)S(1)} %get-tuple-element.67, ...), kind=kLoop, calls=%fused_computation.65 | loop fusion | flops 294912 | bytes 937985 | tf_op jit(solution)/shard_map/jit(_where)/select_n | solution.py:483
  35.2 3.1 %collective-permute-start.6 = (f32[32,1024]{1,0:T(8,128)S(1)}, f32[32,1024]{1,0:T(8,128)S(1)}, u32[]{:S(2)}, u32[]{:S(2)}) collective-permute-start(f32[32,1024]{1,0:T(8,128)S(1)} %get-tuple-element.62), channel_id=1, source_target_pairs={{0,4},{1,5},{2,6},{3,7},{12,8},{13,9},{14,10},{15,11},{16,20},{17,... | collective-permute-start | bytes 393224 | tf_op jit(solution)/shard_map/ppermute | solution.py:491
  38.3 0.1 add_select_fusion.9
  38.4 0.7 collective-permute-start.13
  39.0 1.2 %collective-permute-done.6 = f32[32,1024]{1,0:T(8,128)S(1)} collective-permute-done((f32[32,1024]{1,0:T(8,128)S(1)}, f32[32,1024]{1,0:T(8,128)S(1)}, u32[]{:S(2)}, u32[]{:S(2)}) %collective-permute-start.6) | collective-permute-done | bytes 131104 | tf_op jit(solution)/shard_map/ppermute | solution.py:491
  40.3 0.7 collective-permute-start.7
  40.9 0.1 add_select_fusion.8
  41.0 1.3 %collective-permute-start.14 = (f32[32,1536]{1,0:T(8,128)S(1)}, f32[32,1536]{1,0:T(8,128)S(1)}, u32[]{:S(2)}, u32[]{:S(2)}) collective-permute-start(f32[32,1536]{1,0:T(8,128)S(1)} %get-tuple-element.53), channel_id=1, source_target_pairs={{8,12},{9,13},{10,14},{11,15},{4,0},{5,1},{6,2},{7,3},{24,28},{25,... | collective-permute-start | bytes 589832 | tf_op jit(solution)/shard_map/ppermute | solution.py:491
  42.3 0.1 add_select_fusion.11
  42.4 1.5 %collective-permute-start.8 = (f32[32,1024]{1,0:T(8,128)S(1)}, f32[32,1024]{1,0:T(8,128)S(1)}, u32[]{:S(2)}, u32[]{:S(2)}) collective-permute-start(f32[32,1024]{1,0:T(8,128)S(1)} %get-tuple-element.59), channel_id=1, source_target_pairs={{8,12},{9,13},{10,14},{11,15},{4,0},{5,1},{6,2},{7,3},{24,28},{25,... | collective-permute-start | bytes 393224 | tf_op jit(solution)/shard_map/ppermute | solution.py:491
  43.9 5.9 %collective-permute-done.14 = f32[32,1536]{1,0:T(8,128)S(1)} collective-permute-done((f32[32,1536]{1,0:T(8,128)S(1)}, f32[32,1536]{1,0:T(8,128)S(1)}, u32[]{:S(2)}, u32[]{:S(2)}) %collective-permute-start.14) | collective-permute-done | bytes 196640 | tf_op jit(solution)/shard_map/ppermute | solution.py:491
  49.7 1.1 %fusion.9 = (f32[1,1,32,1536]{3,2,1,0:T(8,128)S(1)}, f32[1,1,32,1536]{3,2,1,0:T(8,128)S(1)}, f32[1,32,1536]{2,1,0:T(8,128)S(1)}, f32[1,32,1536]{2,1,0:T(8,128)S(1)}) fusion(f32[2,32,1536]{2,1,0:T(8,128)} %collective-permute-done.11, f32[1536]{0:T(1024)S(1)} %get-tuple-element.128, pred[]{:T(512)S(6)} %eq.16, f32[32,1536]{1,0:T(8,128)S(1)} %collective-permute-done.14, ...), kind=kLoop, calls=%fused_computation.45 | loop fusion | flops 589824 | bytes 2174979 | tf_op jit(solution)/shard_map/stack | solution.py:507
  50.9 1.1 %collective-permute-start.15 = (f32[2,32,1536]{2,1,0:T(8,128)S(1)}, f32[2,32,1536]{2,1,0:T(8,128)S(1)}, u32[]{:S(2)}, u32[]{:S(2)}) collective-permute-start(f32[2,32,1536]{2,1,0:T(8,128)S(1)} %pad_maximum_fusion.5), channel_id=1, source_target_pairs={{0,2},{1,3},{2,0},{3,1},{4,6},{5,7},{6,4},{7,5},{8,10},{9,11},{10,... | collective-permute-start | bytes 1179656 | tf_op jit(solution)/shard_map/ppermute | solution.py:506
  52.0 1.8 %collective-permute-done.8 = f32[32,1024]{1,0:T(8,128)S(1)} collective-permute-done((f32[32,1024]{1,0:T(8,128)S(1)}, f32[32,1024]{1,0:T(8,128)S(1)}, u32[]{:S(2)}, u32[]{:S(2)}) %collective-permute-start.8) | collective-permute-done | bytes 131104 | tf_op jit(solution)/shard_map/ppermute | solution.py:491
  53.8 1.0 %select_bitcast_fusion.5 = (f32[1,1,32,1024]{3,2,1,0:T(8,128)S(1)}, f32[1,1,32,1024]{3,2,1,0:T(8,128)S(1)}, f32[1,32,1024]{2,1,0:T(8,128)S(1)}, f32[1,32,1024]{2,1,0:T(8,128)S(1)}) fusion(f32[2,32,1024]{2,1,0:T(8,128)} %collective-permute-done.5, f32[1024]{0:T(1024)S(1)} %get-tuple-element.131, pred[]{:T(512)S(6)} %eq.16, ...), kind=kLoop, calls=%fused_computation.62 | loop fusion | flops 393216 | bytes 1449987 | tf_op jit(solution)/shard_map/stack | solution.py:507
  54.9 1.0 %collective-permute-start.9 = (f32[2,32,1024]{2,1,0:T(8,128)S(1)}, f32[2,32,1024]{2,1,0:T(8,128)S(1)}, u32[]{:S(2)}, u32[]{:S(2)}) collective-permute-start(f32[2,32,1024]{2,1,0:T(8,128)S(1)} %pad_maximum_fusion.9), channel_id=1, source_target_pairs={{0,2},{1,3},{2,0},{3,1},{4,6},{5,7},{6,4},{7,5},{8,10},{9,11},{10,... | collective-permute-start | bytes 786440 | tf_op jit(solution)/shard_map/ppermute | solution.py:506
  55.9 1.7 %collective-permute-done.15 = f32[2,32,1536]{2,1,0:T(8,128)S(1)} collective-permute-done((f32[2,32,1536]{2,1,0:T(8,128)S(1)}, f32[2,32,1536]{2,1,0:T(8,128)S(1)}, u32[]{:S(2)}, u32[]{:S(2)}) %collective-permute-start.15) | collective-permute-done | bytes 393248 | tf_op jit(solution)/shard_map/ppermute | solution.py:506
  57.6 0.0 copy-start
  57.6 0.0 copy-start.1
  57.7 0.0 copy-start.4
  57.7 0.0 copy-start.6
  57.7 0.3 add_select_fusion.3
  58.0 0.1 pad_maximum_fusion.1
  58.0 7.8 %collective-permute-start.16 = (f32[2,2,32,1536]{3,2,1,0:T(8,128)S(1)}, f32[2,2,32,1536]{3,2,1,0:T(8,128)S(1)}, u32[]{:S(2)}, u32[]{:S(2)}) collective-permute-start(f32[2,2,32,1536]{3,2,1,0:T(8,128)S(1)} %pad_maximum_fusion.1), channel_id=1, source_target_pairs={{0,1},{1,0},{2,3},{3,2},{4,5},{5,4},{6,7},{7,6},{8,9},{9,8},{10,11... | collective-permute-start | bytes 2359304 | tf_op jit(solution)/shard_map/ppermute | solution.py:521
  65.8 1.2 %add_select_fusion.7 = (f32[1,2,32,1024]{3,2,1,0:T(8,128)S(1)}, f32[1,2,32,1024]{3,2,1,0:T(8,128)S(1)}, f32[1,2,32,1024]{3,2,1,0:T(8,128)S(1)}, f32[1,2,32,1024]{3,2,1,0:T(8,128)S(1)}) fusion(f32[2,2,32,1024]{3,2,1,0:T(8,128)} %collective-permute-done.4, f32[1,1,32,1024]{3,2,1,0:T(8,128)S(1)} %get-tuple-element.91, ...), kind=kLoop, calls=%fused_computation.31 | loop fusion | flops 786432 | bytes 2629633 | tf_op jit(solution)/shard_map/jit(_where)/select_n | solution.py:511
  67.1 2.4 %collective-permute-start.10 = (f32[2,2,32,1024]{3,2,1,0:T(8,128)S(1)}, f32[2,2,32,1024]{3,2,1,0:T(8,128)S(1)}, u32[]{:S(2)}, u32[]{:S(2)}) collective-permute-start(f32[2,2,32,1024]{3,2,1,0:T(8,128)S(1)} %pad_maximum_fusion.3), channel_id=1, source_target_pairs={{0,1},{1,0},{2,3},{3,2},{4,5},{5,4},{6,7},{7,6},{8,9},{9,8},{10,11... | collective-permute-start | bytes 1572872 | tf_op jit(solution)/shard_map/ppermute | solution.py:521
  69.5 0.1 pad_maximum_fusion.mine_ref
  69.6 12.3 %shard_map.103 = (f32[512,2560]{1,0:T(8,128)}, f32[512,2560]{1,0:T(8,128)}, f32[4,256,128]{2,1,0:T(8,128)S(1)}, f32[4,128,128]{2,1,0:T(8,128)S(1)}, f32[512,128]{1,0:T(8,128)S(1)}) custom-call(s32[1]{0:T(128)} %bitcast.slot_ref, bf16[4,256,384]{2,1,0:T(8,128)(2,1)S(1)} %copy-done, bf16[4,256,384]{2,1,0:T(8,128)(2,1)S(1)} %copy-done.1, ...), custom_call_target="tpu_custom_call" | custom-call | flops 14092861440 | bytes 12582912 | tf_op jit(solution)/shard_map/pallas_call | solution.py:394
  82.0 10.7 %shard_map.104 = (f32[512,2560]{1,0:T(8,128)}, f32[512,2560]{1,0:T(8,128)}, f32[4,256,128]{2,1,0:T(8,128)}, f32[4,128,128]{2,1,0:T(8,128)}, f32[512,128]{1,0:T(8...) custom-call(s32[1]{0:T(128)} %bitcast.slot_ref, ...), custom_call_target="tpu_custom_call", output_to_operand_aliasing={{0}: (15, {}), {1}: (16, {})} | custom-call | flops 9395240960 | bytes 8388608 | tf_op jit(solution)/shard_map/pallas_call | solution.py:394
  (40 shorter events, 0.4 us)
Async XLA Ops:
  10.5 4.1 %collective-permute-start.3 = (f32[2560]{0:T(1024)S(1)}, f32[2560]{0:T(1024)S(1)}, u32[]{:S(2)}, u32[]{:S(2)}) collective-permute-start(f32[2560]{0:T(1024)S(1)} %slice_reduce_fusion), channel_id=1, source_target_pairs={{0,3},{1,2},{2,1},{3,0},{4,7},{5,6},{6,5},{7,4},{8,11},{9,10},{10,... | collective-permute-start | bytes 30728 | tf_op jit(solution)/shard_map/ppermute | solution.py:454
  13.2 2.5 %collective-permute-start.2 = (f32[2560]{0:T(1024)S(1)}, f32[2560]{0:T(1024)S(1)}, u32[]{:S(2)}, u32[]{:S(2)}) collective-permute-start(f32[2560]{0:T(1024)S(1)} %slice_reduce_fusion), channel_id=1, source_target_pairs={{0,2},{1,3},{2,0},{3,1},{4,6},{5,7},{6,4},{7,5},{8,10},{9,11},{10,... | collective-permute-start | bytes 30728 | tf_op jit(solution)/shard_map/ppermute | solution.py:454
  13.2 2.5 %collective-permute-start = (f32[2560]{0:T(1024)S(1)}, f32[2560]{0:T(1024)S(1)}, u32[]{:S(2)}, u32[]{:S(2)}) collective-permute-start(f32[2560]{0:T(1024)S(1)} %slice_reduce_fusion), channel_id=1, source_target_pairs={{0,1},{1,0},{2,3},{3,2},{4,5},{5,4},{6,7},{7,6},{8,9},{9,8},{10,11... | collective-permute-start | bytes 30728 | tf_op jit(solution)/shard_map/ppermute | solution.py:454
  13.6 5.1 %collective-permute-start.4 = (f32[2,2,32,1024]{3,2,1,0:T(8,128)S(1)}, f32[2,2,32,1024]{3,2,1,0:T(8,128)}, u32[]{:S(2)}, u32[]{:S(2)}) collective-permute-start(f32[2,2,32,1024]{3,2,1,0:T(8,128)S(1)} %get-tuple-element.41), channel_id=1, source_target_pairs={{0,1},{1,0},{2,3},{3,2},{4,5},{5,4},{6,7},{7,6},{8,9},{9,8},{10,11... | collective-permute-start | bytes 1572872 | tf_op jit(solution)/shard_map/ppermute | solution.py:467
  13.7 3.0 %collective-permute-start.1 = (f32[2,2,32,1536]{3,2,1,0:T(8,128)S(1)}, f32[2,2,32,1536]{3,2,1,0:T(8,128)S(1)}, u32[]{:S(2)}, u32[]{:S(2)}) collective-permute-start(f32[2,2,32,1536]{3,2,1,0:T(8,128)S(1)} %get-tuple-element.31), channel_id=1, source_target_pairs={{0,1},{1,0},{2,3},{3,2},{4,5},{5,4},{6,7},{7,6},{8,9},{9,8},{10,11... | collective-permute-start | bytes 2359304 | tf_op jit(solution)/shard_map/ppermute | solution.py:467
  17.7 10.9 %collective-permute-start.11 = (f32[2,32,1536]{2,1,0:T(8,128)}, f32[2,32,1536]{2,1,0:T(8,128)}, u32[]{:S(2)}, u32[]{:S(2)}) collective-permute-start(f32[2,32,1536]{2,1,0:T(8,128)} %pad_maximum_fusion.4._late), channel_id=1, source_target_pairs={{0,2},{1,3},{2,0},{3,1},{4,6},{5,7},{6,4},{7,5},{8,10},{9,11},{10,... | collective-permute-start | bytes 1179656 | tf_op jit(solution)/shard_map/ppermute | solution.py:471
  20.7 13.5 %collective-permute-start.5 = (f32[2,32,1024]{2,1,0:T(8,128)}, f32[2,32,1024]{2,1,0:T(8,128)}, u32[]{:S(2)}, u32[]{:S(2)}) collective-permute-start(f32[2,32,1024]{2,1,0:T(8,128)} %pad_maximum_fusion.8), channel_id=1, source_target_pairs={{0,2},{1,3},{2,0},{3,1},{4,6},{5,7},{6,4},{7,5},{8,10},{9,11},{10,... | collective-permute-start | bytes 786440 | tf_op jit(solution)/shard_map/ppermute | solution.py:471
  29.7 8.6 %collective-permute-start.12 = (f32[32,1536]{1,0:T(8,128)S(1)}, f32[32,1536]{1,0:T(8,128)S(1)}, u32[]{:S(2)}, u32[]{:S(2)}) collective-permute-start(f32[32,1536]{1,0:T(8,128)S(1)} %get-tuple-element.56), channel_id=1, source_target_pairs={{0,4},{1,5},{2,6},{3,7},{12,8},{13,9},{14,10},{15,11},{16,20},{17,... | collective-permute-start | bytes 589832 | tf_op jit(solution)/shard_map/ppermute | solution.py:491
  35.2 5.0 %collective-permute-start.6 = (f32[32,1024]{1,0:T(8,128)S(1)}, f32[32,1024]{1,0:T(8,128)S(1)}, u32[]{:S(2)}, u32[]{:S(2)}) collective-permute-start(f32[32,1024]{1,0:T(8,128)S(1)} %get-tuple-element.62), channel_id=1, source_target_pairs={{0,4},{1,5},{2,6},{3,7},{12,8},{13,9},{14,10},{15,11},{16,20},{17,... | collective-permute-start | bytes 393224 | tf_op jit(solution)/shard_map/ppermute | solution.py:491
  38.4 2.6 %collective-permute-start.13 = (f32[32,1536]{1,0:T(8,128)S(1)}, f32[32,1536]{1,0:T(8,128)S(1)}, u32[]{:S(2)}, u32[]{:S(2)}) collective-permute-start(f32[32,1536]{1,0:T(8,128)S(1)} %add_select_fusion.9), channel_id=1, source_target_pairs={{4,8},{5,9},{6,10},{7,11},{8,4},{9,5},{10,6},{11,7},{20,24},{21,25... | collective-permute-start | bytes 589832 | tf_op jit(solution)/shard_map/ppermute | solution.py:491
  40.3 2.1 %collective-permute-start.7 = (f32[32,1024]{1,0:T(8,128)S(1)}, f32[32,1024]{1,0:T(8,128)S(1)}, u32[]{:S(2)}, u32[]{:S(2)}) collective-permute-start(f32[32,1024]{1,0:T(8,128)S(1)} %add_select_fusion.12), channel_id=1, source_target_pairs={{4,8},{5,9},{6,10},{7,11},{8,4},{9,5},{10,6},{11,7},{20,24},{21,25... | collective-permute-start | bytes 393224 | tf_op jit(solution)/shard_map/ppermute | solution.py:491
  41.0 8.7 %collective-permute-start.14 = (f32[32,1536]{1,0:T(8,128)S(1)}, f32[32,1536]{1,0:T(8,128)S(1)}, u32[]{:S(2)}, u32[]{:S(2)}) collective-permute-start(f32[32,1536]{1,0:T(8,128)S(1)} %get-tuple-element.53), channel_id=1, source_target_pairs={{8,12},{9,13},{10,14},{11,15},{4,0},{5,1},{6,2},{7,3},{24,28},{25,... | collective-permute-start | bytes 589832 | tf_op jit(solution)/shard_map/ppermute | solution.py:491
  42.4 11.4 %collective-permute-start.8 = (f32[32,1024]{1,0:T(8,128)S(1)}, f32[32,1024]{1,0:T(8,128)S(1)}, u32[]{:S(2)}, u32[]{:S(2)}) collective-permute-start(f32[32,1024]{1,0:T(8,128)S(1)} %get-tuple-element.59), channel_id=1, source_target_pairs={{8,12},{9,13},{10,14},{11,15},{4,0},{5,1},{6,2},{7,3},{24,28},{25,... | collective-permute-start | bytes 393224 | tf_op jit(solution)/shard_map/ppermute | solution.py:491
  50.9 6.7 %collective-permute-start.15 = (f32[2,32,1536]{2,1,0:T(8,128)S(1)}, f32[2,32,1536]{2,1,0:T(8,128)S(1)}, u32[]{:S(2)}, u32[]{:S(2)}) collective-permute-start(f32[2,32,1536]{2,1,0:T(8,128)S(1)} %pad_maximum_fusion.5), channel_id=1, source_target_pairs={{0,2},{1,3},{2,0},{3,1},{4,6},{5,7},{6,4},{7,5},{8,10},{9,11},{10,... | collective-permute-start | bytes 1179656 | tf_op jit(solution)/shard_map/ppermute | solution.py:506
  54.9 10.9 %collective-permute-start.9 = (f32[2,32,1024]{2,1,0:T(8,128)S(1)}, f32[2,32,1024]{2,1,0:T(8,128)S(1)}, u32[]{:S(2)}, u32[]{:S(2)}) collective-permute-start(f32[2,32,1024]{2,1,0:T(8,128)S(1)} %pad_maximum_fusion.9), channel_id=1, source_target_pairs={{0,2},{1,3},{2,0},{3,1},{4,6},{5,7},{6,4},{7,5},{8,10},{9,11},{10,... | collective-permute-start | bytes 786440 | tf_op jit(solution)/shard_map/ppermute | solution.py:506
  57.6 11.9 %copy-start = (bf16[4,256,384]{2,1,0:T(8,128)(2,1)S(1)}, bf16[4,256,384]{2,1,0:T(8,128)(2,1)}, u32[]{:S(2)}) copy-start(bf16[4,256,384]{2,1,0:T(8,128)(2,1)} %get-tuple-element.32.left_y) | copy-start | bytes 2359300
  57.6 11.9 %copy-start.1 = (bf16[4,256,384]{2,1,0:T(8,128)(2,1)S(1)}, bf16[4,256,384]{2,1,0:T(8,128)(2,1)}, u32[]{:S(2)}) copy-start(bf16[4,256,384]{2,1,0:T(8,128)(2,1)} %get-tuple-element.33.left_x) | copy-start | bytes 2359300
  57.6 11.9 %copy-start.2 = (bf16[4,128,384]{2,1,0:T(8,128)(2,1)S(1)}, bf16[4,128,384]{2,1,0:T(8,128)(2,1)}, u32[]{:S(2)}) copy-start(bf16[4,128,384]{2,1,0:T(8,128)(2,1)} %get-tuple-element.34.left_c) | copy-start | bytes 1179652
  57.7 11.9 %copy-start.3 = (bf16[4,128,384]{2,1,0:T(8,128)(2,1)S(1)}, bf16[4,128,384]{2,1,0:T(8,128)(2,1)}, u32[]{:S(2)}) copy-start(bf16[4,128,384]{2,1,0:T(8,128)(2,1)} %get-tuple-element.35.left_b) | copy-start | bytes 1179652
  57.7 11.9 %copy-start.4 = (bf16[512,128]{1,0:T(8,128)(2,1)S(1)}, bf16[512,128]{1,0:T(8,128)(2,1)}, u32[]{:S(2)}) copy-start(bf16[512,128]{1,0:T(8,128)(2,1)} %get-tuple-element.36.up) | copy-start | bytes 393220
  57.7 11.9 %copy-start.5 = (bf16[512,128]{1,0:T(8,128)(2,1)S(1)}, bf16[512,128]{1,0:T(8,128)(2,1)}, u32[]{:S(2)}) copy-start(bf16[512,128]{1,0:T(8,128)(2,1)} %get-tuple-element.37.down) | copy-start | bytes 393220
  57.7 11.9 %copy-start.6 = (bf16[4,16,128]{2,1,0:T(8,128)(2,1)S(1)}, bf16[4,16,128]{2,1,0:T(8,128)(2,1)}, u32[]{:S(2)}) copy-start(bf16[4,16,128]{2,1,0:T(8,128)(2,1)} %get-tuple-element.38.edges) | copy-start | bytes 49156
  57.7 11.9 %copy-start.7 = (f32[1,2560]{1,0:T(1,128)S(1)}, f32[1,2560]{1,0:T(1,128)}, u32[]{:S(2)}) copy-start(f32[1,2560]{1,0:T(1,128)} %get-tuple-element.39.skip_ref) | copy-start | bytes 30724
  58.0 11.5 %collective-permute-start.16 = (f32[2,2,32,1536]{3,2,1,0:T(8,128)S(1)}, f32[2,2,32,1536]{3,2,1,0:T(8,128)S(1)}, u32[]{:S(2)}, u32[]{:S(2)}) collective-permute-start(f32[2,2,32,1536]{3,2,1,0:T(8,128)S(1)} %pad_maximum_fusion.1), channel_id=1, source_target_pairs={{0,1},{1,0},{2,3},{3,2},{4,5},{5,4},{6,7},{7,6},{8,9},{9,8},{10,11... | collective-permute-start | bytes 2359304 | tf_op jit(solution)/shard_map/ppermute | solution.py:521
  67.1 14.9 %collective-permute-start.10 = (f32[2,2,32,1024]{3,2,1,0:T(8,128)S(1)}, f32[2,2,32,1024]{3,2,1,0:T(8,128)S(1)}, u32[]{:S(2)}, u32[]{:S(2)}) collective-permute-start(f32[2,2,32,1024]{3,2,1,0:T(8,128)S(1)} %pad_maximum_fusion.3), channel_id=1, source_target_pairs={{0,1},{1,0},{2,3},{3,2},{4,5},{5,4},{6,7},{7,6},{8,9},{9,8},{10,11... | collective-permute-start | bytes 1572872 | tf_op jit(solution)/shard_map/ppermute | solution.py:521
